TPU v7x, 256 devices: a whole 4x4x8 slice. The times are simulated.
256 devices in a mesh: blk: 32 (over y_lo, z, core), uly: 8 (over y_hi, x).
Axes of the slice: x: 4, y: 4 (y_hi: 2, y_lo: 2; y = y_hi * 2 + y_lo), z: 8, core: 2. Of those that a mesh axis runs over, the one named last changes fastest.
Arguments:
- tokens: bfloat16 [32768, 5120], P(('blk', 'uly')), may hold values from -6 to 6
- query_base: bfloat16 [32768, 5120], P(('blk', 'uly')), may hold values from -9 to 9
- key_base: bfloat16 [32768, 5120], P(('blk', 'uly')), may hold values from -9 to 9
- value_base: bfloat16 [32768, 5120], P(('blk', 'uly')), may hold values from -6 to 6
- out_grad: bfloat16 [32768, 5120], P(('blk', 'uly')), may hold values from -0.059814453 to 0.059814453
- down_q: bfloat16 [5120, 64], replicated, may hold values from -0.078125 to 0.078125
- up_q: bfloat16 [64, 5120], replicated, may hold values from -0.75 to 0.75
- down_v: bfloat16 [5120, 64], replicated, may hold values from -0.078125 to 0.078125
- up_v: bfloat16 [64, 5120], replicated, may hold values from -0.75 to 0.75
Outputs:
- attended: bfloat16 [32768, 5120], P(('blk', 'uly'))
- grad_down_q: bfloat16 [5120, 64], replicated
- grad_up_q: bfloat16 [64, 5120], P(None, 'uly')
- grad_down_v: bfloat16 [5120, 64], replicated
- grad_up_v: bfloat16 [64, 5120], P(None, 'uly')
All inputs are finite; a program needn't handle non-finite values.
Results may differ from a plain program's by a relative error of at most 0.025.
Values may be sent and summed in bfloat16 or wider, within the bound.
No kernel may reach another device: no remote copies, remote signals or barrier semaphores. Data moves between devices by JAX's collectives and lax.ppermute only.
A program may use at most 128 MiB of HBM per device.

v0:
```python
import jax
import jax.numpy as jnp
from jax import lax
from jax.sharding import PartitionSpec as P

HEAD = 128


def passed_along(block, axis, distance):
    devices = range(lax.axis_size(axis))
    route = [(i - distance, i) for i in devices if i - distance in devices]
    return lax.ppermute(block, axis, route)


def inner(left, right):
    return lax.dot_general(
        left, right, (((0,), (0,)), ((), ())), preferred_element_type=jnp.float32
    )


def head_pass(query, keys, values, upstream, usable, scale):
    scores = jnp.dot(query, keys.T, preferred_element_type=jnp.float32) * scale
    scores = jnp.where(usable[None, :], scores, -jnp.inf)
    top = jnp.max(scores, axis=1, keepdims=True)
    total = jnp.sum(jnp.exp(scores - top), axis=1, keepdims=True)
    probs = jnp.exp(scores - top - jnp.log(total)).astype(jnp.bfloat16)
    attended = jnp.dot(probs, values, preferred_element_type=jnp.float32).astype(jnp.bfloat16)
    delta = jnp.sum(
        upstream.astype(jnp.float32) * attended.astype(jnp.float32), axis=1, keepdims=True
    )
    prob_grad = jnp.dot(upstream, values.T, preferred_element_type=jnp.float32)
    score_grad = (probs.astype(jnp.float32) * (prob_grad - delta)).astype(jnp.bfloat16)
    query_grad = (jnp.dot(score_grad, keys, preferred_element_type=jnp.float32) * scale).astype(
        jnp.bfloat16
    )
    value_terms = jnp.dot(probs.T, upstream, preferred_element_type=jnp.float32)
    return (attended, query_grad, value_terms)


def per_device(tokens, query_base, key_base, value_base, out_grad, down_q, up_q, down_v, up_v):
    low_q = jnp.dot(tokens, down_q, preferred_element_type=jnp.float32).astype(jnp.bfloat16)
    low_v = jnp.dot(tokens, down_v, preferred_element_type=jnp.float32).astype(jnp.bfloat16)
    query = (
        query_base.astype(jnp.float32) + jnp.dot(low_q, up_q, preferred_element_type=jnp.float32)
    ).astype(jnp.bfloat16)
    value = (
        value_base.astype(jnp.float32) + jnp.dot(low_v, up_v, preferred_element_type=jnp.float32)
    ).astype(jnp.bfloat16)
    query_h, keys_h, values_h, upstream_h = (
        lax.all_to_all(query, "uly", split_axis=1, concat_axis=0, tiled=True),
        lax.all_to_all(key_base, "uly", split_axis=1, concat_axis=0, tiled=True),
        lax.all_to_all(value, "uly", split_axis=1, concat_axis=0, tiled=True),
        lax.all_to_all(out_grad, "uly", split_axis=1, concat_axis=0, tiled=True),
    )
    rows = query_h.shape[0]
    width = query_h.shape[1]
    heads_here = width // HEAD
    scale = HEAD ** (-0.5)
    earlier = passed_along(jnp.stack([keys_h, values_h]), "blk", 1)
    keys_all = jnp.concatenate([earlier[0], keys_h], 0)
    values_all = jnp.concatenate([earlier[1], values_h], 0)
    column = jnp.arange(2 * rows)
    usable = jnp.logical_or(column >= rows, lax.axis_index("blk") > 0)

    def per_head(index, carry):
        attended, query_grad, own_terms, prior_terms = carry
        start = index * HEAD
        result = head_pass(
            lax.dynamic_slice_in_dim(query_h, start, HEAD, 1),
            lax.dynamic_slice_in_dim(keys_all, start, HEAD, 1),
            lax.dynamic_slice_in_dim(values_all, start, HEAD, 1),
            lax.dynamic_slice_in_dim(upstream_h, start, HEAD, 1),
            usable,
            scale,
        )
        attended = lax.dynamic_update_slice_in_dim(attended, result[0], start, 1)
        query_grad = lax.dynamic_update_slice_in_dim(query_grad, result[1], start, 1)
        prior_terms = lax.dynamic_update_slice_in_dim(prior_terms, result[2][:rows], start, 1)
        own_terms = lax.dynamic_update_slice_in_dim(own_terms, result[2][rows:], start, 1)
        return (attended, query_grad, own_terms, prior_terms)

    empty_half = jnp.zeros((rows, width), jnp.bfloat16)
    empty_full = jnp.zeros((rows, width), jnp.float32)
    attended_h, query_grad_h, own_terms, prior_terms = lax.fori_loop(
        0, heads_here, per_head, (empty_half, empty_half, empty_full, empty_full)
    )
    returned = passed_along(prior_terms, "blk", -1)
    value_grad_h = (own_terms + returned).astype(jnp.bfloat16)
    rank = down_q.shape[1]
    first_col = lax.axis_index("uly") * width
    attended, query_grad, value_grad = (
        lax.all_to_all(attended_h, "uly", split_axis=0, concat_axis=1, tiled=True),
        lax.all_to_all(query_grad_h, "uly", split_axis=0, concat_axis=1, tiled=True),
        lax.all_to_all(value_grad_h, "uly", split_axis=0, concat_axis=1, tiled=True),
    )
    lowrank = jnp.concatenate(
        [
            jnp.dot(query_grad, up_q.T, preferred_element_type=jnp.float32),
            jnp.dot(value_grad, up_v.T, preferred_element_type=jnp.float32),
        ],
        1,
    ).astype(jnp.bfloat16)
    down_terms = inner(tokens, lowrank)
    up_q_terms = inner(low_q, query_grad)
    up_v_terms = inner(low_v, value_grad)
    down_total, up_q_total, up_v_total = lax.psum(
        (down_terms, up_q_terms, up_v_terms), ("blk", "uly")
    )
    up_q_part = lax.dynamic_slice_in_dim(up_q_total, first_col, width, 1)
    up_v_part = lax.dynamic_slice_in_dim(up_v_total, first_col, width, 1)
    return (
        attended,
        down_total[:, :rank].astype(jnp.bfloat16),
        up_q_part.astype(jnp.bfloat16),
        down_total[:, rank:].astype(jnp.bfloat16),
        up_v_part.astype(jnp.bfloat16),
    )


def solution(mesh):
    return jax.shard_map(
        per_device,
        mesh=mesh,
        in_specs=(
            P(("blk", "uly"), None),
            P(("blk", "uly"), None),
            P(("blk", "uly"), None),
            P(("blk", "uly"), None),
            P(("blk", "uly"), None),
            P(),
            P(),
            P(),
            P(),
        ),
        out_specs=(P(("blk", "uly"), None), P(), P(None, "uly"), P(), P(None, "uly")),
        check_vma=False,
    )
```

profile of v0, /device:TPU:1, one launch (start us, length us, event | category | flops | bytes accessed | tf_op | source)
XLA Modules:
  0.0 463.8 jit_solution(9758977872020225476)
XLA Ops:
  0.7 1.3 copy-done
  2.0 1.7 convolution_convert_fusion.3
  3.6 1.6 fusion.20
  6.5 7.5 %all-to-all-start.2 = ((bf16[128,8,640]{2,0,1:T(8,128)(2,1)}), bf16[128,8,640]{2,0,1:T(8,128)(2,1)S(1)}, u32[]{:S(2)}, u32[]{:S(2)}) async-start(bf16[128,8,640]{2,0,1:T(8,128)(2,1)} %bitcast.90), calls=%async_computation.2 | async-start | bytes 2621440 | tf_op jit(solution)/shard_map/all_to_all | solution.py:52
  13.9 2.5 copy.67
  16.4 17.6 %all-to-all-done.2 = bf16[128,8,640]{2,0,1:T(8,128)(2,1)S(1)} async-done(((bf16[128,8,640]{2,0,1:T(8,128)(2,1)}), bf16[128,8,640]{2,0,1:T(8,128)(2,1)S(1)}, u32[]{:S(2)}, u32[]{:S(2)}) %all-to-all-start.2) | async-done | bytes 1310752 | tf_op jit(solution)/shard_map/all_to_all | solution.py:52
  34.0 22.7 %all_to_all.133 = bf16[128,8,640]{2,0,1:T(8,128)(2,1)S(1)} all-to-all(bf16[128,8,640]{2,0,1:T(8,128)(2,1)} %bitcast.91), channel_id=1, replica_groups=mesh['blk'=32,'uly'=8] {'uly'}, dimensions={1} | all-to-all | bytes 2621440 | tf_op jit(solution)/shard_map/all_to_all | solution.py:51
  56.7 1.9 pad_maximum_fusion
  58.6 5.2 %collective-permute-start = (bf16[2,1024,640]{2,1,0:T(8,128)(2,1)}, bf16[2,1024,640]{2,1,0:T(8,128)(2,1)}, u32[]{:S(2)}, u32[]{:S(2)}) collective-permute-start(bf16[2,1024,640]{2,1,0:T(8,128)(2,1)} %pad_maximum_fusion), channel_id=1, source_target_pairs={{0,8},{8,16},{16,24},{24,32},{32,40},{40,48},{48,56},{56,64},{64,7... | collective-permute-start | bytes 7864328 | tf_op jit(solution)/shard_map/ppermute | solution.py:12
  63.8 2.5 copy.48
  66.4 4.4 all-to-all-start.3
  70.8 1.8 convolution_convert_fusion.4
  74.3 35.5 %all-to-all-done.3 = bf16[128,8,640]{0,2,1:T(8,128)(2,1)} async-done(((bf16[128,8,640]{0,2,1:T(8,128)(2,1)}), bf16[128,8,640]{0,2,1:T(8,128)(2,1)}, u32[]{:S(2)}, u32[]{:S(2)}) %all-to-all-start.3) | async-done | bytes 1310752 | tf_op jit(solution)/shard_map/all_to_all | solution.py:53
  109.8 4.4 all-to-all-start
  114.2 2.4 copy.49
  116.6 2.0 slice_bitcast_fusion
  118.7 6.8 %pad_maximum_fusion.1 = (bf16[2048,640]{1,0:T(8,128)(2,1)}, bf16[2048,640]{1,0:T(8,128)(2,1)}) fusion(bf16[1024,640]{1,0:T(8,128)(2,1)S(1)} %bitcast.77, bf16[1024,640]{1,0:T(8,128)(2,1)S(1)} %get-tuple-element.289, bf16[1024,640]{1,0:T(8,128)(2,1)S(1)} %bitcast.75, bf16[1024,640]{1,0:T(8,128)(2,1)S(1)} %get-tuple-element.288), kind=kLoop, calls=%fused_computation.33 | loop fusion | flops 10485760 | bytes 10485760 | tf_op jit(solution)/shard_map/concatenate | solution.py:60
  125.5 9.0 %all-to-all-done = bf16[128,8,640]{2,0,1:T(8,128)(2,1)} async-done(((bf16[128,8,640]{2,0,1:T(8,128)(2,1)}), bf16[128,8,640]{2,0,1:T(8,128)(2,1)}, u32[]{:S(2)}, u32[]{:S(2)}) %all-to-all-start) | async-done | bytes 1310752 | tf_op jit(solution)/shard_map/all_to_all | solution.py:50
  134.4 1.6 broadcast_in_dim.43
  136.1 1.7 broadcast_in_dim.43.clone
  139.0 103.0 %while.20 = (s32[]{:T(128)}, bf16[1024,640]{1,0:T(8,128)(2,1)S(1)}, bf16[1024,640]{1,0:T(8,128)(2,1)}, f32[1024,640]{1,0:T(8,128)}, f32[1024,640]{1,0:T(8,128)},...) while((s32[]{:T(128)}, bf16[1024,640]{1,0:T(8,128)(2,1)S(1)}, ...), condition=%wide.region_4.5_spmd.clone, body=%wide.region_0.4_spmd.clone.sunk | while | flops 2718827520 | bytes 67680992 | solution.py:84
  139.0 2.6 fusion.67
  141.6 2.2 exponential_reduce_fusion.2
  143.8 2.3 exponential_convert_fusion.2
  149.9 3.8 multiply_reduce_fusion.2
  153.8 5.6 %fusion.68 = bf16[1024,640]{1,0:T(8,128)(2,1)} fusion(bf16[1024,640]{1,0:T(8,128)(2,1)} %get-tuple-element.383, s32[]{:T(128)S(6)} %select_n.43, bf16[1024,2048]{1,0:T(8,128)(2,1)} %copy-done.1, bf16[1024,128]{1,0:T(8,128)(2,1)S(1)} %constant_dynamic-slice_fusion.2, f32[1024]{0:T(1024)S(1)} %get-tuple-element.364, ...), kind=kOutput, calls=%fused_computation.10.clone.1 | convolution fusion | flops 1082392576 | bytes 5772800 | tf_op jit(solution)/shard_map/while/body/eval_jaxpr/dot_general | solution.py:33
  159.7 2.6 fusion.67
  162.3 2.2 exponential_reduce_fusion.2
  164.5 2.3 exponential_convert_fusion.2
  170.5 3.8 multiply_reduce_fusion.2
  174.4 5.6 %fusion.68 = bf16[1024,640]{1,0:T(8,128)(2,1)} fusion(bf16[1024,640]{1,0:T(8,128)(2,1)} %get-tuple-element.383, s32[]{:T(128)S(6)} %select_n.43, bf16[1024,2048]{1,0:T(8,128)(2,1)} %copy-done.1, bf16[1024,128]{1,0:T(8,128)(2,1)S(1)} %constant_dynamic-slice_fusion.2, f32[1024]{0:T(1024)S(1)} %get-tuple-element.364, ...), kind=kOutput, calls=%fused_computation.10.clone.1 | convolution fusion | flops 1082392576 | bytes 5772800 | tf_op jit(solution)/shard_map/while/body/eval_jaxpr/dot_general | solution.py:33
  180.3 2.6 fusion.67
  182.8 2.2 exponential_reduce_fusion.2
  185.1 2.3 exponential_convert_fusion.2
  191.1 3.8 multiply_reduce_fusion.2
  195.0 5.6 %fusion.68 = bf16[1024,640]{1,0:T(8,128)(2,1)} fusion(bf16[1024,640]{1,0:T(8,128)(2,1)} %get-tuple-element.383, s32[]{:T(128)S(6)} %select_n.43, bf16[1024,2048]{1,0:T(8,128)(2,1)} %copy-done.1, bf16[1024,128]{1,0:T(8,128)(2,1)S(1)} %constant_dynamic-slice_fusion.2, f32[1024]{0:T(1024)S(1)} %get-tuple-element.364, ...), kind=kOutput, calls=%fused_computation.10.clone.1 | convolution fusion | flops 1082392576 | bytes 5772800 | tf_op jit(solution)/shard_map/while/body/eval_jaxpr/dot_general | solution.py:33
  200.9 2.6 fusion.67
  203.5 2.2 exponential_reduce_fusion.2
  205.7 2.3 exponential_convert_fusion.2
  211.7 3.8 multiply_reduce_fusion.2
  215.5 5.6 %fusion.68 = bf16[1024,640]{1,0:T(8,128)(2,1)} fusion(bf16[1024,640]{1,0:T(8,128)(2,1)} %get-tuple-element.383, s32[]{:T(128)S(6)} %select_n.43, bf16[1024,2048]{1,0:T(8,128)(2,1)} %copy-done.1, bf16[1024,128]{1,0:T(8,128)(2,1)S(1)} %constant_dynamic-slice_fusion.2, f32[1024]{0:T(1024)S(1)} %get-tuple-element.364, ...), kind=kOutput, calls=%fused_computation.10.clone.1 | convolution fusion | flops 1082392576 | bytes 5772800 | tf_op jit(solution)/shard_map/while/body/eval_jaxpr/dot_general | solution.py:33
  221.5 2.6 fusion.67
  224.0 2.2 exponential_reduce_fusion.2
  226.2 2.3 exponential_convert_fusion.2
  232.3 3.8 multiply_reduce_fusion.2
  236.1 5.6 %fusion.68 = bf16[1024,640]{1,0:T(8,128)(2,1)} fusion(bf16[1024,640]{1,0:T(8,128)(2,1)} %get-tuple-element.383, s32[]{:T(128)S(6)} %select_n.43, bf16[1024,2048]{1,0:T(8,128)(2,1)} %copy-done.1, bf16[1024,128]{1,0:T(8,128)(2,1)S(1)} %constant_dynamic-slice_fusion.2, f32[1024]{0:T(1024)S(1)} %get-tuple-element.364, ...), kind=kOutput, calls=%fused_computation.10.clone.1 | convolution fusion | flops 1082392576 | bytes 5772800 | tf_op jit(solution)/shard_map/while/body/eval_jaxpr/dot_general | solution.py:33
  242.0 2.7 collective-permute-start.1
  244.8 24.5 %all_to_all.134 = bf16[8,128,640]{2,1,0:T(8,128)(2,1)} all-to-all(bf16[8,128,640]{2,1,0:T(8,128)(2,1)} %bitcast.88), channel_id=1, replica_groups=mesh['blk'=32,'uly'=8] {'uly'}, dimensions={0} | all-to-all | bytes 2621440 | tf_op jit(solution)/shard_map/all_to_all | solution.py:93
  269.3 3.6 all-to-all-start.4
  272.9 2.4 collective-permute-done.1
  275.3 3.8 add_convert_fusion
  279.2 13.9 %all-to-all-done.4 = bf16[8,128,640]{2,1,0:T(8,128)(2,1)S(1)} async-done(((bf16[8,128,640]{2,1,0:T(8,128)(2,1)}), bf16[8,128,640]{2,1,0:T(8,128)(2,1)S(1)}, u32[]{:S(2)}, u32[]{:S(2)}) %all-to-all-start.4) | async-done | bytes 1310752 | tf_op jit(solution)/shard_map/all_to_all | solution.py:92
  293.0 4.5 all-to-all-start.6
  297.5 1.8 copy.54
  299.3 1.6 fusion.27
  300.9 2.5 copy.53
  303.4 2.4 copy.56
  306.2 11.3 %all-to-all-done.6 = bf16[8,128,640]{2,1,0:T(8,128)(2,1)} async-done(((bf16[8,128,640]{2,1,0:T(8,128)(2,1)}), bf16[8,128,640]{2,1,0:T(8,128)(2,1)}, u32[]{:S(2)}, u32[]{:S(2)}) %all-to-all-start.6) | async-done | bytes 1310752 | tf_op jit(solution)/shard_map/all_to_all | solution.py:94
  317.5 1.8 copy.55
  319.6 1.6 fusion.28
  321.2 2.0 convolution_bitcast_fusion
  323.2 135.9 %all-reduce.2 = (bf16[5120,128]{0,1:T(8,128)(2,1)}, bf16[64,5120]{1,0:T(8,128)(2,1)S(1)}, bf16[64,5120]{1,0:T(8,128)(2,1)}) all-reduce(f32[5120,128]{0,1:T(8,128)} %convolution_bitcast_fusion, f32[64,5120]{1,0:T(8,128)S(1)} %copy-done.4, f32[64,5120]{1,0:T(8,128)} %fusion.28), channel_id=1, replica_groups=mesh['blk'=32,'uly'=8] {'blk','uly'}, use_global_device_ids=true, to_apply=%region_5.6 | all-reduce | flops 1310720 | bytes 7864320 | tf_op jit(solution)/shard_map/psum | solution.py:106
  459.2 2.4 fusion.25
  461.6 1.5 dynamic-slice_convert_fusion
  (80 shorter events, 25.6 us)
Async XLA Ops:
  0.6 1.3 copy-start
  0.6 3.0 copy-start.10
  6.5 27.6 %all-to-all-start.2 = ((bf16[128,8,640]{2,0,1:T(8,128)(2,1)}), bf16[128,8,640]{2,0,1:T(8,128)(2,1)S(1)}, u32[]{:S(2)}, u32[]{:S(2)}) async-start(bf16[128,8,640]{2,0,1:T(8,128)(2,1)} %bitcast.90), calls=%async_computation.2 | async-start | bytes 2621440 | tf_op jit(solution)/shard_map/all_to_all | solution.py:52
  56.7 1.9 copy-start.2
  58.6 58.0 %collective-permute-start = (bf16[2,1024,640]{2,1,0:T(8,128)(2,1)}, bf16[2,1024,640]{2,1,0:T(8,128)(2,1)}, u32[]{:S(2)}, u32[]{:S(2)}) collective-permute-start(bf16[2,1024,640]{2,1,0:T(8,128)(2,1)} %pad_maximum_fusion), channel_id=1, source_target_pairs={{0,8},{8,16},{16,24},{24,32},{32,40},{40,48},{48,56},{56,64},{64,7... | collective-permute-start | bytes 7864328 | tf_op jit(solution)/shard_map/ppermute | solution.py:12
  66.4 6.2 %copy-start.7 = (bf16[64,5120]{1,0:T(8,128)(2,1)S(1)}, bf16[64,5120]{1,0:T(8,128)(2,1)}, u32[]{:S(2)}) copy-start(bf16[64,5120]{1,0:T(8,128)(2,1)} %param.17) | copy-start | bytes 1966084
  66.4 43.4 %all-to-all-start.3 = ((bf16[128,8,640]{0,2,1:T(8,128)(2,1)}), bf16[128,8,640]{0,2,1:T(8,128)(2,1)}, u32[]{:S(2)}, u32[]{:S(2)}) async-start(bf16[128,8,640]{0,2,1:T(8,128)(2,1)} %bitcast.89), calls=%async_computation.3 | async-start | bytes 2621440 | tf_op jit(solution)/shard_map/all_to_all | solution.py:53
  70.8 1.8 copy-start.11
  109.8 24.7 %all-to-all-start = ((bf16[128,8,640]{2,0,1:T(8,128)(2,1)}), bf16[128,8,640]{2,0,1:T(8,128)(2,1)}, u32[]{:S(2)}, u32[]{:S(2)}) async-start(bf16[128,8,640]{2,0,1:T(8,128)(2,1)} %bitcast.86), calls=%async_computation | async-start | bytes 2621440 | tf_op jit(solution)/shard_map/all_to_all | solution.py:50
  116.6 2.1 copy-start.3
  146.1 2.5 copy-start.1
  166.8 2.5 copy-start.1
  187.3 2.5 copy-start.1
  208.0 2.5 copy-start.1
  228.5 2.5 copy-start.1
  242.0 27.3 %copy-start.6 = (bf16[1024,640]{1,0:T(8,128)(2,1)}, bf16[1024,640]{1,0:T(8,128)(2,1)S(1)}, u32[]{:S(2)}) copy-start(bf16[1024,640]{1,0:T(8,128)(2,1)S(1)} %get-tuple-element.177) | copy-start | bytes 3932164
  242.0 33.3 %collective-permute-start.1 = (f32[1024,640]{1,0:T(8,128)}, f32[1024,640]{1,0:T(8,128)}, u32[]{:S(2)}, u32[]{:S(2)}) collective-permute-start(f32[1024,640]{1,0:T(8,128)} %get-tuple-element.180), channel_id=1, source_target_pairs={{8,0},{16,8},{24,16},{32,24},{40,32},{48,40},{56,48},{64,56},{72,6... | collective-permute-start | bytes 7864328 | tf_op jit(solution)/shard_map/ppermute | solution.py:12
  269.3 23.7 %all-to-all-start.4 = ((bf16[8,128,640]{2,1,0:T(8,128)(2,1)}), bf16[8,128,640]{2,1,0:T(8,128)(2,1)S(1)}, u32[]{:S(2)}, u32[]{:S(2)}) async-start(bf16[8,128,640]{2,1,0:T(8,128)(2,1)} %bitcast.87), calls=%async_computation.4 | async-start | bytes 2621440 | tf_op jit(solution)/shard_map/all_to_all | solution.py:92
  293.0 4.5 copy-start.5
  293.0 24.4 %all-to-all-start.6 = ((bf16[8,128,640]{2,1,0:T(8,128)(2,1)}), bf16[8,128,640]{2,1,0:T(8,128)(2,1)}, u32[]{:S(2)}, u32[]{:S(2)}) async-start(bf16[8,128,640]{2,1,0:T(8,128)(2,1)} %bitcast.93), calls=%async_computation.6 | async-start | bytes 2621440 | tf_op jit(solution)/shard_map/all_to_all | solution.py:94
  300.9 4.9 %copy-start.8 = (bf16[64,5120]{1,0:T(8,128)(2,1)S(1)}, bf16[64,5120]{1,0:T(8,128)(2,1)}, u32[]{:S(2)}) copy-start(bf16[64,5120]{1,0:T(8,128)(2,1)} %param.17) | copy-start | bytes 1966084
  306.2 13.0 %copy-start.9 = (bf16[64,5120]{1,0:T(8,128)(2,1)S(1)}, bf16[64,5120]{1,0:T(8,128)(2,1)}, u32[]{:S(2)}) copy-start(bf16[64,5120]{1,0:T(8,128)(2,1)} %param.19) | copy-start | bytes 1966084
  321.2 2.0 copy-start.4
where the time goes:
time: 466 us; the launch traced here: 464 us
  blocking collectives  183 us (39%)
  waiting for transfers between devices  89.6 us (19%)
  matrix products  78.2 us (17%)
  local copies, waits for them, and re-layouts  44.3 us (10%)
  other arithmetic  34.9 us (7%)
  starting transfers between devices  32.2 us (7%)
    psum x1, blocking collectives, per_device(): lax.psum((down_terms, up_q_terms, up_v_terms), ('blk', 'uly'))  136 us
    all_to_all x1, waiting for transfers between devices, per_device(): lax.all_to_all(out_grad, 'uly', split_axis=1, concat_axis=0, tiled=True)  35.5 us
    dot_general x5, matrix products, head_pass(): jnp.dot(score_grad, keys, preferred_element_type=jnp.float32) * scale  28.2 us
    all_to_all x1, blocking collectives, per_device(): lax.all_to_all(query_grad_h, 'uly', split_axis=0, concat_axis=1, tiled=True)  24.5 us
    all_to_all x1, blocking collectives, per_device(): lax.all_to_all(key_base, 'uly', split_axis=1, concat_axis=0, tiled=True)  22.7 us
    dot_general x5, matrix products, head_pass(): jnp.dot(probs, values, preferred_element_type=jnp.float32)  19.2 us
    all_to_all x1, waiting for transfers between devices, per_device(): lax.all_to_all(value, 'uly', split_axis=1, concat_axis=0, tiled=True)  17.6 us
    all_to_all x1, waiting for transfers between devices, per_device(): lax.all_to_all(attended_h, 'uly', split_axis=0, concat_axis=1, tiled=True)  13.9 us
  transfers between devices with their start and end apart: 7, of which 6 were waited for; matrix products, arithmetic and copies ran while one was open for 7% of the time, Pallas kernels for 0%

commit v1 on v0

v1 whole, which is shorter than its diff:
```python
import functools

import jax
import jax.numpy as jnp
from jax import lax
from jax.experimental import pallas as pl
from jax.experimental.pallas import tpu as pltpu
from jax.sharding import PartitionSpec as P

HEAD = 128
TILE = 256
LOG2E = 1.4426950408889634
F32 = jnp.float32
BF16 = jnp.bfloat16

Y_CORE = [[half * 16 + z * 2 + core for half in range(2) for core in range(2)] for z in range(8)]
Z_RING = [[half * 16 + z * 2 + core for z in range(8)] for half in range(2) for core in range(2)]


def dot(left, right):
    return jnp.dot(left, right, preferred_element_type=F32)


def dot_t(left, right):
    return lax.dot_general(left, right, (((1,), (1,)), ((), ())), preferred_element_type=F32)


def t_dot(left, right):
    return lax.dot_general(left, right, (((0,), (0,)), ((), ())), preferred_element_type=F32)


def pack_kernel(
    tokens, query_base, key_base, value_base, out_grad, down_q, down_v, up_q, up_v, kvl, qg, low
):
    width = key_base.shape[1]
    rank = down_q.shape[1]

    @pl.when(pl.program_id(0) == 0)
    def _():
        low[:, :rank] = dot(tokens[...], down_q[...]).astype(BF16)
        low[:, rank:] = dot(tokens[...], down_v[...]).astype(BF16)

    kvl[:, :width] = key_base[...]
    kvl[:, width : 2 * width] = (
        value_base[...].astype(F32) + dot(low[:, rank:], up_v[...])
    ).astype(BF16)
    kvl[:, 2 * width :] = low[...]
    qg[:, :width] = (query_base[...].astype(F32) + dot(low[:, :rank], up_q[...])).astype(BF16)
    qg[:, width:] = out_grad[...]


def pack(tokens, query_base, key_base, value_base, out_grad, down_q, up_q, down_v, up_v, parts):
    rows, columns = tokens.shape
    rank = down_q.shape[1]
    width = columns // parts
    whole = lambda j: (0, 0)
    part = lambda j: (0, j)
    once = pl.Buffered(1)
    return pl.pallas_call(
        pack_kernel,
        grid=(parts,),
        in_specs=[pl.BlockSpec((rows, columns), whole, pipeline_mode=once)]
        + [pl.BlockSpec((rows, width), part)] * 4
        + [pl.BlockSpec((columns, rank), whole, pipeline_mode=once)] * 2
        + [pl.BlockSpec((rank, width), part)] * 2,
        out_specs=[
            pl.BlockSpec((rows, 2 * width + 2 * rank), lambda j: (j, 0)),
            pl.BlockSpec((rows, 2 * width), lambda j: (j, 0)),
        ],
        out_shape=[
            jax.ShapeDtypeStruct((parts * rows, 2 * width + 2 * rank), BF16),
            jax.ShapeDtypeStruct((parts * rows, 2 * width), BF16),
        ],
        scratch_shapes=[pltpu.VMEM((rows, 2 * rank), BF16)],
        compiler_params=pltpu.CompilerParams(vmem_limit_bytes=40 << 20),
        name="pack",
    )(tokens, query_base, key_base, value_base, out_grad, down_q, down_v, up_q, up_v)


def attention_kernel(
    place, q, g, k_own, v_own, k_prior, v_prior, low_own, low_prior, up_q, up_v,
    out, ups, lq, lo, lp, dv_own, dv_prior,
):
    head = pl.program_id(0)
    heads = pl.num_programs(0)
    rows = q.shape[0]
    rank = up_q.shape[0]
    scale = HEAD ** (-0.5)
    factor = scale * LOG2E
    has_prior = place[1] > 0

    @pl.when(head == 0)
    def _():
        lq[...] = jnp.zeros_like(lq)
        lo[...] = jnp.zeros_like(lo)
        lp[...] = jnp.zeros_like(lp)

    up_q_grad = jnp.zeros((HEAD, rank), F32)
    for step in range(rows // TILE):
        here = slice(step * TILE, (step + 1) * TILE)
        q_t = q[here, :]
        g_t = g[here, :]
        s_own = dot_t(q_t, k_own[...])
        s_prior = dot_t(q_t, k_prior[...])
        top_own = jnp.max(s_own, axis=1, keepdims=True)
        top_prior = jnp.max(s_prior, axis=1, keepdims=True)
        top = jnp.where(has_prior, jnp.maximum(top_own, top_prior), top_own) * factor
        top_p = jnp.where(has_prior, top, jnp.float32(1e38))
        p_own = jnp.exp2(s_own * factor - top)
        p_prior = jnp.exp2(s_prior * factor - top_p)
        total = jnp.sum(p_own, axis=1, keepdims=True) + jnp.sum(p_prior, axis=1, keepdims=True)
        inverse = 1.0 / total
        p_own = p_own.astype(BF16)
        p_prior = p_prior.astype(BF16)
        attended = ((dot(p_own, v_own[...]) + dot(p_prior, v_prior[...])) * inverse).astype(BF16)
        out[here, pl.ds(pl.multiple_of(head * HEAD, HEAD), HEAD)] = attended
        delta = jnp.sum(g_t.astype(F32) * attended.astype(F32), axis=1, keepdims=True)
        ds_own = (p_own.astype(F32) * (dot_t(g_t, v_own[...]) - delta)).astype(BF16)
        ds_prior = (p_prior.astype(F32) * (dot_t(g_t, v_prior[...]) - delta)).astype(BF16)
        dq = ((dot(ds_own, k_own[...]) + dot(ds_prior, k_prior[...])) * (inverse * scale)).astype(
            BF16
        )
        scaled = (g_t.astype(F32) * inverse).astype(BF16)
        if step == 0:
            dv_own[...] = t_dot(p_own, scaled)
            dv_prior[...] = t_dot(p_prior, scaled)
        else:
            dv_own[...] += t_dot(p_own, scaled)
            dv_prior[...] += t_dot(p_prior, scaled)
        lq[here, :] += dot_t(dq, up_q[...])
        up_q_grad += t_dot(dq, low_own[here, :rank])
    own = dv_own[...].astype(BF16)
    prior = dv_prior[...].astype(BF16)
    lo[...] += dot_t(own, up_v[...])
    lp[...] += dot_t(prior, up_v[...])
    ups[:, :rank] = up_q_grad.astype(BF16)
    ups[:, rank:] = (t_dot(own, low_own[:, rank:]) + t_dot(prior, low_prior[:, rank:])).astype(
        BF16
    )

    @pl.when(head == heads - 1)
    def _():
        width = heads * HEAD
        first = out.shape[1] - 4 * rank
        out[:, first : first + rank] = lq[...].astype(BF16)
        out[:, first + rank : first + 2 * rank] = lo[...].astype(BF16)
        out[:, first + 2 * rank : first + 3 * rank] = lp[...].astype(BF16)
        out[:, first + 3 * rank :] = jnp.zeros((rows, rank), BF16)


def attention(place, qg, kvl, kvl_prior, up_q, up_v):
    rows = qg.shape[0]
    width = qg.shape[1] // 2
    heads = width // HEAD
    rank = up_q.shape[0]
    column = lambda offset: pl.BlockSpec((rows, HEAD), lambda h, place: (0, h + offset))
    fixed = lambda at: pl.BlockSpec((rows, HEAD), lambda h, place: (0, at))
    up = pl.BlockSpec((rank, HEAD), lambda h, place: (0, place[0] * heads + h))
    matmuls = 5 * 2 * heads * rows * 2 * rows * HEAD
    return pl.pallas_call(
        attention_kernel,
        grid_spec=pltpu.PrefetchScalarGridSpec(
            num_scalar_prefetch=1,
            grid=(heads,),
            in_specs=[
                column(0),
                column(heads),
                column(0),
                column(heads),
                column(0),
                column(heads),
                fixed(2 * heads),
                fixed(2 * heads),
                up,
                up,
            ],
            out_specs=[
                pl.BlockSpec((rows, width + 4 * rank), lambda h, place: (0, 0)),
                pl.BlockSpec((HEAD, 2 * rank), lambda h, place: (h, 0)),
            ],
            scratch_shapes=[pltpu.VMEM((rows, rank), F32)] * 3
            + [pltpu.VMEM((rows, HEAD), F32)] * 2,
        ),
        out_shape=[
            jax.ShapeDtypeStruct((rows, width + 4 * rank), BF16),
            jax.ShapeDtypeStruct((width, 2 * rank), BF16),
        ],
        compiler_params=pltpu.CompilerParams(vmem_limit_bytes=56 << 20),
        cost_estimate=pl.CostEstimate(
            flops=matmuls, bytes_accessed=12 << 20, transcendentals=heads * rows * 2 * rows
        ),
        name="attention",
    )(place, qg, qg, kvl, kvl, kvl_prior, kvl_prior, kvl, kvl_prior, up_q, up_v)


def exchange(array, axis, groups=None):
    return lax.all_to_all(
        array, axis, split_axis=0, concat_axis=0, tiled=True, axis_index_groups=groups
    )


def summed(array, axis, size, groups=None):
    got = exchange(array, axis, groups)
    return jnp.sum(got.reshape(size, -1, array.shape[1]).astype(F32), axis=0)


def gathered(array, axis, size, groups=None):
    return exchange(jnp.concatenate([array] * size, 0), axis, groups)


def per_device(tokens, query_base, key_base, value_base, out_grad, down_q, up_q, down_v, up_v):
    blocks = lax.axis_size("blk")
    parts = lax.axis_size("uly")
    rows, columns = tokens.shape
    rank = down_q.shape[1]
    width = columns // parts
    kvl, qg = pack(
        tokens, query_base, key_base, value_base, out_grad, down_q, up_q, down_v, up_v, parts
    )
    kvl = exchange(kvl, "uly")
    kvl_prior = lax.ppermute(kvl, "blk", [(i, i + 1) for i in range(blocks - 1)])
    qg, _ = lax.optimization_barrier((qg, kvl))
    qg = exchange(qg, "uly")
    place = jnp.stack([lax.axis_index("uly"), lax.axis_index("blk")]).astype(jnp.int32)
    out, ups = attention(place, qg, kvl, kvl_prior, up_q, up_v)
    back = exchange(out, "uly").reshape(parts, rows, -1)
    attended = back[:, :, :width].transpose(1, 0, 2).reshape(rows, columns)
    low_terms = jnp.sum(back[:, :, width : width + 3 * rank].astype(F32), axis=0)
    returned = lax.ppermute(
        low_terms[:, 2 * rank :], "blk", [(i, i - 1) for i in range(1, blocks)]
    )
    lowrank = jnp.concatenate(
        [low_terms[:, :rank], low_terms[:, rank : 2 * rank] + returned], 1
    ).astype(BF16)
    down = t_dot(tokens, lowrank).astype(BF16)
    quarter = columns // 4
    both = jnp.concatenate(
        [down.reshape(4, quarter, 2 * rank), ups.reshape(4, width // 4, 2 * rank)], 1
    ).reshape(-1, 2 * rank)
    both = summed(both, "blk", 4, Y_CORE)
    down = summed(both[:quarter].astype(BF16), "uly", parts)
    piece = quarter // parts // 8
    both = jnp.concatenate(
        [down.reshape(8, piece, 2 * rank), both[quarter:].reshape(8, piece, 2 * rank)], 1
    ).reshape(-1, 2 * rank)
    both = summed(both.astype(BF16), "blk", 8, Z_RING).astype(BF16)
    both = gathered(both, "blk", 8, Z_RING).reshape(8, 2 * piece, 2 * rank)
    down = gathered(both[:, :piece].reshape(-1, 2 * rank), "uly", parts)
    ups = both[:, piece:].reshape(-1, 2 * rank)
    both = gathered(jnp.concatenate([down, ups], 0), "blk", 4, Y_CORE).reshape(4, -1, 2 * rank)
    down = both[:, :quarter].reshape(columns, 2 * rank)
    ups = both[:, quarter:].reshape(width, 2 * rank)
    return (
        attended,
        down[:, :rank],
        ups[:, :rank].T,
        down[:, rank:],
        ups[:, rank:].T,
    )


def solution(mesh):
    rows = P(("blk", "uly"), None)
    return jax.shard_map(
        per_device,
        mesh=mesh,
        in_specs=(rows,) * 5 + (P(),) * 4,
        out_specs=(rows, P(), P(None, "uly"), P(), P(None, "uly")),
        check_vma=False,
    )
```

time: 466 us -> 326 us (0.70)
  matrix products: 78.2 us -> 1.67 us
  blocking collectives: 183 us -> 114 us
  Pallas kernels: 0 us -> 50.1 us
  other arithmetic: 34.9 us -> 2.7 us
  local copies, waits for them, and re-layouts: 44.3 us -> 33.3 us
    psum x1 -> x0, blocking collectives: 136 us -> none  [per_device(): lax.psum((down_terms, up_q_terms, up_v_terms), ('blk', 'uly'))]
    dot_general x29 -> x1, matrix products: 78.2 us -> 1.67 us  [t_dot(): lax.dot_general(left, right, (((0,), (0,)), ((), ())), preferred_element_...]
    all_to_all x2 -> x5, blocking collectives: 47.2 us -> 114 us  [exchange(): lax.all_to_all(array, axis, split_axis=0, concat_axis=0, tiled=True, axis...]
    pallas_call x0 -> x2, Pallas kernels: none -> 50.1 us  [the longest x1 44.3 us: attention(): pl.pallas_call(attention_kernel, grid_spec=pltpu.PrefetchScalarGridSpec(n...]
    unnamed x24 -> x48, local copies, waits for them, and re-layouts: 6.33 us -> 25.3 us
    convert_element_type x6 -> x0, other arithmetic: 15.1 us -> none  [the longest x5 11.3 us: head_pass(): probs = jnp.exp(scores - top - jnp.log(total)).astype(jnp.bfloat16)]
    all_to_all x7 -> x0, local copies, waits for them, and re-layouts: 13.3 us -> none  [the longest x1 2.5 us: per_device(): lax.all_to_all(key_base, 'uly', split_axis=1, concat_axis=0, tiled=True)]
    reduce_sum x5 -> x4, other arithmetic: 11.1 us -> 1.91 us  [the longest x3 1.83 us: summed(): return jnp.sum(got.reshape(size, -1, array.shape[1]).astype(F32), axis=0)]
  transfers between devices with their start and end apart: 7 -> 6, of which waited for: 6 -> 5; matrix products, arithmetic and copies ran while one was open for 7% -> 1% of each run, Pallas kernels for 0% -> 0%
where the time goes in v1:
time: 326 us; the launch traced here: 325 us
  blocking collectives  114 us (35%)
  waiting for transfers between devices  94.2 us (29%)
  Pallas kernels  50.1 us (15%)
  local copies, waits for them, and re-layouts  33.3 us (10%)
  starting transfers between devices  28.3 us (9%)
    all_to_all x5, blocking collectives, exchange(): lax.all_to_all(array, axis, split_axis=0, concat_axis=0, tiled=True, axis...  114 us
    all_to_all x4, waiting for transfers between devices, exchange(): lax.all_to_all(array, axis, split_axis=0, concat_axis=0, tiled=True, axis...  92.2 us
    pallas_call x1, Pallas kernels, attention(): pl.pallas_call(attention_kernel, grid_spec=pltpu.PrefetchScalarGridSpec(n...  44.3 us
    unnamed x48, local copies, waits for them, and re-layouts  25.3 us
    all_to_all x4, starting transfers between devices, exchange(): lax.all_to_all(array, axis, split_axis=0, concat_axis=0, tiled=True, axis...  19.6 us
  transfers between devices with their start and end apart: 6, of which 5 were waited for; matrix products, arithmetic and copies ran while one was open for 1% of the time, Pallas kernels for 0%

profile of v1, /device:TPU:1, one launch (start us, length us, event | category | flops | bytes accessed | tf_op | source)
XLA Modules:
  0.0 324.9 jit_solution(7128802335329858669)
XLA Ops:
  0.6 0.0 copy-start.7
  0.6 0.0 copy-start
  0.7 1.8 copy.36.down_q
  2.5 2.3 copy.37.down_v
  4.8 1.3 copy-done.1
  6.1 1.3 copy-done.3
  7.4 1.3 copy-done.4
  8.7 1.3 copy-done.5
  10.0 1.3 copy-done.6
  11.4 1.1 copy-done.8
  12.4 5.8 %pack.1 = (bf16[1024,1408]{1,0:T(8,128)(2,1)}, bf16[1024,1280]{1,0:T(8,128)(2,1)S(1)}) custom-call(bf16[128,5120]{1,0:T(8,128)(2,1)S(1)} %copy-done, bf16[128,5120]{1,0:T(8,128)(2,1)S(1)} %copy-done.3, bf16[128,5120]{1,0:T(8,128)(2,1)S(1)} %copy-done.4, bf16[128,5120]{1,0:T(8,128)(2,1)S(1)} %copy-done.5, bf16[128,5120]{1,0:T(8,128)(2,1)S(1)} %copy-done.6, ...), custom_call_target="tpu_custom_call" | custom-call | tf_op jit(solution)/shard_map/pack/pallas_call | solution.py:59
  18.2 43.6 %all_to_all.82 = bf16[8,128,1408]{2,1,0:T(8,128)(2,1)} all-to-all(bf16[8,128,1408]{2,1,0:T(8,128)(2,1)} %bitcast.34), channel_id=1, replica_groups=mesh['blk'=32,'uly'=8] {'uly'}, dimensions={0} | all-to-all | bytes 5767168 | tf_op jit(solution)/shard_map/all_to_all | solution.py:197
  61.8 0.0 copy-done.2
  61.8 5.2 %collective-permute-start = (bf16[1024,1408]{1,0:T(8,128)(2,1)}, bf16[1024,1408]{1,0:T(8,128)(2,1)}, u32[]{:S(2)}, u32[]{:S(2)}) collective-permute-start(bf16[1024,1408]{1,0:T(8,128)(2,1)} %bitcast.3.k_own.v_own.low_own), channel_id=1, source_target_pairs={{0,8},{8,16},{16,24},{24,32},{32,40},{40,48},{48,56},{56,64},{64,7... | collective-permute-start | bytes 8650760 | tf_op jit(solution)/shard_map/ppermute | solution.py:221
  67.0 4.4 %all-to-all-start.1 = ((bf16[8,128,1280]{2,1,0:T(8,128)(2,1)}), bf16[8,128,1280]{2,1,0:T(8,128)(2,1)}, u32[]{:S(2)}, u32[]{:S(2)}) async-start(bf16[8,128,1280]{2,1,0:T(8,128)(2,1)} %bitcast.27), calls=%async_computation.1 | async-start | bytes 5242880 | tf_op jit(solution)/shard_map/all_to_all | solution.py:197
  71.5 0.6 pad_add_fusion.place
  72.1 57.7 %all-to-all-done.1 = bf16[8,128,1280]{2,1,0:T(8,128)(2,1)} async-done(((bf16[8,128,1280]{2,1,0:T(8,128)(2,1)}), bf16[8,128,1280]{2,1,0:T(8,128)(2,1)}, u32[]{:S(2)}, u32[]{:S(2)}) %all-to-all-start.1) | async-done | bytes 2621472 | tf_op jit(solution)/shard_map/all_to_all | solution.py:197
  129.8 0.0 collective-permute-done.k_prior.v_prior.low_prior
  129.8 44.3 %attention.1 = (bf16[1024,896]{1,0:T(8,128)(2,1)}, bf16[640,128]{1,0:T(8,128)(2,1)}) custom-call(s32[2]{0:T(128)} %pad_add_fusion.place, bf16[1024,1280]{1,0:T(8,128)(2,1)} %bitcast.5.q.g, bf16[1024,1280]{1,0:T(8,128)(2,1)} %bitcast.5.q.g, bf16[1024,1408]{1,0:T(8,128)(2,1)} %bitcast.3.k_own.v_own.low_own, bf16[1024,1408]{1,0:T(8,128)(2,1)} %bitcast.3.k_own.v_own.low_own, ...), custom_call_target="tpu_custom_call" | custom-call | flops 13421772800 | bytes 12582912 | tf_op jit(solution)/shard_map/attention/pallas_call | solution.py:160
  174.1 29.6 %all_to_all.83 = bf16[8,128,896]{2,1,0:T(8,128)(2,1)S(1)} all-to-all(bf16[8,128,896]{2,1,0:T(8,128)(2,1)} %bitcast.35), channel_id=1, replica_groups=mesh['blk'=32,'uly'=8] {'uly'}, dimensions={0} | all-to-all | bytes 3670016 | tf_op jit(solution)/shard_map/all_to_all | solution.py:197
  203.7 0.1 convert_reduce_fusion
  203.8 3.5 %collective-permute-start.1 = (f32[128,64]{1,0:T(8,128)S(1)}, f32[128,64]{1,0:T(8,128)S(1)}, u32[]{:S(2)}, u32[]{:S(2)}) collective-permute-start(f32[128,64]{1,0:T(8,128)S(1)} %slice.67), channel_id=1, source_target_pairs={{8,0},{16,8},{24,16},{32,24},{40,32},{48,40},{56,48},{64,56},{72,6... | collective-permute-start | bytes 98312 | tf_op jit(solution)/shard_map/ppermute | solution.py:229
  207.4 2.0 collective-permute-done.1
  209.4 0.1 fusion.1
  209.5 1.7 fusion
  211.2 1.8 copy.47
  213.0 0.1 pad_maximum_fusion
  213.1 20.8 %all_to_all.84 = bf16[4,1440,128]{2,1,0:T(8,128)(2,1)} all-to-all(bf16[4,1440,128]{2,1,0:T(8,128)(2,1)S(1)} %pad_maximum_fusion), channel_id=1, replica_groups={{0,8,128,136},{16,24,144,152},{32,40,160,168},{48,56,176,184},{64,72,19..., dimensions={0} | all-to-all | bytes 2949120 | tf_op jit(solution)/shard_map/all_to_all | solution.py:197
  233.9 1.8 reduce.2
  235.7 0.7 slice.68
  236.4 3.4 %all-to-all-start.4 = ((bf16[8,160,128]{2,1,0:T(8,128)(2,1)}), bf16[8,160,128]{2,1,0:T(8,128)(2,1)S(1)}, u32[]{:S(2)}, u32[]{:S(2)}) async-start(bf16[8,160,128]{2,1,0:T(8,128)(2,1)} %bitcast.11), calls=%async_computation.4 | async-start | bytes 655360 | tf_op jit(solution)/shard_map/all_to_all | solution.py:197
  239.9 9.6 %all-to-all-done.4 = bf16[8,160,128]{2,1,0:T(8,128)(2,1)S(1)} async-done(((bf16[8,160,128]{2,1,0:T(8,128)(2,1)}), bf16[8,160,128]{2,1,0:T(8,128)(2,1)S(1)}, u32[]{:S(2)}, u32[]{:S(2)}) %all-to-all-start.4) | async-done | bytes 327712 | tf_op jit(solution)/shard_map/all_to_all | solution.py:197
  249.5 9.8 %all_to_all.85 = bf16[8,40,128]{2,1,0:T(8,128)(2,1)S(1)} all-to-all(bf16[8,40,128]{2,1,0:T(8,128)(2,1)S(1)} %pad_maximum_fusion.1), channel_id=1, replica_groups={{0,16,32,48,64,80,96,112},{8,24,40,56,72,88,104,120},{128,144,160,176,1..., dimensions={0} | all-to-all | bytes 163840 | tf_op jit(solution)/shard_map/all_to_all | solution.py:197
  259.5 9.9 %all_to_all.86 = bf16[8,40,128]{2,1,0:T(8,128)(2,1)S(1)} all-to-all(bf16[8,40,128]{2,1,0:T(8,128)(2,1)S(1)} %bitcast.39), channel_id=1, replica_groups={{0,16,32,48,64,80,96,112},{8,24,40,56,72,88,104,120},{128,144,160,176,1..., dimensions={0} | all-to-all | bytes 163840 | tf_op jit(solution)/shard_map/all_to_all | solution.py:197
  269.4 0.6 constant_dynamic-update-slice_fusion.15
  270.0 0.6 constant_dynamic-update-slice_fusion.14
  270.6 0.6 constant_dynamic-update-slice_fusion.13
  271.3 0.6 constant_dynamic-update-slice_fusion.12
  271.9 0.6 constant_dynamic-update-slice_fusion.11
  272.5 0.6 constant_dynamic-update-slice_fusion.10
  273.1 0.6 constant_dynamic-update-slice_fusion.9
  273.7 0.6 constant_dynamic-update-slice_fusion.8
  274.4 3.4 %all-to-all-start.7 = ((bf16[8,160,128]{2,1,0:T(8,128)(2,1)}), bf16[8,160,128]{2,1,0:T(8,128)(2,1)S(1)}, u32[]{:S(2)}, u32[]{:S(2)}) async-start(bf16[8,160,128]{2,1,0:T(8,128)(2,1)} %bitcast.13), calls=%async_computation.7 | async-start | bytes 655360 | tf_op jit(solution)/shard_map/all_to_all | solution.py:197
  277.8 8.0 %all-to-all-done.7 = bf16[8,160,128]{2,1,0:T(8,128)(2,1)S(1)} async-done(((bf16[8,160,128]{2,1,0:T(8,128)(2,1)}), bf16[8,160,128]{2,1,0:T(8,128)(2,1)S(1)}, u32[]{:S(2)}, u32[]{:S(2)}) %all-to-all-start.7) | async-done | bytes 327712 | tf_op jit(solution)/shard_map/all_to_all | solution.py:197
  285.8 0.7 constant_dynamic-update-slice_fusion.23
  286.6 0.6 constant_dynamic-update-slice_fusion.22
  287.2 0.8 constant_dynamic-update-slice_fusion.21
  288.0 0.6 constant_dynamic-update-slice_fusion.20
  288.6 0.7 constant_dynamic-update-slice_fusion.19
  289.3 0.6 constant_dynamic-update-slice_fusion.18
  289.9 0.8 constant_dynamic-update-slice_fusion.17
  290.7 0.6 constant_dynamic-update-slice_fusion.16
  291.3 8.3 %all-to-all-start.8 = ((bf16[4,1440,128]{2,1,0:T(8,128)(2,1)}), bf16[4,1440,128]{2,1,0:T(8,128)(2,1)}, u32[]{:S(2)}, u32[]{:S(2)}) async-start(bf16[4,1440,128]{2,1,0:T(8,128)(2,1)} %bitcast.15), calls=%async_computation.8 | async-start | bytes 2949120 | tf_op jit(solution)/shard_map/all_to_all | solution.py:197
  299.6 0.1 slice_bitcast_fusion
  299.7 1.2 copy.53
  301.0 16.9 %all-to-all-done.8 = bf16[4,1440,128]{2,1,0:T(8,128)(2,1)} async-done(((bf16[4,1440,128]{2,1,0:T(8,128)(2,1)}), bf16[4,1440,128]{2,1,0:T(8,128)(2,1)}, u32[]{:S(2)}, u32[]{:S(2)}) %all-to-all-start.8) | async-done | bytes 1474592 | tf_op jit(solution)/shard_map/all_to_all | solution.py:197
  317.9 0.9 slice.74
  318.8 0.1 slice_bitcast_fusion.1
  318.9 0.8 copy.46
  319.7 0.8 copy.45
  320.4 1.4 slice.72
  321.8 0.5 fusion.6
  322.3 1.3 copy.52
  323.6 1.3 copy.51
  (30 shorter events, 0.3 us)
Async XLA Ops:
  0.6 4.1 %copy-start.7 = (bf16[64,5120]{1,0:T(8,128)(2,1)S(1)}, bf16[64,5120]{1,0:T(8,128)(2,1)}, u32[]{:S(2)}) copy-start(bf16[64,5120]{1,0:T(8,128)(2,1)} %up_q.3) | copy-start | bytes 1966084
  0.6 4.1 %copy-start = (bf16[128,5120]{1,0:T(8,128)(2,1)S(1)}, bf16[128,5120]{1,0:T(8,128)(2,1)}, u32[]{:S(2)}) copy-start(bf16[128,5120]{1,0:T(8,128)(2,1)} %tokens.1) | copy-start | bytes 3932164
  4.8 1.3 copy-start.1
  6.1 1.3 copy-start.3
  7.4 1.3 copy-start.4
  8.7 1.3 copy-start.5
  10.0 1.3 copy-start.6
  11.4 1.1 copy-start.8
  18.2 43.6 %copy-start.2 = (bf16[1024,1280]{1,0:T(8,128)(2,1)}, bf16[1024,1280]{1,0:T(8,128)(2,1)S(1)}, u32[]{:S(2)}) copy-start(bf16[1024,1280]{1,0:T(8,128)(2,1)S(1)} %get-tuple-element.12) | copy-start | bytes 7864324
  61.8 68.0 %collective-permute-start = (bf16[1024,1408]{1,0:T(8,128)(2,1)}, bf16[1024,1408]{1,0:T(8,128)(2,1)}, u32[]{:S(2)}, u32[]{:S(2)}) collective-permute-start(bf16[1024,1408]{1,0:T(8,128)(2,1)} %bitcast.3.k_own.v_own.low_own), channel_id=1, source_target_pairs={{0,8},{8,16},{16,24},{24,32},{32,40},{40,48},{48,56},{56,64},{64,7... | collective-permute-start | bytes 8650760 | tf_op jit(solution)/shard_map/ppermute | solution.py:221
  67.0 62.8 %all-to-all-start.1 = ((bf16[8,128,1280]{2,1,0:T(8,128)(2,1)}), bf16[8,128,1280]{2,1,0:T(8,128)(2,1)}, u32[]{:S(2)}, u32[]{:S(2)}) async-start(bf16[8,128,1280]{2,1,0:T(8,128)(2,1)} %bitcast.27), calls=%async_computation.1 | async-start | bytes 5242880 | tf_op jit(solution)/shard_map/all_to_all | solution.py:197
  203.8 5.6 %collective-permute-start.1 = (f32[128,64]{1,0:T(8,128)S(1)}, f32[128,64]{1,0:T(8,128)S(1)}, u32[]{:S(2)}, u32[]{:S(2)}) collective-permute-start(f32[128,64]{1,0:T(8,128)S(1)} %slice.67), channel_id=1, source_target_pairs={{8,0},{16,8},{24,16},{32,24},{40,32},{48,40},{56,48},{64,56},{72,6... | collective-permute-start | bytes 98312 | tf_op jit(solution)/shard_map/ppermute | solution.py:229
  211.2 1.8 copy-start.9
  236.4 13.0 %all-to-all-start.4 = ((bf16[8,160,128]{2,1,0:T(8,128)(2,1)}), bf16[8,160,128]{2,1,0:T(8,128)(2,1)S(1)}, u32[]{:S(2)}, u32[]{:S(2)}) async-start(bf16[8,160,128]{2,1,0:T(8,128)(2,1)} %bitcast.11), calls=%async_computation.4 | async-start | bytes 655360 | tf_op jit(solution)/shard_map/all_to_all | solution.py:197
  274.4 11.5 %all-to-all-start.7 = ((bf16[8,160,128]{2,1,0:T(8,128)(2,1)}), bf16[8,160,128]{2,1,0:T(8,128)(2,1)S(1)}, u32[]{:S(2)}, u32[]{:S(2)}) async-start(bf16[8,160,128]{2,1,0:T(8,128)(2,1)} %bitcast.13), calls=%async_computation.7 | async-start | bytes 655360 | tf_op jit(solution)/shard_map/all_to_all | solution.py:197
  291.3 26.5 %all-to-all-start.8 = ((bf16[4,1440,128]{2,1,0:T(8,128)(2,1)}), bf16[4,1440,128]{2,1,0:T(8,128)(2,1)}, u32[]{:S(2)}, u32[]{:S(2)}) async-start(bf16[4,1440,128]{2,1,0:T(8,128)(2,1)} %bitcast.15), calls=%async_computation.8 | async-start | bytes 2949120 | tf_op jit(solution)/shard_map/all_to_all | solution.py:197

commit v2 on v1

v2 whole, which is shorter than its diff:
```python
import functools

import jax
import jax.numpy as jnp
from jax import lax
from jax.experimental import pallas as pl
from jax.experimental.pallas import tpu as pltpu
from jax.sharding import PartitionSpec as P

HEAD = 128
TILE = 256
LOG2E = 1.4426950408889634
F32 = jnp.float32
BF16 = jnp.bfloat16
GROUPS = (3, 2)
CALLS = ((2, 1), (2,))

PAIR = [[2 * i, 2 * i + 1] for i in range(16)]
Z_RING = [[half * 16 + z * 2 + core for z in range(8)] for half in range(2) for core in range(2)]
Y_PAIR = [(i, i ^ 16) for i in range(32)]


def dot(left, right):
    return jnp.dot(left, right, preferred_element_type=F32)


def dot_t(left, right):
    return lax.dot_general(left, right, (((1,), (1,)), ((), ())), preferred_element_type=F32)


def t_dot(left, right):
    return lax.dot_general(left, right, (((0,), (0,)), ((), ())), preferred_element_type=F32)


def pack_kernel(
    tokens, query_base, key_base, value_base, out_grad, down_q, down_v, up_q, up_v, *rest
):
    outs, low = rest[:-1], rest[-1]
    rank = down_q.shape[0]

    @pl.when(pl.program_id(0) == 0)
    def _():
        low[:, :rank] = dot_t(tokens[...], down_q[...]).astype(BF16)
        low[:, rank:] = dot_t(tokens[...], down_v[...]).astype(BF16)

    value = (value_base[...].astype(F32) + dot(low[:, rank:], up_v[...])).astype(BF16)
    query = (query_base[...].astype(F32) + dot(low[:, :rank], up_q[...])).astype(BF16)
    first = 0
    for group, heads in enumerate(GROUPS):
        kvl, qg = outs[2 * group], outs[2 * group + 1]
        width = heads * HEAD
        here = slice(first, first + width)
        kvl[:, :width] = key_base[:, here]
        kvl[:, width : 2 * width] = value[:, here]
        if group == 0:
            kvl[:, 2 * width :] = low[...]
        qg[:, :width] = query[:, here]
        qg[:, width:] = out_grad[:, here]
        first += width


def pack(tokens, query_base, key_base, value_base, out_grad, down_q, up_q, down_v, up_v, parts):
    rows, columns = tokens.shape
    rank = down_q.shape[0]
    width = columns // parts
    whole = lambda j: (0, 0)
    part = lambda j: (0, j)
    once = pl.Buffered(1)
    sizes = []
    for group, heads in enumerate(GROUPS):
        sizes += [2 * heads * HEAD + (2 * rank if group == 0 else 0), 2 * heads * HEAD]
    return pl.pallas_call(
        pack_kernel,
        grid=(parts,),
        in_specs=[pl.BlockSpec((rows, columns), whole, pipeline_mode=once)]
        + [pl.BlockSpec((rows, width), part)] * 4
        + [pl.BlockSpec((rank, columns), whole, pipeline_mode=once)] * 2
        + [pl.BlockSpec((rank, width), part)] * 2,
        out_specs=[pl.BlockSpec((rows, size), lambda j: (j, 0)) for size in sizes],
        out_shape=[jax.ShapeDtypeStruct((parts * rows, size), BF16) for size in sizes],
        scratch_shapes=[pltpu.VMEM((rows, 2 * rank), BF16)],
        compiler_params=pltpu.CompilerParams(vmem_limit_bytes=60 << 20),
        cost_estimate=pl.CostEstimate(flops=1 << 29, bytes_accessed=14 << 20, transcendentals=0),
        name="pack",
    )(tokens, query_base, key_base, value_base, out_grad, down_q, down_v, up_q, up_v)


def attention_kernel(
    last, place, q, g, k_own, v_own, k_prior, v_prior, low_own, low_prior, up_q, up_v, low_in,
    buffer, out, ups, *rest,
):
    low_out = None if last else rest[0]
    lq, lo, lp, dv_own, dv_prior = rest[-5:]
    head = pl.program_id(0)
    heads = pl.num_programs(0)
    rows = q.shape[0]
    rank = up_q.shape[0]
    scale = HEAD ** (-0.5)
    factor = scale * LOG2E
    has_prior = place[1] > 0

    @pl.when(head == 0)
    def _():
        lq[...] = low_in[:, :rank]
        lo[...] = low_in[:, rank : 2 * rank]
        lp[...] = low_in[:, 2 * rank : 3 * rank]

    up_q_grad = jnp.zeros((rank, HEAD), F32)
    for step in range(rows // TILE):
        here = slice(step * TILE, (step + 1) * TILE)
        q_t = q[here, :]
        g_t = g[here, :]
        s_own = dot_t(q_t, k_own[...])
        s_prior = dot_t(q_t, k_prior[...])
        top_own = jnp.max(s_own, axis=1, keepdims=True)
        top_prior = jnp.max(s_prior, axis=1, keepdims=True)
        top = jnp.where(has_prior, jnp.maximum(top_own, top_prior), top_own) * factor
        top_p = jnp.where(has_prior, top, jnp.float32(1e38))
        p_own = jnp.exp2(s_own * factor - top)
        p_prior = jnp.exp2(s_prior * factor - top_p)
        total = jnp.sum(p_own, axis=1, keepdims=True) + jnp.sum(p_prior, axis=1, keepdims=True)
        inverse = 1.0 / total
        p_own = p_own.astype(BF16)
        p_prior = p_prior.astype(BF16)
        attended = ((dot(p_own, v_own[...]) + dot(p_prior, v_prior[...])) * inverse).astype(BF16)
        if last:
            out[here, pl.ds(pl.multiple_of(head * HEAD, HEAD), HEAD)] = attended
        else:
            out[here, :] = attended
        delta = jnp.sum(g_t.astype(F32) * attended.astype(F32), axis=1, keepdims=True)
        ds_own = (p_own.astype(F32) * (dot_t(g_t, v_own[...]) - delta)).astype(BF16)
        ds_prior = (p_prior.astype(F32) * (dot_t(g_t, v_prior[...]) - delta)).astype(BF16)
        dq = ((dot(ds_own, k_own[...]) + dot(ds_prior, k_prior[...])) * (inverse * scale)).astype(
            BF16
        )
        scaled = (g_t.astype(F32) * inverse).astype(BF16)
        if step == 0:
            dv_own[...] = t_dot(p_own, scaled)
            dv_prior[...] = t_dot(p_prior, scaled)
        else:
            dv_own[...] += t_dot(p_own, scaled)
            dv_prior[...] += t_dot(p_prior, scaled)
        lq[here, :] += dot_t(dq, up_q[...])
        up_q_grad += t_dot(low_own[here, :rank], dq)
    own = dv_own[...].astype(BF16)
    prior = dv_prior[...].astype(BF16)
    lo[...] += dot_t(own, up_v[...])
    lp[...] += dot_t(prior, up_v[...])
    ups[0] = up_q_grad.astype(BF16)
    ups[1] = (t_dot(low_own[:, rank:], own) + t_dot(low_prior[:, rank:], prior)).astype(BF16)

    @pl.when(head == heads - 1)
    def _():
        to = out if last else low_out
        first = to.shape[1] - 4 * rank
        to[:, first : first + rank] = lq[...].astype(to.dtype)
        to[:, first + rank : first + 2 * rank] = lo[...].astype(to.dtype)
        to[:, first + 2 * rank : first + 3 * rank] = lp[...].astype(to.dtype)
        to[:, first + 3 * rank :] = jnp.zeros((rows, rank), to.dtype)


def attention(place, qg, kvl, kvl_prior, low, low_prior, up_q, up_v, low_in, buffer, at, heads, last):
    rows = qg.shape[0]
    width = qg.shape[1] // 2
    held = width // HEAD
    rank = up_q.shape[0]
    total = sum(GROUPS)
    group_first, first = at
    column = lambda offset: pl.BlockSpec((rows, HEAD), lambda h, place: (0, h + offset))
    fixed = pl.BlockSpec((rows, HEAD), lambda h, place: (0, 2 * GROUPS[0]))
    up = pl.BlockSpec(
        (rank, HEAD), lambda h, place: (0, place[0] * total + group_first + first + h)
    )
    lows = pl.BlockSpec((rows, 4 * rank), lambda h, place: (0, 0))
    out_width = width + 4 * rank if last else width
    out_specs = [
        pl.BlockSpec((rows, out_width), lambda h, place: (0, 0)) if last else column(first),
        pl.BlockSpec((2, rank, HEAD), lambda h, place: (0, h, 0)),
    ]
    out_shape = [
        jax.ShapeDtypeStruct((rows, out_width), BF16),
        jax.ShapeDtypeStruct((2, heads * rank, HEAD), BF16),
    ]
    if not last:
        out_specs.append(lows)
        out_shape.append(jax.ShapeDtypeStruct((rows, 4 * rank), F32))
    aliases = {12: 0}
    if buffer is None:
        buffer = place
        aliases = {}
    return pl.pallas_call(
        functools.partial(attention_kernel, last),
        grid_spec=pltpu.PrefetchScalarGridSpec(
            num_scalar_prefetch=1,
            grid=(heads,),
            in_specs=[
                column(first),
                column(held + first),
                column(first),
                column(held + first),
                column(first),
                column(held + first),
                fixed,
                fixed,
                up,
                up,
                lows,
                pl.BlockSpec(memory_space=pl.ANY),
            ],
            out_specs=out_specs,
            scratch_shapes=[pltpu.VMEM((rows, rank), F32)] * 3
            + [pltpu.VMEM((rows, HEAD), F32)] * 2,
        ),
        out_shape=out_shape,
        input_output_aliases=aliases,
        compiler_params=pltpu.CompilerParams(vmem_limit_bytes=60 << 20),
        cost_estimate=pl.CostEstimate(
            flops=5 * 2 * heads * rows * 2 * rows * HEAD * 4,
            bytes_accessed=heads << 21,
            transcendentals=heads * rows * 2 * rows,
        ),
        name="attention",
    )(place, qg, qg, kvl, kvl, kvl_prior, kvl_prior, low, low_prior, up_q, up_v, low_in, buffer)


def outer_kernel(lows, tokens, earlier, *rest):
    ups, out = rest[:-2], rest[-1]
    rows, columns = tokens.shape
    rank = lows.shape[1] // 4
    low = jnp.sum(lows[...].reshape(-1, rows, 4 * rank).astype(F32), axis=0).astype(BF16)
    grad_q = t_dot(low[:, :rank], tokens[...])
    grad_v = t_dot(low[:, rank : 2 * rank], tokens[...]) + t_dot(
        low[:, 2 * rank : 3 * rank], earlier[...]
    )
    for block in range(columns // HEAD):
        to = slice(block * rank, (block + 1) * rank)
        out[0, to, :] = grad_q[:, block * HEAD : (block + 1) * HEAD].astype(BF16)
        out[1, to, :] = grad_v[:, block * HEAD : (block + 1) * HEAD].astype(BF16)
    first = columns // HEAD * rank
    for up in ups:
        size = up.shape[1]
        out[:, first : first + size, :] = up[...]
        first += size


def outer(lows, tokens, earlier, ups, rank, settled):
    length = tokens.shape[1] // HEAD * rank + sum(up.shape[1] for up in ups)
    whole = lambda array: pl.BlockSpec(array.shape, lambda i: (0,) * array.ndim)
    at = lows.shape[1] // (4 * rank) - 1
    return pl.pallas_call(
        outer_kernel,
        grid=(1,),
        in_specs=[pl.BlockSpec((lows.shape[0], 4 * rank), lambda i: (0, at))]
        + [whole(array) for array in (tokens, earlier, *ups)]
        + [pl.BlockSpec(memory_space=pl.ANY)],
        out_specs=pl.BlockSpec((2, length, HEAD), lambda i: (0, 0, 0)),
        out_shape=jax.ShapeDtypeStruct((2, length, HEAD), BF16),
        compiler_params=pltpu.CompilerParams(vmem_limit_bytes=60 << 20),
        cost_estimate=pl.CostEstimate(flops=1 << 29, bytes_accessed=8 << 20, transcendentals=0),
        name="outer",
    )(lows, tokens, earlier, *ups, settled)


def unpack_kernel(both, down_q, down_v, up_q, up_v):
    rank, columns = down_q.shape
    first = columns // HEAD * rank
    for part, (down, up) in enumerate(((down_q, up_q), (down_v, up_v))):
        for block in range(columns // HEAD):
            down[:, block * HEAD : (block + 1) * HEAD] = both[
                part, block * rank : (block + 1) * rank, :
            ]
        for block in range(up.shape[1] // HEAD):
            up[:, block * HEAD : (block + 1) * HEAD] = both[
                part, first + block * rank : first + (block + 1) * rank, :
            ]


def unpack(both, rank, columns, width):
    return pl.pallas_call(
        unpack_kernel,
        out_shape=[jax.ShapeDtypeStruct((rank, columns), BF16)] * 2
        + [jax.ShapeDtypeStruct((rank, width), BF16)] * 2,
        compiler_params=pltpu.CompilerParams(vmem_limit_bytes=60 << 20),
        name="unpack",
    )(both)


def exchange(array, axis, groups=None):
    return lax.all_to_all(
        array, axis, split_axis=0, concat_axis=0, tiled=True, axis_index_groups=groups
    )


def summed(array, axis, size, groups=None):
    got = exchange(array, axis, groups)
    return jnp.sum(got.reshape(size, -1, array.shape[1]).astype(F32), axis=0).astype(BF16)


def gathered(array, axis, size, groups=None):
    copies = jnp.broadcast_to(array[None], (size,) + array.shape)
    return exchange(copies.reshape(-1, array.shape[1]), axis, groups)


def after(array, *others):
    return pl.pallas_call(
        lambda *refs: None,
        in_specs=[pl.BlockSpec(memory_space=pl.ANY)] * (1 + len(others)),
        out_specs=pl.BlockSpec(memory_space=pl.ANY),
        out_shape=jax.ShapeDtypeStruct(array.shape, array.dtype),
        input_output_aliases={0: 0},
        name="after",
    )(array, *others)


def per_device(tokens, query_base, key_base, value_base, out_grad, down_q, up_q, down_v, up_v):
    blocks = lax.axis_size("blk")
    parts = lax.axis_size("uly")
    rows, columns = tokens.shape
    rank = down_q.shape[1]
    width = columns // parts
    forward = [(i, i + 1) for i in range(blocks - 1)]
    packed = pack(
        tokens, query_base, key_base, value_base, out_grad, down_q.T, up_q, down_v.T, up_v, parts
    )
    place = jnp.stack([lax.axis_index("uly"), lax.axis_index("blk")]).astype(jnp.int32)
    lows = jnp.zeros((parts * rows, 4 * rank), F32)

    def calls(group, received, low, lows):
        kvl, prior, qg = received
        out, ups, first = None, [], 0
        for heads in CALLS[group]:
            last = group == len(GROUPS) - 1
            result = attention(
                place, qg, kvl, prior, *low, up_q, up_v, lows, out,
                (sum(GROUPS[:group]), first), heads, last,
            )
            out = result[0]
            ups.append(result[1])
            lows = None if last else result[2]
            first += heads
            yield out, ups, lows

    kvl_a = exchange(packed[0], "uly")
    prior_a = lax.ppermute(kvl_a, "blk", forward)
    qg_a = exchange(after(packed[1], kvl_a), "uly")
    low = (kvl_a, prior_a)
    kvl_b = exchange(after(packed[2], prior_a, qg_a), "uly")
    run = calls(0, (kvl_a, prior_a, qg_a), low, lows)
    out, ups, lows = next(run)
    kvl_b = after(kvl_b, out)
    prior_b = lax.ppermute(kvl_b, "blk", forward)
    qg_b = exchange(after(packed[3], kvl_b), "uly")
    earlier = lax.ppermute(tokens, "blk", forward)
    out_a, ups, lows = next(run)
    piece_a = exchange(out_a, "uly")
    out_b, ups_b, _ = next(calls(1, (kvl_b, prior_b, qg_b), low, lows))
    back = exchange(out_b, "uly")
    pieces = [piece_a, back]
    both = outer(back, tokens, earlier, ups + ups_b, rank, piece_a)
    both = summed(both.reshape(-1, HEAD), "blk", 2, PAIR)
    length = columns // HEAD * rank
    down = summed(both[:length], "uly", parts)
    piece = length // parts // 8
    both = jnp.concatenate(
        [down.reshape(8, piece, HEAD), both[length:].reshape(8, -1, HEAD)], 1
    ).reshape(-1, HEAD)
    both = summed(both, "blk", 8, Z_RING)
    both = (both.astype(F32) + lax.ppermute(both, "blk", Y_PAIR).astype(F32)).astype(BF16)
    both = gathered(both, "blk", 8, Z_RING).reshape(8, -1, HEAD)
    down = gathered(both[:, :piece].reshape(-1, HEAD), "uly", parts)
    both = jnp.concatenate([down, both[:, piece:].reshape(-1, HEAD)], 0)
    both = gathered(both, "blk", 2, PAIR).reshape(2, -1, HEAD)
    down_q, down_v, up_q, up_v = unpack(both, rank, columns, width)
    attended = jnp.concatenate(
        [
            p.reshape(parts, rows, -1)[:, :, : heads * HEAD]
            for p, heads in zip(pieces, GROUPS)
        ],
        2,
    )
    attended = attended.transpose(1, 0, 2).reshape(rows, columns)
    return (attended, down_q.T, up_q, down_v.T, up_v)


def solution(mesh):
    rows = P(("blk", "uly"), None)
    return jax.shard_map(
        per_device,
        mesh=mesh,
        in_specs=(rows,) * 5 + (P(),) * 4,
        out_specs=(rows, P(), P(None, "uly"), P(), P(None, "uly")),
        check_vma=False,
    )
```

time: 326 us -> 289 us (0.89)
  blocking collectives: 114 us -> 71.3 us
  local copies, waits for them, and re-layouts: 33.3 us -> 7.4 us
  Pallas kernels: 50.1 us -> 68.8 us
  starting transfers between devices: 28.3 us -> 41.5 us
    all_to_all x5, blocking collectives: 114 us -> 71.3 us  [exchange(): lax.all_to_all(array, axis, split_axis=0, concat_axis=0, tiled=True, axis...]
    unnamed x48 -> x18, local copies, waits for them, and re-layouts: 25.3 us -> 3.14 us
    pallas_call x1 -> x9, Pallas kernels: 44.3 us -> 58.5 us  [the longest x3 52 us: attention(): pl.pallas_call(functools.partial(attention_kernel, last), grid_spec=pltpu...]
    all_to_all x4 -> x7, starting transfers between devices: 19.6 us -> 32.4 us  [exchange(): lax.all_to_all(array, axis, split_axis=0, concat_axis=0, tiled=True, axis...]
    pallas_call x1, Pallas kernels: 5.75 us -> 10.4 us  [pack(): pl.pallas_call(pack_kernel, grid=(parts,), in_specs=[pl.BlockSpec((rows,...]
    all_to_all x4 -> x7, waiting for transfers between devices: 92.2 us -> 93.5 us  [exchange(): lax.all_to_all(array, axis, split_axis=0, concat_axis=0, tiled=True, axis...]
    ppermute x2 -> x4, starting transfers between devices: 8.78 us -> 9.14 us  [the longest x1 5.21 us: per_device(): prior_a = lax.ppermute(kvl_a, 'blk', forward)]
  transfers between devices with their start and end apart: 6 -> 11, of which waited for: 5 -> 6; matrix products, arithmetic and copies ran while one was open for 1% -> 1% of each run, Pallas kernels for 0% -> 18%
where the time goes in v2:
time: 289 us; the launch traced here: 288 us
  waiting for transfers between devices  96.1 us (33%)
  blocking collectives  71.3 us (25%)
  Pallas kernels  68.8 us (24%)
  starting transfers between devices  41.5 us (14%)
  local copies, waits for them, and re-layouts  7.4 us (3%)
    all_to_all x7, waiting for transfers between devices, exchange(): lax.all_to_all(array, axis, split_axis=0, concat_axis=0, tiled=True, axis...  93.5 us
    all_to_all x5, blocking collectives, exchange(): lax.all_to_all(array, axis, split_axis=0, concat_axis=0, tiled=True, axis...  71.3 us
    pallas_call x3, Pallas kernels, attention(): pl.pallas_call(functools.partial(attention_kernel, last), grid_spec=pltpu...  52 us
    all_to_all x7, starting transfers between devices, exchange(): lax.all_to_all(array, axis, split_axis=0, concat_axis=0, tiled=True, axis...  32.4 us
    pallas_call x1, Pallas kernels, pack(): pl.pallas_call(pack_kernel, grid=(parts,), in_specs=[pl.BlockSpec((rows,...  10.4 us
  transfers between devices with their start and end apart: 11, of which 6 were waited for; matrix products, arithmetic and copies ran while one was open for 1% of the time, Pallas kernels for 18%

profile of v2, /device:TPU:1, one launch (start us, length us, event | category | flops | bytes accessed | tf_op | source)
XLA Modules:
  0.0 287.8 jit_solution(13274101606360936990)
XLA Ops:
  0.6 10.4 %pack.1 = (bf16[1024,896]{1,0:T(8,128)(2,1)}, bf16[1024,768]{1,0:T(8,128)(2,1)}, bf16[1024,512]{1,0:T(8,128)(2,1)}, bf16[1024,512]{1,0:T(8,128)(2,1)}) custom-call(bf16[128,5120]{1,0:T(8,128)(2,1)} %tokens.3, bf16[128,5120]{1,0:T(8,128)(2,1)} %query_base.1, bf16[128,5120]{1,0:T(8,128)(2,1)} %key_base.1, bf16[128,5120]{1,0:T(8,128)(2,1)} %value_base.1, ...), custom_call_target="tpu_custom_call" | custom-call | flops 536870912 | bytes 14680064 | tf_op jit(solution)/shard_map/pack/pallas_call | solution.py:72
  11.0 32.3 %all_to_all.108 = bf16[8,128,896]{2,1,0:T(8,128)(2,1)S(1)} all-to-all(bf16[8,128,896]{2,1,0:T(8,128)(2,1)} %bitcast.50), channel_id=1, replica_groups=mesh['blk'=32,'uly'=8] {'uly'}, dimensions={0} | all-to-all | bytes 3670016 | tf_op jit(solution)/shard_map/all_to_all | solution.py:289
  43.3 0.0 copy-start.1
  43.3 5.2 %collective-permute-start = (bf16[1024,896]{1,0:T(8,128)(2,1)S(1)}, bf16[1024,896]{1,0:T(8,128)(2,1)}, u32[]{:S(2)}, u32[]{:S(2)}) collective-permute-start(bf16[1024,896]{1,0:T(8,128)(2,1)S(1)} %bitcast.29), channel_id=1, source_target_pairs={{0,8},{8,16},{16,24},{24,32},{32,40},{40,48},{48,56},{56,64},{64,7... | collective-permute-start | bytes 5505032 | tf_op jit(solution)/shard_map/ppermute | solution.py:344
  48.5 0.0 copy-done.1
  48.5 3.6 %all-to-all-start.1 = ((bf16[8,128,768]{2,1,0:T(8,128)(2,1)}), bf16[8,128,768]{2,1,0:T(8,128)(2,1)S(1)}, u32[]{:S(2)}, u32[]{:S(2)}) async-start(bf16[8,128,768]{2,1,0:T(8,128)(2,1)} %bitcast.40), calls=%async_computation.1 | async-start | bytes 3145728 | tf_op jit(solution)/shard_map/all_to_all | solution.py:289
  52.1 0.6 pad_add_fusion.place.buffer
  52.7 35.7 %all-to-all-done.1 = bf16[8,128,768]{2,1,0:T(8,128)(2,1)S(1)} async-done(((bf16[8,128,768]{2,1,0:T(8,128)(2,1)}), bf16[8,128,768]{2,1,0:T(8,128)(2,1)S(1)}, u32[]{:S(2)}, u32[]{:S(2)}) %all-to-all-start.1) | async-done | bytes 1572896 | tf_op jit(solution)/shard_map/all_to_all | solution.py:289
  88.4 0.0 copy-start.6
  88.4 0.0 collective-permute-done.k_prior.v_prior.low_prior.refs_1_
  88.4 1.2 copy-done.6
  89.6 4.4 %all-to-all-start.3 = ((bf16[8,128,512]{2,1,0:T(8,128)(2,1)}), bf16[8,128,512]{2,1,0:T(8,128)(2,1)S(1)}, u32[]{:S(2)}, u32[]{:S(2)}) async-start(bf16[8,128,512]{2,1,0:T(8,128)(2,1)} %bitcast.47), calls=%async_computation.3 | async-start | bytes 2097152 | tf_op jit(solution)/shard_map/all_to_all | solution.py:289
  94.0 1.1 broadcast_in_dim.10.low_in
  95.1 20.3 %attention.3 = (bf16[1024,384]{1,0:T(8,128)(2,1)}, bf16[2,128,128]{2,1,0:T(8,128)(2,1)}, f32[1024,256]{1,0:T(8,128)}) custom-call(s32[2]{0:T(128)} %pad_add_fusion.place.buffer, bf16[1024,768]{1,0:T(8,128)(2,1)} %bitcast.42, bf16[1024,768]{1,0:T(8,128)(2,1)} %bitcast.43, bf16[1024,896]{1,0:T(8,128)(2,1)} %bitcast.31, bf16[1024,896]{1,0:T(8,128)(2,1)} %bitcast.32, ...), custom_call_target="tpu_custom_call" | custom-call | flops 21474836480 | bytes 4194304 | tf_op jit(solution)/shard_map/attention/pallas_call | solution.py:191
  115.4 0.0 copy-start.7
  115.4 0.0 all-to-all-done.3
  115.4 0.0 copy-start
  115.4 1.0 copy-done
  116.4 1.9 collective-permute-start.1
  118.3 0.0 copy-done.7
  118.3 1.9 collective-permute-start.2
  120.2 6.7 %all-to-all-start.4 = ((bf16[8,128,512]{2,1,0:T(8,128)(2,1)}), bf16[8,128,512]{2,1,0:T(8,128)(2,1)S(1)}, u32[]{:S(2)}, u32[]{:S(2)}) async-start(bf16[8,128,512]{2,1,0:T(8,128)(2,1)} %bitcast.46), calls=%async_computation.4 | async-start | bytes 2097152 | tf_op jit(solution)/shard_map/all_to_all | solution.py:289
  126.9 11.6 %attention.4 = (bf16[1024,384]{1,0:T(8,128)(2,1)}, bf16[2,64,128]{2,1,0:T(8,128)(2,1)}, f32[1024,256]{1,0:T(8,128)}) custom-call(s32[2]{0:T(128)} %pad_add_fusion.place.buffer, bf16[1024,768]{1,0:T(8,128)(2,1)} %bitcast.44, bf16[1024,768]{1,0:T(8,128)(2,1)} %bitcast.45, bf16[1024,896]{1,0:T(8,128)(2,1)} %bitcast.34, ...), custom_call_target="tpu_custom_call", output_to_operand_aliasing={{0}: (12, {})} | custom-call | flops 10737418240 | bytes 2097152 | tf_op jit(solution)/shard_map/attention/pallas_call | solution.py:191
  138.5 19.0 %all-to-all-done.4 = bf16[8,128,512]{2,1,0:T(8,128)(2,1)S(1)} async-done(((bf16[8,128,512]{2,1,0:T(8,128)(2,1)}), bf16[8,128,512]{2,1,0:T(8,128)(2,1)S(1)}, u32[]{:S(2)}, u32[]{:S(2)}) %all-to-all-start.4) | async-done | bytes 1048608 | tf_op jit(solution)/shard_map/all_to_all | solution.py:289
  157.4 0.0 copy-start.8
  157.4 4.0 %all-to-all-start.2 = ((bf16[8,128,384]{2,1,0:T(8,128)(2,1)}), bf16[8,128,384]{2,1,0:T(8,128)(2,1)S(1)}, u32[]{:S(2)}, u32[]{:S(2)}) async-start(bf16[8,128,384]{2,1,0:T(8,128)(2,1)} %bitcast.48), calls=%async_computation.2 | async-start | bytes 1572864 | tf_op jit(solution)/shard_map/all_to_all | solution.py:289
  161.4 0.0 collective-permute-done.1.k_prior.v_prior
  161.4 0.0 copy-done.8
  161.4 20.2 %attention.5 = (bf16[1024,512]{1,0:T(8,128)(2,1)}, bf16[2,128,128]{2,1,0:T(8,128)(2,1)}) custom-call(s32[2]{0:T(128)} %pad_add_fusion.place.buffer, bf16[1024,512]{1,0:T(8,128)(2,1)} %bitcast.52, bf16[1024,512]{1,0:T(8,128)(2,1)} %bitcast.53, bf16[1024,512]{1,0:T(8,128)(2,1)} %after.6.refs_1_.k_own.v_own, bf16[1024,512]{1,0:T(8,128)(2,1)} %after.6.refs_1_.k_own.v_own, ...), custom_call_target="tpu_custom_call" | custom-call | flops 21474836480 | bytes 4194304 | tf_op jit(solution)/shard_map/attention/pallas_call | solution.py:191
  181.6 0.0 all-to-all-done.2
  181.6 0.0 copy-start.2
  181.6 6.7 %all-to-all-start.5 = ((bf16[8,128,512]{2,1,0:T(8,128)(2,1)}), bf16[8,128,512]{2,1,0:T(8,128)(2,1)S(1)}, u32[]{:S(2)}, u32[]{:S(2)}) async-start(bf16[8,128,512]{2,1,0:T(8,128)(2,1)} %bitcast.54), calls=%async_computation.5 | async-start | bytes 2097152 | tf_op jit(solution)/shard_map/all_to_all | solution.py:289
  188.3 0.0 collective-permute-done.2.earlier
  188.3 17.3 %all-to-all-done.5 = bf16[8,128,512]{2,1,0:T(8,128)(2,1)S(1)} async-done(((bf16[8,128,512]{2,1,0:T(8,128)(2,1)}), bf16[8,128,512]{2,1,0:T(8,128)(2,1)S(1)}, u32[]{:S(2)}, u32[]{:S(2)}) %all-to-all-start.5) | async-done | bytes 1048608 | tf_op jit(solution)/shard_map/all_to_all | solution.py:289
  205.6 0.0 copy-start.4
  205.6 0.0 copy-done.2
  205.6 1.0 copy-done.4
  206.5 3.8 %outer.1 = bf16[2,2880,128]{2,1,0:T(8,128)(2,1)} custom-call(bf16[1024,512]{1,0:T(8,128)(2,1)} %bitcast.39, bf16[128,5120]{1,0:T(8,128)(2,1)} %tokens.3, bf16[128,5120]{1,0:T(8,128)(2,1)} %collective-permute-done.2.earlier, bf16[2,128,128]{2,1,0:T(8,128)(2,1)} %get-tuple-element.30.rest_0_, bf16[2,64,128]{2,1,0:T(8,128)(2,1)} %get-tuple-element.31.rest_1_, ...), custom_call_target="tpu_custom_call" | custom-call | flops 536870912 | bytes 8388608 | tf_op jit(solution)/shard_map/outer/pallas_call | solution.py:250
  210.3 6.5 %all_to_all.109 = bf16[2,2880,128]{2,1,0:T(8,128)(2,1)S(1)} all-to-all(bf16[2,2880,128]{2,1,0:T(8,128)(2,1)} %outer.1), channel_id=1, replica_groups={{0,8},{16,24},{32,40},{48,56},{64,72},{80,88},{96,104},{112,120},{128,1..., dimensions={0} | all-to-all | bytes 2949120 | tf_op jit(solution)/shard_map/all_to_all | solution.py:289
  216.9 0.8 reduce_sum.36
  217.6 0.9 slice.21
  218.5 3.5 %all-to-all-start.7 = ((bf16[8,320,128]{2,1,0:T(8,128)(2,1)}), bf16[8,320,128]{2,1,0:T(8,128)(2,1)S(1)}, u32[]{:S(2)}, u32[]{:S(2)}) async-start(bf16[8,320,128]{2,1,0:T(8,128)(2,1)} %bitcast.17), calls=%async_computation.7 | async-start | bytes 1310720 | tf_op jit(solution)/shard_map/all_to_all | solution.py:289
  222.1 13.1 %all-to-all-done.7 = bf16[8,320,128]{2,1,0:T(8,128)(2,1)S(1)} async-done(((bf16[8,320,128]{2,1,0:T(8,128)(2,1)}), bf16[8,320,128]{2,1,0:T(8,128)(2,1)S(1)}, u32[]{:S(2)}, u32[]{:S(2)}) %all-to-all-start.7) | async-done | bytes 655392 | tf_op jit(solution)/shard_map/all_to_all | solution.py:289
  235.2 0.1 reduce_sum.37
  235.3 10.8 %all_to_all.110 = bf16[8,80,128]{2,1,0:T(8,128)(2,1)S(1)} all-to-all(bf16[8,80,128]{2,1,0:T(8,128)(2,1)S(1)} %pad_maximum_fusion.1), channel_id=1, replica_groups={{0,16,32,48,64,80,96,112},{8,24,40,56,72,88,104,120},{128,144,160,176,1..., dimensions={0} | all-to-all | bytes 327680 | tf_op jit(solution)/shard_map/all_to_all | solution.py:289
  246.1 0.0 copy-start.5
  246.1 0.1 collective-permute-start.3
  246.2 2.6 collective-permute-done.3
  248.9 11.0 %all_to_all.111 = bf16[8,80,128]{2,1,0:T(8,128)(2,1)S(1)} all-to-all(bf16[8,80,128]{2,1,0:T(8,128)(2,1)S(1)} %broadcast_in_dim.11), channel_id=1, replica_groups={{0,16,32,48,64,80,96,112},{8,24,40,56,72,88,104,120},{128,144,160,176,1..., dimensions={0} | all-to-all | bytes 327680 | tf_op jit(solution)/shard_map/all_to_all | solution.py:289
  259.9 0.0 copy-start.3
  259.9 0.9 broadcast_in_dim.25
  260.8 3.5 %all-to-all-start.10 = ((bf16[8,320,128]{2,1,0:T(8,128)(2,1)}), bf16[8,320,128]{2,1,0:T(8,128)(2,1)S(1)}, u32[]{:S(2)}, u32[]{:S(2)}) async-start(bf16[8,320,128]{2,1,0:T(8,128)(2,1)} %broadcast_in_dim.25), calls=%async_computation.10 | async-start | bytes 1310720 | tf_op jit(solution)/shard_map/all_to_all | solution.py:289
  264.4 0.0 copy-done.5
  264.4 0.0 copy-done.3
  264.5 0.2 maximum_bitcast_fusion
  264.6 1.2 copy.21
  265.8 8.3 %all-to-all-done.10 = bf16[8,320,128]{2,1,0:T(8,128)(2,1)S(1)} async-done(((bf16[8,320,128]{2,1,0:T(8,128)(2,1)}), bf16[8,320,128]{2,1,0:T(8,128)(2,1)S(1)}, u32[]{:S(2)}, u32[]{:S(2)}) %all-to-all-start.10) | async-done | bytes 655392 | tf_op jit(solution)/shard_map/all_to_all | solution.py:289
  274.2 0.1 broadcast_in_dim.26
  274.3 10.7 %all_to_all.112.both = bf16[2,2880,128]{2,1,0:T(8,128)(2,1)} all-to-all(bf16[2,2880,128]{2,1,0:T(8,128)(2,1)S(1)} %broadcast_in_dim.26), channel_id=1, replica_groups={{0,8},{16,24},{32,40},{48,56},{64,72},{80,88},{96,104},{112,120},{128,1..., dimensions={0} | all-to-all | bytes 2949120 | tf_op jit(solution)/shard_map/all_to_all | solution.py:289
  285.0 2.7 unpack.1
  (12 shorter events, 0.2 us)
Async XLA Ops:
  43.3 5.2 %copy-start.1 = (bf16[8,128,896]{2,1,0:T(8,128)(2,1)}, bf16[8,128,896]{2,1,0:T(8,128)(2,1)S(1)}, u32[]{:S(2)}) copy-start(bf16[8,128,896]{2,1,0:T(8,128)(2,1)S(1)} %all_to_all.108) | copy-start | bytes 5505028
  43.3 45.2 %collective-permute-start = (bf16[1024,896]{1,0:T(8,128)(2,1)S(1)}, bf16[1024,896]{1,0:T(8,128)(2,1)}, u32[]{:S(2)}, u32[]{:S(2)}) collective-permute-start(bf16[1024,896]{1,0:T(8,128)(2,1)S(1)} %bitcast.29), channel_id=1, source_target_pairs={{0,8},{8,16},{16,24},{24,32},{32,40},{40,48},{48,56},{56,64},{64,7... | collective-permute-start | bytes 5505032 | tf_op jit(solution)/shard_map/ppermute | solution.py:344
  48.5 39.9 %all-to-all-start.1 = ((bf16[8,128,768]{2,1,0:T(8,128)(2,1)}), bf16[8,128,768]{2,1,0:T(8,128)(2,1)S(1)}, u32[]{:S(2)}, u32[]{:S(2)}) async-start(bf16[8,128,768]{2,1,0:T(8,128)(2,1)} %bitcast.40), calls=%async_computation.1 | async-start | bytes 3145728 | tf_op jit(solution)/shard_map/all_to_all | solution.py:289
  88.4 1.2 copy-start.6
  89.6 25.8 %all-to-all-start.3 = ((bf16[8,128,512]{2,1,0:T(8,128)(2,1)}), bf16[8,128,512]{2,1,0:T(8,128)(2,1)S(1)}, u32[]{:S(2)}, u32[]{:S(2)}) async-start(bf16[8,128,512]{2,1,0:T(8,128)(2,1)} %bitcast.47), calls=%async_computation.3 | async-start | bytes 2097152 | tf_op jit(solution)/shard_map/all_to_all | solution.py:289
  115.4 2.9 %copy-start.7 = (bf16[128,5120]{1,0:T(8,128)(2,1)S(1)}, bf16[128,5120]{1,0:T(8,128)(2,1)}, u32[]{:S(2)}) copy-start(bf16[128,5120]{1,0:T(8,128)(2,1)} %tokens.3) | copy-start | bytes 3932164
  115.4 1.0 copy-start
  116.4 45.1 %collective-permute-start.1 = (bf16[1024,512]{1,0:T(8,128)(2,1)}, bf16[1024,512]{1,0:T(8,128)(2,1)}, u32[]{:S(2)}, u32[]{:S(2)}) collective-permute-start(bf16[1024,512]{1,0:T(8,128)(2,1)} %after.6.refs_1_.k_own.v_own), channel_id=1, source_target_pairs={{0,8},{8,16},{16,24},{24,32},{32,40},{40,48},{48,56},{56,64},{64,7... | collective-permute-start | bytes 3145736 | tf_op jit(solution)/shard_map/ppermute | solution.py:351
  118.3 70.0 %collective-permute-start.2 = (bf16[128,5120]{1,0:T(8,128)(2,1)S(1)}, bf16[128,5120]{1,0:T(8,128)(2,1)}, u32[]{:S(2)}, u32[]{:S(2)}) collective-permute-start(bf16[128,5120]{1,0:T(8,128)(2,1)S(1)} %copy-done.7), channel_id=1, source_target_pairs={{0,8},{8,16},{16,24},{24,32},{32,40},{40,48},{48,56},{56,64},{64,7... | collective-permute-start | bytes 3932168 | tf_op jit(solution)/shard_map/ppermute | solution.py:353
  120.2 37.2 %all-to-all-start.4 = ((bf16[8,128,512]{2,1,0:T(8,128)(2,1)}), bf16[8,128,512]{2,1,0:T(8,128)(2,1)S(1)}, u32[]{:S(2)}, u32[]{:S(2)}) async-start(bf16[8,128,512]{2,1,0:T(8,128)(2,1)} %bitcast.46), calls=%async_computation.4 | async-start | bytes 2097152 | tf_op jit(solution)/shard_map/all_to_all | solution.py:289
  157.4 4.0 %copy-start.8 = (bf16[8,128,512]{2,1,0:T(8,128)(2,1)}, bf16[8,128,512]{2,1,0:T(8,128)(2,1)S(1)}, u32[]{:S(2)}) copy-start(bf16[8,128,512]{2,1,0:T(8,128)(2,1)S(1)} %all-to-all-done.4) | copy-start | bytes 3145732
  157.4 24.2 %all-to-all-start.2 = ((bf16[8,128,384]{2,1,0:T(8,128)(2,1)}), bf16[8,128,384]{2,1,0:T(8,128)(2,1)S(1)}, u32[]{:S(2)}, u32[]{:S(2)}) async-start(bf16[8,128,384]{2,1,0:T(8,128)(2,1)} %bitcast.48), calls=%async_computation.2 | async-start | bytes 1572864 | tf_op jit(solution)/shard_map/all_to_all | solution.py:289
  181.6 24.0 %copy-start.2 = (bf16[8,128,384]{2,1,0:T(8,128)(2,1)}, bf16[8,128,384]{2,1,0:T(8,128)(2,1)S(1)}, u32[]{:S(2)}) copy-start(bf16[8,128,384]{2,1,0:T(8,128)(2,1)S(1)} %all-to-all-done.2) | copy-start | bytes 2359300
  181.6 24.0 %all-to-all-start.5 = ((bf16[8,128,512]{2,1,0:T(8,128)(2,1)}), bf16[8,128,512]{2,1,0:T(8,128)(2,1)S(1)}, u32[]{:S(2)}, u32[]{:S(2)}) async-start(bf16[8,128,512]{2,1,0:T(8,128)(2,1)} %bitcast.54), calls=%async_computation.5 | async-start | bytes 2097152 | tf_op jit(solution)/shard_map/all_to_all | solution.py:289
  205.6 1.0 copy-start.4
  218.5 16.7 %all-to-all-start.7 = ((bf16[8,320,128]{2,1,0:T(8,128)(2,1)}), bf16[8,320,128]{2,1,0:T(8,128)(2,1)S(1)}, u32[]{:S(2)}, u32[]{:S(2)}) async-start(bf16[8,320,128]{2,1,0:T(8,128)(2,1)} %bitcast.17), calls=%async_computation.7 | async-start | bytes 1310720 | tf_op jit(solution)/shard_map/all_to_all | solution.py:289
  246.1 18.3 %copy-start.5 = (bf16[8,128,512]{2,1,0:T(8,128)(2,1)S(1)}, bf16[8,128,512]{2,1,0:T(8,128)(2,1)}, u32[]{:S(2)}) copy-start(bf16[8,128,512]{2,1,0:T(8,128)(2,1)} %copy-done.4) | copy-start | bytes 3145732
  246.1 2.7 collective-permute-start.3
  259.9 4.5 %copy-start.3 = (bf16[8,128,384]{2,1,0:T(8,128)(2,1)S(1)}, bf16[8,128,384]{2,1,0:T(8,128)(2,1)}, u32[]{:S(2)}) copy-start(bf16[8,128,384]{2,1,0:T(8,128)(2,1)} %copy-done.2) | copy-start | bytes 2359300
  260.8 13.3 %all-to-all-start.10 = ((bf16[8,320,128]{2,1,0:T(8,128)(2,1)}), bf16[8,320,128]{2,1,0:T(8,128)(2,1)S(1)}, u32[]{:S(2)}, u32[]{:S(2)}) async-start(bf16[8,320,128]{2,1,0:T(8,128)(2,1)} %broadcast_in_dim.25), calls=%async_computation.10 | async-start | bytes 1310720 | tf_op jit(solution)/shard_map/all_to_all | solution.py:289

commit v3 on v2

v3 whole, which is shorter than its diff:
```python
import functools

import jax
import jax.numpy as jnp
from jax import lax
from jax.experimental import pallas as pl
from jax.experimental.pallas import tpu as pltpu
from jax.sharding import PartitionSpec as P

HEAD = 128
TILE = 256
LOG2E = 1.4426950408889634
F32 = jnp.float32
BF16 = jnp.bfloat16
CALLS = (3, 2)

PAIR = [[2 * i, 2 * i + 1] for i in range(16)]
Z_RING = [[half * 16 + z * 2 + core for z in range(8)] for half in range(2) for core in range(2)]
Y_PAIR = [(i, i ^ 16) for i in range(32)]


def dot(left, right):
    return jnp.dot(left, right, preferred_element_type=F32)


def dot_t(left, right):
    return lax.dot_general(left, right, (((1,), (1,)), ((), ())), preferred_element_type=F32)


def t_dot(left, right):
    return lax.dot_general(left, right, (((0,), (0,)), ((), ())), preferred_element_type=F32)


def spread_kernel(array, out):
    out[...] = array[...]


def spread(array, parts):
    rows, columns = array.shape
    width = columns // parts
    return pl.pallas_call(
        spread_kernel,
        grid=(parts,),
        in_specs=[pl.BlockSpec((rows, width), lambda j: (0, j))],
        out_specs=pl.BlockSpec((rows, width), lambda j: (j, 0)),
        out_shape=jax.ShapeDtypeStruct((parts * rows, width), BF16),
        compiler_params=pltpu.CompilerParams(vmem_limit_bytes=60 << 20),
        name="spread",
    )(array)


def pack_kernel(
    tokens, query_base, value_base, out_grad, down_q, down_v, up_q, up_v, vl, qg, copy, low
):
    rank = down_q.shape[0]
    width = value_base.shape[1]

    @pl.when(pl.program_id(0) == 0)
    def _():
        low[:, :rank] = dot_t(tokens[...], down_q[...]).astype(BF16)
        low[:, rank:] = dot_t(tokens[...], down_v[...]).astype(BF16)
        copy[...] = tokens[...]

    vl[:, :width] = (value_base[...].astype(F32) + dot(low[:, rank:], up_v[...])).astype(BF16)
    vl[:, width:] = low[...]
    qg[:, :width] = (query_base[...].astype(F32) + dot(low[:, :rank], up_q[...])).astype(BF16)
    qg[:, width:] = out_grad[...]


def pack(tokens, query_base, value_base, out_grad, down_q, up_q, down_v, up_v, parts):
    rows, columns = tokens.shape
    rank = down_q.shape[0]
    width = columns // parts
    whole = lambda j: (0, 0)
    part = lambda j: (0, j)
    once = pl.Buffered(1)
    sizes = (width + 2 * rank, 2 * width)
    return pl.pallas_call(
        pack_kernel,
        grid=(parts,),
        in_specs=[pl.BlockSpec((rows, columns), whole, pipeline_mode=once)]
        + [pl.BlockSpec((rows, width), part)] * 3
        + [pl.BlockSpec((rank, columns), whole, pipeline_mode=once)] * 2
        + [pl.BlockSpec((rank, width), part)] * 2,
        out_specs=[pl.BlockSpec((rows, size), lambda j: (j, 0)) for size in sizes]
        + [pl.BlockSpec((rows, columns), whole)],
        out_shape=[jax.ShapeDtypeStruct((parts * rows, size), BF16) for size in sizes]
        + [jax.ShapeDtypeStruct((rows, columns), BF16)],
        scratch_shapes=[pltpu.VMEM((rows, 2 * rank), BF16)],
        compiler_params=pltpu.CompilerParams(vmem_limit_bytes=60 << 20),
        cost_estimate=pl.CostEstimate(flops=1 << 29, bytes_accessed=14 << 20, transcendentals=0),
        name="pack",
    )(tokens, query_base, value_base, out_grad, down_q, down_v, up_q, up_v)


def attention_kernel(
    begins, ends, place, q, g, k_own, v_own, k_prior, v_prior, low_own, low_prior, up_q, up_v, *rest
):
    rest = list(rest)
    low_in = None if begins else [rest.pop(0) for _ in range(3)]
    out, ups = rest.pop(0), rest.pop(0)
    low_out = None if ends else [rest.pop(0) for _ in range(3)]
    lq, lo, lp, dv_own, dv_prior = rest
    head = pl.program_id(0)
    heads = pl.num_programs(0)
    rows = q.shape[0]
    rank = up_q.shape[0]
    scale = HEAD ** (-0.5)
    factor = scale * LOG2E
    has_prior = place[1] > 0

    @pl.when(head == 0)
    def _():
        if begins:
            lq[...] = jnp.zeros_like(lq)
            lo[...] = jnp.zeros_like(lo)
            lp[...] = jnp.zeros_like(lp)
        else:
            lq[...] = low_in[0][...]
            lo[...] = low_in[1][...]
            lp[...] = low_in[2][...]

    def softmax(step):
        here = slice(step * TILE, (step + 1) * TILE)
        q_t = q[here, :]
        s_own = dot_t(q_t, k_own[...])
        s_prior = dot_t(q_t, k_prior[...])
        top_own = jnp.max(s_own, axis=1, keepdims=True)
        top_prior = jnp.max(s_prior, axis=1, keepdims=True)
        top = jnp.where(has_prior, jnp.maximum(top_own, top_prior), top_own) * factor
        top_p = jnp.where(has_prior, top, jnp.float32(1e38))
        p_own = jnp.exp2(s_own * factor - top)
        p_prior = jnp.exp2(s_prior * factor - top_p)
        total = jnp.sum(p_own, axis=1, keepdims=True) + jnp.sum(p_prior, axis=1, keepdims=True)
        return here, p_own.astype(BF16), p_prior.astype(BF16), 1.0 / total

    up_q_grad = jnp.zeros((rank, HEAD), F32)
    steps = rows // TILE
    following = softmax(0)
    for step in range(steps):
        here, p_own, p_prior, inverse = following
        if step + 1 < steps:
            following = softmax(step + 1)
        g_t = g[here, :]
        attended = ((dot(p_own, v_own[...]) + dot(p_prior, v_prior[...])) * inverse).astype(BF16)
        if ends:
            out[here, pl.ds(pl.multiple_of(head * HEAD, HEAD), HEAD)] = attended
        else:
            out[here, :] = attended
        delta = jnp.sum(g_t.astype(F32) * attended.astype(F32), axis=1, keepdims=True)
        ds_own = (p_own.astype(F32) * (dot_t(g_t, v_own[...]) - delta)).astype(BF16)
        ds_prior = (p_prior.astype(F32) * (dot_t(g_t, v_prior[...]) - delta)).astype(BF16)
        dq = ((dot(ds_own, k_own[...]) + dot(ds_prior, k_prior[...])) * (inverse * scale)).astype(
            BF16
        )
        scaled = (g_t.astype(F32) * inverse).astype(BF16)
        if step == 0:
            dv_own[...] = t_dot(scaled, p_own)
            dv_prior[...] = t_dot(scaled, p_prior)
        else:
            dv_own[...] += t_dot(scaled, p_own)
            dv_prior[...] += t_dot(scaled, p_prior)
        lq[here, :] += dot_t(dq, up_q[...])
        up_q_grad += t_dot(low_own[here, :rank], dq)
    own = dv_own[...].astype(BF16)
    prior = dv_prior[...].astype(BF16)
    lo[...] += dot(up_v[...], own)
    lp[...] += dot(up_v[...], prior)
    ups[0] = up_q_grad.astype(BF16)
    ups[1] = (dot(own, low_own[:, rank:]) + dot(prior, low_prior[:, rank:])).T.astype(BF16)

    @pl.when(head == heads - 1)
    def _():
        if ends:
            first = out.shape[1] - 4 * rank
            out[:, first : first + rank] = lq[...].astype(BF16)
            out[:, first + rank : first + 2 * rank] = lo[...].T.astype(BF16)
            out[:, first + 2 * rank : first + 3 * rank] = lp[...].T.astype(BF16)
            out[:, first + 3 * rank :] = jnp.zeros((rows, rank), BF16)
        else:
            low_out[0][...] = lq[...]
            low_out[1][...] = lo[...]
            low_out[2][...] = lp[...]


def attention(place, qg, k, k_prior, vl, vl_prior, up_q, up_v, lows, first, heads, ends):
    rows = qg.shape[0]
    total = k.shape[1] // HEAD
    rank = up_q.shape[0]
    begins = lows is None
    column = lambda offset: pl.BlockSpec((rows, HEAD), lambda h, place: (0, first + h + offset))
    fixed = pl.BlockSpec((rows, HEAD), lambda h, place: (0, total))
    up = pl.BlockSpec((rank, HEAD), lambda h, place: (0, place[0] * total + first + h))
    shapes = ((rows, rank), (rank, rows), (rank, rows))
    whole = lambda shape: pl.BlockSpec(shape, lambda h, place: (0, 0))
    width = heads * HEAD
    out_width = width + 4 * rank if ends else width
    out_specs = [
        whole((rows, out_width)) if ends else pl.BlockSpec((rows, HEAD), lambda h, place: (0, h)),
        pl.BlockSpec((2, rank, HEAD), lambda h, place: (0, h, 0)),
    ]
    out_shape = [
        jax.ShapeDtypeStruct((rows, out_width), BF16),
        jax.ShapeDtypeStruct((2, heads * rank, HEAD), BF16),
    ]
    if not ends:
        out_specs += [whole(shape) for shape in shapes]
        out_shape += [jax.ShapeDtypeStruct(shape, F32) for shape in shapes]
    return pl.pallas_call(
        functools.partial(attention_kernel, begins, ends),
        grid_spec=pltpu.PrefetchScalarGridSpec(
            num_scalar_prefetch=1,
            grid=(heads,),
            in_specs=[
                column(0),
                column(total),
                column(0),
                column(0),
                column(0),
                column(0),
                fixed,
                fixed,
                up,
                up,
            ]
            + ([] if begins else [whole(shape) for shape in shapes]),
            out_specs=out_specs,
            scratch_shapes=[pltpu.VMEM(shape, F32) for shape in shapes]
            + [pltpu.VMEM((HEAD, rows), F32)] * 2,
        ),
        out_shape=out_shape,
        compiler_params=pltpu.CompilerParams(vmem_limit_bytes=60 << 20),
        cost_estimate=pl.CostEstimate(
            flops=5 * 2 * heads * rows * 2 * rows * HEAD * 4,
            bytes_accessed=heads << 21,
            transcendentals=heads * rows * 2 * rows,
        ),
        name="attention",
    )(
        place, qg, qg, k, vl, k_prior, vl_prior, vl, vl_prior, up_q, up_v,
        *(() if begins else lows),
    )


def outer_kernel(lows, tokens, earlier, *rest):
    ups, out = rest[:-2], rest[-1]
    rows, columns = tokens.shape
    rank = lows.shape[1] // 4
    low = jnp.sum(lows[...].reshape(-1, rows, 4 * rank).astype(F32), axis=0).astype(BF16)
    grad_q = t_dot(low[:, :rank], tokens[...])
    grad_v = t_dot(low[:, rank : 2 * rank], tokens[...]) + t_dot(
        low[:, 2 * rank : 3 * rank], earlier[...]
    )
    for block in range(columns // HEAD):
        to = slice(block * rank, (block + 1) * rank)
        out[0, to, :] = grad_q[:, block * HEAD : (block + 1) * HEAD].astype(BF16)
        out[1, to, :] = grad_v[:, block * HEAD : (block + 1) * HEAD].astype(BF16)
    first = columns // HEAD * rank
    for up in ups:
        size = up.shape[1]
        out[:, first : first + size, :] = up[...]
        first += size


def outer(lows, tokens, earlier, ups, rank, settled):
    length = tokens.shape[1] // HEAD * rank + sum(up.shape[1] for up in ups)
    whole = lambda array: pl.BlockSpec(array.shape, lambda i: (0,) * array.ndim)
    at = lows.shape[1] // (4 * rank) - 1
    return pl.pallas_call(
        outer_kernel,
        grid=(1,),
        in_specs=[pl.BlockSpec((lows.shape[0], 4 * rank), lambda i: (0, at))]
        + [whole(array) for array in (tokens, earlier, *ups)]
        + [pl.BlockSpec(memory_space=pl.ANY)],
        out_specs=pl.BlockSpec((2, length, HEAD), lambda i: (0, 0, 0)),
        out_shape=jax.ShapeDtypeStruct((2, length, HEAD), BF16),
        compiler_params=pltpu.CompilerParams(vmem_limit_bytes=60 << 20),
        cost_estimate=pl.CostEstimate(flops=1 << 29, bytes_accessed=8 << 20, transcendentals=0),
        name="outer",
    )(lows, tokens, earlier, *ups, settled)


def unpack_kernel(both, down_q, down_v, up_q, up_v):
    rank, columns = down_q.shape
    first = columns // HEAD * rank
    for part, (down, up) in enumerate(((down_q, up_q), (down_v, up_v))):
        for block in range(columns // HEAD):
            down[:, block * HEAD : (block + 1) * HEAD] = both[
                part, block * rank : (block + 1) * rank, :
            ]
        for block in range(up.shape[1] // HEAD):
            up[:, block * HEAD : (block + 1) * HEAD] = both[
                part, first + block * rank : first + (block + 1) * rank, :
            ]


def unpack(both, rank, columns, width):
    return pl.pallas_call(
        unpack_kernel,
        out_shape=[jax.ShapeDtypeStruct((rank, columns), BF16)] * 2
        + [jax.ShapeDtypeStruct((rank, width), BF16)] * 2,
        compiler_params=pltpu.CompilerParams(vmem_limit_bytes=60 << 20),
        name="unpack",
    )(both)


def exchange(array, axis, groups=None):
    return lax.all_to_all(
        array, axis, split_axis=0, concat_axis=0, tiled=True, axis_index_groups=groups
    )


def summed(array, axis, size, groups=None):
    got = exchange(array, axis, groups)
    return jnp.sum(got.reshape(size, -1, array.shape[1]).astype(F32), axis=0).astype(BF16)


def gathered(array, axis, size, groups=None):
    copies = jnp.broadcast_to(array[None], (size,) + array.shape)
    return exchange(copies.reshape(-1, array.shape[1]), axis, groups)


def after(array, *others):
    return pl.pallas_call(
        lambda *refs: None,
        in_specs=[pl.BlockSpec(memory_space=pl.ANY)] * (1 + len(others)),
        out_specs=pl.BlockSpec(memory_space=pl.ANY),
        out_shape=jax.ShapeDtypeStruct(array.shape, array.dtype),
        input_output_aliases={0: 0},
        name="after",
    )(array, *others)


def shifted(array, blocks):
    wrap = blocks // 2 - 1
    half = array.shape[0] // 2
    direct = lax.ppermute(
        array, "blk", [(i, i + 1) for i in range(blocks - 1) if i != wrap]
    )
    upper = lax.ppermute(array[:half], "blk", [(wrap, wrap + 1)])
    lower = lax.ppermute(array[half:], "blk", [(wrap, blocks - 1)])
    lower = lax.ppermute(lower, "blk", [(blocks - 1, wrap + 1)])
    return direct + jnp.concatenate([upper, lower], 0)


def per_device(tokens, query_base, key_base, value_base, out_grad, down_q, up_q, down_v, up_v):
    blocks = lax.axis_size("blk")
    parts = lax.axis_size("uly")
    rows, columns = tokens.shape
    rank = down_q.shape[1]
    width = columns // parts
    vl, qg, copy = pack(
        tokens, query_base, value_base, out_grad, down_q.T, up_q, down_v.T, up_v, parts
    )
    k = exchange(spread(key_base, parts), "uly")
    k_prior = shifted(k, blocks)
    vl = exchange(vl, "uly")
    vl_prior = shifted(vl, blocks)
    qg = exchange(after(qg, vl), "uly")
    earlier = lax.ppermute(
        after(copy, vl_prior), "blk", [(i, i + 1) for i in range(blocks - 1)]
    )
    place = jnp.stack([lax.axis_index("uly"), lax.axis_index("blk")]).astype(jnp.int32)
    ready = (place, qg, k, k_prior, vl, vl_prior, up_q, up_v)
    out, ups_a, *lows = attention(*ready, None, 0, CALLS[0], False)
    piece = exchange(out, "uly")
    out, ups_b = attention(*ready, lows, CALLS[0], CALLS[1], True)
    back = exchange(out, "uly")
    pieces = (piece, back)
    both = outer(back, tokens, earlier, (ups_a, ups_b), rank, piece)
    both = summed(both.reshape(-1, HEAD), "blk", 2, PAIR)
    length = columns // HEAD * rank
    down = summed(both[:length], "uly", parts)
    piece = length // parts // 8
    both = jnp.concatenate(
        [down.reshape(8, piece, HEAD), both[length:].reshape(8, -1, HEAD)], 1
    ).reshape(-1, HEAD)
    both = summed(both, "blk", 8, Z_RING)
    both = (both.astype(F32) + lax.ppermute(both, "blk", Y_PAIR).astype(F32)).astype(BF16)
    both = gathered(both, "blk", 8, Z_RING).reshape(8, -1, HEAD)
    down = gathered(both[:, :piece].reshape(-1, HEAD), "uly", parts)
    both = jnp.concatenate([down, both[:, piece:].reshape(-1, HEAD)], 0)
    both = gathered(both, "blk", 2, PAIR).reshape(2, -1, HEAD)
    down_q, down_v, up_q, up_v = unpack(both, rank, columns, width)
    attended = jnp.concatenate(
        [
            p.reshape(parts, rows, -1)[:, :, : heads * HEAD]
            for p, heads in zip(pieces, CALLS)
        ],
        2,
    )
    attended = attended.transpose(1, 0, 2).reshape(rows, columns)
    return (attended, down_q.T, up_q, down_v.T, up_v)


def solution(mesh):
    rows = P(("blk", "uly"), None)
    return jax.shard_map(
        per_device,
        mesh=mesh,
        in_specs=(rows,) * 5 + (P(),) * 4,
        out_specs=(rows, P(), P(None, "uly"), P(), P(None, "uly")),
        check_vma=False,
    )
```

time: 289 us -> 286 us (0.990)
  starting transfers between devices: 41.5 us -> 57.8 us
  blocking collectives: 71.3 us -> 57.1 us
  other arithmetic: 1.68 us -> 8.06 us
  waiting for transfers between devices: 96.1 us -> 89.8 us
  Pallas kernels: 68.8 us -> 64.8 us
    all_to_all x5 -> x4, blocking collectives: 71.3 us -> 57.1 us  [exchange(): lax.all_to_all(array, axis, split_axis=0, concat_axis=0, tiled=True, axis...]
    all_to_all x7, waiting for transfers between devices: 93.5 us -> 80.2 us  [exchange(): lax.all_to_all(array, axis, split_axis=0, concat_axis=0, tiled=True, axis...]
    ppermute x3 -> x9, starting transfers between devices: 9.05 us -> 21.5 us  [the longest x2 8.52 us: shifted(): lax.ppermute(array, 'blk', [(i, i + 1) for i in range(blocks - 1) if i !=...]
    ppermute x3 -> x9, waiting for transfers between devices: 0.01 us -> 8.49 us  [the longest x2 8.47 us: shifted(): lax.ppermute(array, 'blk', [(i, i + 1) for i in range(blocks - 1) if i !=...]
    add x0 -> x2, other arithmetic: none -> 6.38 us  [shifted(): return direct + jnp.concatenate([upper, lower], 0)]
    pallas_call x3, Pallas kernels: 52 us -> 48.3 us  [the longest x2 42.9 us: attention(): pl.pallas_call(functools.partial(attention_kernel, begins, ends), grid_sp...]
  transfers between devices with their start and end apart: 11 -> 17, of which waited for: 6 -> 9; matrix products, arithmetic and copies ran while one was open for 1% -> 3% of each run, Pallas kernels for 18% -> 19%
where the time goes in v3:
time: 286 us; the launch traced here: 285 us
  waiting for transfers between devices  89.8 us (31%)
  Pallas kernels  64.8 us (23%)
  starting transfers between devices  57.8 us (20%)
  blocking collectives  57.1 us (20%)
  other arithmetic  8.06 us (3%)
  local copies, waits for them, and re-layouts  6.57 us (2%)
    all_to_all x7, waiting for transfers between devices, exchange(): lax.all_to_all(array, axis, split_axis=0, concat_axis=0, tiled=True, axis...  80.2 us
    all_to_all x4, blocking collectives, exchange(): lax.all_to_all(array, axis, split_axis=0, concat_axis=0, tiled=True, axis...  57.1 us
    pallas_call x2, Pallas kernels, attention(): pl.pallas_call(functools.partial(attention_kernel, begins, ends), grid_sp...  42.9 us
    all_to_all x7, starting transfers between devices, exchange(): lax.all_to_all(array, axis, split_axis=0, concat_axis=0, tiled=True, axis...  34.6 us
    pallas_call x1, Pallas kernels, pack(): pl.pallas_call(pack_kernel, grid=(parts,), in_specs=[pl.BlockSpec((rows,...  10.1 us
    ppermute x2, starting transfers between devices, shifted(): lax.ppermute(array, 'blk', [(i, i + 1) for i in range(blocks - 1) if i !=...  8.52 us
    ppermute x2, waiting for transfers between devices, shifted(): lax.ppermute(array, 'blk', [(i, i + 1) for i in range(blocks - 1) if i !=...  8.47 us
    add x2, other arithmetic, shifted(): return direct + jnp.concatenate([upper, lower], 0)  6.38 us
  transfers between devices with their start and end apart: 17, of which 9 were waited for; matrix products, arithmetic and copies ran while one was open for 3% of the time, Pallas kernels for 19%

profile of v3, /device:TPU:1, one launch (start us, length us, event | category | flops | bytes accessed | tf_op | source)
XLA Modules:
  0.0 285.1 jit_solution(713727491231813016)
XLA Ops:
  0.6 5.3 %spread.1 = bf16[1024,640]{1,0:T(8,128)(2,1)} custom-call(bf16[128,5120]{1,0:T(8,128)(2,1)} %array.1), custom_call_target="tpu_custom_call" | custom-call | tf_op jit(solution)/shard_map/spread/pallas_call | solution.py:41
  6.0 7.5 %all-to-all-start.2 = ((bf16[8,128,640]{2,1,0:T(8,128)(2,1)}), bf16[8,128,640]{2,1,0:T(8,128)(2,1)S(1)}, u32[]{:S(2)}, u32[]{:S(2)}) async-start(bf16[8,128,640]{2,1,0:T(8,128)(2,1)} %bitcast.42), calls=%async_computation.2 | async-start | bytes 2621440 | tf_op jit(solution)/shard_map/all_to_all | solution.py:308
  13.4 10.1 %pack.1 = (bf16[1024,768]{1,0:T(8,128)(2,1)}, bf16[1024,1280]{1,0:T(8,128)(2,1)}, bf16[128,5120]{1,0:T(8,128)(2,1)}) custom-call(bf16[128,5120]{1,0:T(8,128)(2,1)} %tokens.3, bf16[128,5120]{1,0:T(8,128)(2,1)} %query_base.1, bf16[128,5120]{1,0:T(8,128)(2,1)} %value_base.1, bf16[128,5120]{1,0:T(8,128)(2,1)} %out_grad.1, bf16[64,5120]{1,0:T(8,128)(2,1)} %bitcast.51, ...), custom_call_target="tpu_custom_call" | custom-call | flops 536870912 | bytes 14680064 | tf_op jit(solution)/shard_map/pack/pallas_call | solution.py:78
  23.5 10.1 %all-to-all-done.2 = bf16[8,128,640]{2,1,0:T(8,128)(2,1)S(1)} async-done(((bf16[8,128,640]{2,1,0:T(8,128)(2,1)}), bf16[8,128,640]{2,1,0:T(8,128)(2,1)S(1)}, u32[]{:S(2)}, u32[]{:S(2)}) %all-to-all-start.2) | async-done | bytes 1310752 | tf_op jit(solution)/shard_map/all_to_all | solution.py:308
  33.6 3.6 %all-to-all-start = ((bf16[8,128,768]{2,1,0:T(8,128)(2,1)}), bf16[8,128,768]{2,1,0:T(8,128)(2,1)S(1)}, u32[]{:S(2)}, u32[]{:S(2)}) async-start(bf16[8,128,768]{2,1,0:T(8,128)(2,1)} %bitcast.44), calls=%async_computation | async-start | bytes 3145728 | tf_op jit(solution)/shard_map/all_to_all | solution.py:308
  37.2 4.3 %collective-permute-start = (bf16[1024,640]{1,0:T(8,128)(2,1)S(1)}, bf16[1024,640]{1,0:T(8,128)(2,1)}, u32[]{:S(2)}, u32[]{:S(2)}) collective-permute-start(bf16[1024,640]{1,0:T(8,128)(2,1)S(1)} %bitcast.39), channel_id=1, source_target_pairs={{0,8},{8,16},{16,24},{24,32},{32,40},{40,48},{48,56},{56,64},{64,7... | collective-permute-start | bytes 3932168 | tf_op jit(solution)/shard_map/ppermute | solution.py:337
  41.4 18.6 %all-to-all-done = bf16[8,128,768]{2,1,0:T(8,128)(2,1)S(1)} async-done(((bf16[8,128,768]{2,1,0:T(8,128)(2,1)}), bf16[8,128,768]{2,1,0:T(8,128)(2,1)S(1)}, u32[]{:S(2)}, u32[]{:S(2)}) %all-to-all-start) | async-done | bytes 1572896 | tf_op jit(solution)/shard_map/all_to_all | solution.py:308
  60.0 1.2 copy-done
  61.2 4.4 %all-to-all-start.1 = ((bf16[8,128,1280]{2,1,0:T(8,128)(2,1)}), bf16[8,128,1280]{2,1,0:T(8,128)(2,1)}, u32[]{:S(2)}, u32[]{:S(2)}) async-start(bf16[8,128,1280]{2,1,0:T(8,128)(2,1)} %bitcast.36), calls=%async_computation.1 | async-start | bytes 5242880 | tf_op jit(solution)/shard_map/all_to_all | solution.py:308
  65.6 0.0 copy-done.6
  65.6 0.0 copy-start.1
  65.7 0.1 fusion.1
  65.8 1.6 collective-permute-start.2
  67.4 0.0 copy-done.1
  67.4 1.1 fusion
  68.5 1.5 collective-permute-start.6
  70.0 4.2 %collective-permute-start.4 = (bf16[1024,768]{1,0:T(8,128)(2,1)S(1)}, bf16[1024,768]{1,0:T(8,128)(2,1)}, u32[]{:S(2)}, u32[]{:S(2)}) collective-permute-start(bf16[1024,768]{1,0:T(8,128)(2,1)S(1)} %bitcast.35), channel_id=1, source_target_pairs={{0,8},{8,16},{16,24},{24,32},{32,40},{40,48},{48,56},{56,64},{64,7... | collective-permute-start | bytes 4718600 | tf_op jit(solution)/shard_map/ppermute | solution.py:337
  74.3 0.7 collective-permute-start.1
  75.0 0.0 collective-permute-done.2
  75.0 1.5 collective-permute-start.3
  76.5 0.0 collective-permute-done.1
  76.5 1.6 collective-permute-start.5
  78.1 0.0 collective-permute-done.6
  78.1 1.5 collective-permute-start.7
  79.6 0.6 pad_add_fusion.place
  80.2 0.0 collective-permute-done
  80.2 0.0 collective-permute-done.3
  80.2 2.9 %maximum_add_fusion.1.k_prior = bf16[1024,640]{1,0:T(8,128)(2,1)} fusion(bf16[1024,640]{1,0:T(8,128)(2,1)} %collective-permute-done, bf16[512,640]{1,0:T(8,128)(2,1)} %collective-permute-done.3, bf16[512,640]{1,0:T(8,128)(2,1)S(1)} %collective-permute-done.1), kind=kLoop, calls=%fused_computation.1 | loop fusion | flops 3932160 | bytes 3932160 | tf_op jit(solution)/shard_map/add | solution.py:343
  83.1 0.0 collective-permute-done.5
  83.1 0.0 collective-permute-done.7
  83.1 8.5 %collective-permute-done.4 = bf16[1024,768]{1,0:T(8,128)(2,1)} collective-permute-done((bf16[1024,768]{1,0:T(8,128)(2,1)S(1)}, bf16[1024,768]{1,0:T(8,128)(2,1)}, u32[]{:S(2)}, u32[]{:S(2)}) %collective-permute-start.4) | collective-permute-done | bytes 1572896 | tf_op jit(solution)/shard_map/ppermute | solution.py:337
  91.6 3.5 %maximum_add_fusion.v_prior.low_prior.refs_1_ = bf16[1024,768]{1,0:T(8,128)(2,1)} fusion(bf16[1024,768]{1,0:T(8,128)(2,1)} %collective-permute-done.4, bf16[512,768]{1,0:T(8,128)(2,1)} %collective-permute-done.7, bf16[512,768]{1,0:T(8,128)(2,1)} %collective-permute-done.5), kind=kLoop, calls=%fused_computation | loop fusion | flops 4718592 | bytes 4718592 | tf_op jit(solution)/shard_map/add | solution.py:343
  95.1 4.5 %collective-permute-start.8 = (bf16[128,5120]{1,0:T(8,128)(2,1)}, bf16[128,5120]{1,0:T(8,128)(2,1)S(1)}, u32[]{:S(2)}, u32[]{:S(2)}) collective-permute-start(bf16[128,5120]{1,0:T(8,128)(2,1)} %after.3), channel_id=1, source_target_pairs={{0,8},{8,16},{16,24},{24,32},{32,40},{40,48},{48,56},{56,64},{64,7... | collective-permute-start | bytes 3932168 | tf_op jit(solution)/shard_map/ppermute | solution.py:360
  99.6 5.5 %all-to-all-done.1 = bf16[8,128,1280]{2,1,0:T(8,128)(2,1)} async-done(((bf16[8,128,1280]{2,1,0:T(8,128)(2,1)}), bf16[8,128,1280]{2,1,0:T(8,128)(2,1)}, u32[]{:S(2)}, u32[]{:S(2)}) %all-to-all-start.1) | async-done | bytes 2621472 | tf_op jit(solution)/shard_map/all_to_all | solution.py:308
  105.1 24.7 %attention.2 = (bf16[1024,384]{1,0:T(8,128)(2,1)}, bf16[2,192,128]{2,1,0:T(8,128)(2,1)}, f32[1024,64]{1,0:T(8,128)}, f32[64,1024]{1,0:T(8,128)}, f32[64,1024]{1,0:T(8,128)}) custom-call(s32[2]{0:T(128)} %pad_add_fusion.place, bf16[1024,1280]{1,0:T(8,128)(2,1)} %bitcast.7.q.g, bf16[1024,1280]{1,0:T(8,128)(2,1)} %bitcast.7.q.g, bf16[1024,640]{1,0:T(8,128)(2,1)} %bitcast.40, ...), custom_call_target="tpu_custom_call" | custom-call | flops 32212254720 | bytes 6291456 | tf_op jit(solution)/shard_map/attention/pallas_call | solution.py:209
  129.8 8.1 %all-to-all-start.3 = ((bf16[8,128,384]{2,1,0:T(8,128)(2,1)}), bf16[8,128,384]{2,1,0:T(8,128)(2,1)S(1)}, u32[]{:S(2)}, u32[]{:S(2)}) async-start(bf16[8,128,384]{2,1,0:T(8,128)(2,1)} %bitcast.47), calls=%async_computation.3 | async-start | bytes 1572864 | tf_op jit(solution)/shard_map/all_to_all | solution.py:308
  137.8 18.3 %attention.3 = (bf16[1024,512]{1,0:T(8,128)(2,1)}, bf16[2,128,128]{2,1,0:T(8,128)(2,1)}) custom-call(s32[2]{0:T(128)} %pad_add_fusion.place, bf16[1024,1280]{1,0:T(8,128)(2,1)} %bitcast.7.q.g, bf16[1024,1280]{1,0:T(8,128)(2,1)} %bitcast.7.q.g, bf16[1024,640]{1,0:T(8,128)(2,1)} %bitcast.41, bf16[1024,768]{1,0:T(8,128)(2,1)} %bitcast.33, ...), custom_call_target="tpu_custom_call" | custom-call | flops 21474836480 | bytes 4194304 | tf_op jit(solution)/shard_map/attention/pallas_call | solution.py:209
  156.1 7.2 %all-to-all-done.3 = bf16[8,128,384]{2,1,0:T(8,128)(2,1)S(1)} async-done(((bf16[8,128,384]{2,1,0:T(8,128)(2,1)}), bf16[8,128,384]{2,1,0:T(8,128)(2,1)S(1)}, u32[]{:S(2)}, u32[]{:S(2)}) %all-to-all-start.3) | async-done | bytes 786464 | tf_op jit(solution)/shard_map/all_to_all | solution.py:308
  163.3 4.0 %all-to-all-start.4 = ((bf16[8,128,512]{2,1,0:T(8,128)(2,1)}), bf16[8,128,512]{2,1,0:T(8,128)(2,1)S(1)}, u32[]{:S(2)}, u32[]{:S(2)}) async-start(bf16[8,128,512]{2,1,0:T(8,128)(2,1)} %bitcast.46), calls=%async_computation.4 | async-start | bytes 2097152 | tf_op jit(solution)/shard_map/all_to_all | solution.py:308
  167.3 0.0 collective-permute-done.8.earlier
  167.3 0.0 copy-start.7
  167.3 17.3 %all-to-all-done.4 = bf16[8,128,512]{2,1,0:T(8,128)(2,1)S(1)} async-done(((bf16[8,128,512]{2,1,0:T(8,128)(2,1)}), bf16[8,128,512]{2,1,0:T(8,128)(2,1)S(1)}, u32[]{:S(2)}, u32[]{:S(2)}) %all-to-all-start.4) | async-done | bytes 1048608 | tf_op jit(solution)/shard_map/all_to_all | solution.py:308
  184.7 1.0 copy-done.4
  185.6 3.8 %outer.1 = bf16[2,2880,128]{2,1,0:T(8,128)(2,1)} custom-call(bf16[1024,512]{1,0:T(8,128)(2,1)} %bitcast.38, bf16[128,5120]{1,0:T(8,128)(2,1)} %tokens.3, bf16[128,5120]{1,0:T(8,128)(2,1)} %copy-done.7, bf16[2,192,128]{2,1,0:T(8,128)(2,1)} %get-tuple-element.27.rest_0_, bf16[2,128,128]{2,1,0:T(8,128)(2,1)} %get-tuple-element.28.rest_1_, ...), custom_call_target="tpu_custom_call" | custom-call | flops 536870912 | bytes 8388608 | tf_op jit(solution)/shard_map/outer/pallas_call | solution.py:269
  189.4 6.5 %all_to_all.97 = bf16[2,2880,128]{2,1,0:T(8,128)(2,1)S(1)} all-to-all(bf16[2,2880,128]{2,1,0:T(8,128)(2,1)} %outer.1), channel_id=1, replica_groups={{0,8},{16,24},{32,40},{48,56},{64,72},{80,88},{96,104},{112,120},{128,1..., dimensions={0} | all-to-all | bytes 2949120 | tf_op jit(solution)/shard_map/all_to_all | solution.py:308
  195.9 0.8 reduce_sum.36
  196.7 0.9 slice.57
  197.5 3.5 %all-to-all-start.6 = ((bf16[8,320,128]{2,1,0:T(8,128)(2,1)}), bf16[8,320,128]{2,1,0:T(8,128)(2,1)S(1)}, u32[]{:S(2)}, u32[]{:S(2)}) async-start(bf16[8,320,128]{2,1,0:T(8,128)(2,1)} %bitcast.19), calls=%async_computation.6 | async-start | bytes 1310720 | tf_op jit(solution)/shard_map/all_to_all | solution.py:308
  201.1 13.1 %all-to-all-done.6 = bf16[8,320,128]{2,1,0:T(8,128)(2,1)S(1)} async-done(((bf16[8,320,128]{2,1,0:T(8,128)(2,1)}), bf16[8,320,128]{2,1,0:T(8,128)(2,1)S(1)}, u32[]{:S(2)}, u32[]{:S(2)}) %all-to-all-start.6) | async-done | bytes 655392 | tf_op jit(solution)/shard_map/all_to_all | solution.py:308
  214.2 0.1 reduce_sum.37
  214.3 28.7 %all_to_all.98 = bf16[8,80,128]{2,1,0:T(8,128)(2,1)S(1)} all-to-all(bf16[8,80,128]{2,1,0:T(8,128)(2,1)S(1)} %pad_maximum_fusion.1), channel_id=1, replica_groups={{0,16,32,48,64,80,96,112},{8,24,40,56,72,88,104,120},{128,144,160,176,1..., dimensions={0} | all-to-all | bytes 327680 | tf_op jit(solution)/shard_map/all_to_all | solution.py:308
  243.1 1.8 collective-permute-start.9
  244.8 1.2 collective-permute-done.9
  246.1 10.9 %all_to_all.99 = bf16[8,80,128]{2,1,0:T(8,128)(2,1)S(1)} all-to-all(bf16[8,80,128]{2,1,0:T(8,128)(2,1)S(1)} %broadcast_in_dim.8), channel_id=1, replica_groups={{0,16,32,48,64,80,96,112},{8,24,40,56,72,88,104,120},{128,144,160,176,1..., dimensions={0} | all-to-all | bytes 327680 | tf_op jit(solution)/shard_map/all_to_all | solution.py:308
  257.0 0.0 copy-start.3
  257.0 0.9 broadcast_in_dim.10
  257.9 3.5 %all-to-all-start.9 = ((bf16[8,320,128]{2,1,0:T(8,128)(2,1)}), bf16[8,320,128]{2,1,0:T(8,128)(2,1)S(1)}, u32[]{:S(2)}, u32[]{:S(2)}) async-start(bf16[8,320,128]{2,1,0:T(8,128)(2,1)} %broadcast_in_dim.10), calls=%async_computation.9 | async-start | bytes 1310720 | tf_op jit(solution)/shard_map/all_to_all | solution.py:308
  261.4 0.0 copy-done.5
  261.5 0.2 maximum_bitcast_fusion
  261.7 1.2 copy.18
  262.9 8.3 %all-to-all-done.9 = bf16[8,320,128]{2,1,0:T(8,128)(2,1)S(1)} async-done(((bf16[8,320,128]{2,1,0:T(8,128)(2,1)}), bf16[8,320,128]{2,1,0:T(8,128)(2,1)S(1)}, u32[]{:S(2)}, u32[]{:S(2)}) %all-to-all-start.9) | async-done | bytes 655392 | tf_op jit(solution)/shard_map/all_to_all | solution.py:308
  271.3 0.1 broadcast_in_dim.22
  271.4 11.0 %all_to_all.100.both = bf16[2,2880,128]{2,1,0:T(8,128)(2,1)} all-to-all(bf16[2,2880,128]{2,1,0:T(8,128)(2,1)S(1)} %broadcast_in_dim.22), channel_id=1, replica_groups={{0,8},{16,24},{32,40},{48,56},{64,72},{80,88},{96,104},{112,120},{128,1..., dimensions={0} | all-to-all | bytes 2949120 | tf_op jit(solution)/shard_map/all_to_all | solution.py:308
  282.3 2.7 unpack.1
  (18 shorter events, 0.2 us)
Async XLA Ops:
  6.0 27.6 %all-to-all-start.2 = ((bf16[8,128,640]{2,1,0:T(8,128)(2,1)}), bf16[8,128,640]{2,1,0:T(8,128)(2,1)S(1)}, u32[]{:S(2)}, u32[]{:S(2)}) async-start(bf16[8,128,640]{2,1,0:T(8,128)(2,1)} %bitcast.42), calls=%async_computation.2 | async-start | bytes 2621440 | tf_op jit(solution)/shard_map/all_to_all | solution.py:308
  33.6 32.1 %copy-start.6 = (bf16[8,128,640]{2,1,0:T(8,128)(2,1)}, bf16[8,128,640]{2,1,0:T(8,128)(2,1)S(1)}, u32[]{:S(2)}) copy-start(bf16[8,128,640]{2,1,0:T(8,128)(2,1)S(1)} %all-to-all-done.2) | copy-start | bytes 3932164
  33.6 26.5 %all-to-all-start = ((bf16[8,128,768]{2,1,0:T(8,128)(2,1)}), bf16[8,128,768]{2,1,0:T(8,128)(2,1)S(1)}, u32[]{:S(2)}, u32[]{:S(2)}) async-start(bf16[8,128,768]{2,1,0:T(8,128)(2,1)} %bitcast.44), calls=%async_computation | async-start | bytes 3145728 | tf_op jit(solution)/shard_map/all_to_all | solution.py:308
  37.2 43.1 %collective-permute-start = (bf16[1024,640]{1,0:T(8,128)(2,1)S(1)}, bf16[1024,640]{1,0:T(8,128)(2,1)}, u32[]{:S(2)}, u32[]{:S(2)}) collective-permute-start(bf16[1024,640]{1,0:T(8,128)(2,1)S(1)} %bitcast.39), channel_id=1, source_target_pairs={{0,8},{8,16},{16,24},{24,32},{32,40},{40,48},{48,56},{56,64},{64,7... | collective-permute-start | bytes 3932168 | tf_op jit(solution)/shard_map/ppermute | solution.py:337
  60.0 1.2 copy-start
  61.2 43.9 %all-to-all-start.1 = ((bf16[8,128,1280]{2,1,0:T(8,128)(2,1)}), bf16[8,128,1280]{2,1,0:T(8,128)(2,1)}, u32[]{:S(2)}, u32[]{:S(2)}) async-start(bf16[8,128,1280]{2,1,0:T(8,128)(2,1)} %bitcast.36), calls=%async_computation.1 | async-start | bytes 5242880 | tf_op jit(solution)/shard_map/all_to_all | solution.py:308
  65.6 1.8 copy-start.1
  65.8 9.2 %collective-permute-start.2 = (bf16[512,640]{1,0:T(8,128)(2,1)S(1)}, bf16[512,640]{1,0:T(8,128)(2,1)}, u32[]{:S(2)}, u32[]{:S(2)}) collective-permute-start(bf16[512,640]{1,0:T(8,128)(2,1)S(1)} %bitcast.50), channel_id=1, source_target_pairs={{120,248},{121,249},{122,250},{123,251},{124,252},{125,253},{126,2... | collective-permute-start | bytes 1966088 | tf_op jit(solution)/shard_map/ppermute | solution.py:341
  68.5 9.6 %collective-permute-start.6 = (bf16[512,768]{1,0:T(8,128)(2,1)S(1)}, bf16[512,768]{1,0:T(8,128)(2,1)}, u32[]{:S(2)}, u32[]{:S(2)}) collective-permute-start(bf16[512,768]{1,0:T(8,128)(2,1)S(1)} %bitcast.48), channel_id=1, source_target_pairs={{120,248},{121,249},{122,250},{123,251},{124,252},{125,253},{126,2... | collective-permute-start | bytes 2359304 | tf_op jit(solution)/shard_map/ppermute | solution.py:341
  70.0 21.6 %collective-permute-start.4 = (bf16[1024,768]{1,0:T(8,128)(2,1)S(1)}, bf16[1024,768]{1,0:T(8,128)(2,1)}, u32[]{:S(2)}, u32[]{:S(2)}) collective-permute-start(bf16[1024,768]{1,0:T(8,128)(2,1)S(1)} %bitcast.35), channel_id=1, source_target_pairs={{0,8},{8,16},{16,24},{24,32},{32,40},{40,48},{48,56},{56,64},{64,7... | collective-permute-start | bytes 4718600 | tf_op jit(solution)/shard_map/ppermute | solution.py:337
  74.3 2.3 collective-permute-start.1
  75.0 5.2 %collective-permute-start.3 = (bf16[512,640]{1,0:T(8,128)(2,1)}, bf16[512,640]{1,0:T(8,128)(2,1)}, u32[]{:S(2)}, u32[]{:S(2)}) collective-permute-start(bf16[512,640]{1,0:T(8,128)(2,1)} %collective-permute-done.2), channel_id=1, source_target_pairs={{248,128},{249,129},{250,130},{251,131},{252,132},{253,133},{254,1... | collective-permute-start | bytes 1966088 | tf_op jit(solution)/shard_map/ppermute | solution.py:342
  76.5 6.6 %collective-permute-start.5 = (bf16[512,768]{1,0:T(8,128)(2,1)}, bf16[512,768]{1,0:T(8,128)(2,1)}, u32[]{:S(2)}, u32[]{:S(2)}) collective-permute-start(bf16[512,768]{1,0:T(8,128)(2,1)} %bitcast.12), channel_id=1, source_target_pairs={{120,128},{121,129},{122,130},{123,131},{124,132},{125,133},{126,1... | collective-permute-start | bytes 2359304 | tf_op jit(solution)/shard_map/ppermute | solution.py:340
  78.1 5.0 %collective-permute-start.7 = (bf16[512,768]{1,0:T(8,128)(2,1)}, bf16[512,768]{1,0:T(8,128)(2,1)}, u32[]{:S(2)}, u32[]{:S(2)}) collective-permute-start(bf16[512,768]{1,0:T(8,128)(2,1)} %collective-permute-done.6), channel_id=1, source_target_pairs={{248,128},{249,129},{250,130},{251,131},{252,132},{253,133},{254,1... | collective-permute-start | bytes 2359304 | tf_op jit(solution)/shard_map/ppermute | solution.py:342
  95.1 72.2 %collective-permute-start.8 = (bf16[128,5120]{1,0:T(8,128)(2,1)}, bf16[128,5120]{1,0:T(8,128)(2,1)S(1)}, u32[]{:S(2)}, u32[]{:S(2)}) collective-permute-start(bf16[128,5120]{1,0:T(8,128)(2,1)} %after.3), channel_id=1, source_target_pairs={{0,8},{8,16},{16,24},{24,32},{32,40},{40,48},{48,56},{56,64},{64,7... | collective-permute-start | bytes 3932168 | tf_op jit(solution)/shard_map/ppermute | solution.py:360
  129.8 33.6 %all-to-all-start.3 = ((bf16[8,128,384]{2,1,0:T(8,128)(2,1)}), bf16[8,128,384]{2,1,0:T(8,128)(2,1)S(1)}, u32[]{:S(2)}, u32[]{:S(2)}) async-start(bf16[8,128,384]{2,1,0:T(8,128)(2,1)} %bitcast.47), calls=%async_computation.3 | async-start | bytes 1572864 | tf_op jit(solution)/shard_map/all_to_all | solution.py:308
  163.3 21.3 %copy-start.2 = (bf16[8,128,384]{2,1,0:T(8,128)(2,1)}, bf16[8,128,384]{2,1,0:T(8,128)(2,1)S(1)}, u32[]{:S(2)}) copy-start(bf16[8,128,384]{2,1,0:T(8,128)(2,1)S(1)} %all-to-all-done.3) | copy-start | bytes 2359300
  163.3 21.3 %all-to-all-start.4 = ((bf16[8,128,512]{2,1,0:T(8,128)(2,1)}), bf16[8,128,512]{2,1,0:T(8,128)(2,1)S(1)}, u32[]{:S(2)}, u32[]{:S(2)}) async-start(bf16[8,128,512]{2,1,0:T(8,128)(2,1)} %bitcast.46), calls=%async_computation.4 | async-start | bytes 2097152 | tf_op jit(solution)/shard_map/all_to_all | solution.py:308
  167.3 17.3 %copy-start.7 = (bf16[128,5120]{1,0:T(8,128)(2,1)}, bf16[128,5120]{1,0:T(8,128)(2,1)S(1)}, u32[]{:S(2)}) copy-start(bf16[128,5120]{1,0:T(8,128)(2,1)S(1)} %collective-permute-done.8.earlier) | copy-start | bytes 3932164
  184.6 1.0 copy-start.4
  197.5 16.7 %all-to-all-start.6 = ((bf16[8,320,128]{2,1,0:T(8,128)(2,1)}), bf16[8,320,128]{2,1,0:T(8,128)(2,1)S(1)}, u32[]{:S(2)}, u32[]{:S(2)}) async-start(bf16[8,320,128]{2,1,0:T(8,128)(2,1)} %bitcast.19), calls=%async_computation.6 | async-start | bytes 1310720 | tf_op jit(solution)/shard_map/all_to_all | solution.py:308
  243.1 18.4 %copy-start.5 = (bf16[8,128,512]{2,1,0:T(8,128)(2,1)S(1)}, bf16[8,128,512]{2,1,0:T(8,128)(2,1)}, u32[]{:S(2)}) copy-start(bf16[8,128,512]{2,1,0:T(8,128)(2,1)} %copy-done.4) | copy-start | bytes 3145732
  243.1 2.9 %collective-permute-start.9 = (bf16[80,128]{1,0:T(8,128)(2,1)S(1)}, bf16[80,128]{1,0:T(8,128)(2,1)S(1)}, u32[]{:S(2)}, u32[]{:S(2)}) collective-permute-start(bf16[80,128]{1,0:T(8,128)(2,1)S(1)} %reduce_sum.38), channel_id=1, source_target_pairs={{0,128},{8,136},{16,144},{24,152},{32,160},{40,168},{48,176},{56,1... | collective-permute-start | bytes 61448 | tf_op jit(solution)/shard_map/ppermute | solution.py:379
  257.0 4.5 %copy-start.3 = (bf16[8,128,384]{2,1,0:T(8,128)(2,1)S(1)}, bf16[8,128,384]{2,1,0:T(8,128)(2,1)}, u32[]{:S(2)}) copy-start(bf16[8,128,384]{2,1,0:T(8,128)(2,1)} %copy-done.2) | copy-start | bytes 2359300
  257.9 13.3 %all-to-all-start.9 = ((bf16[8,320,128]{2,1,0:T(8,128)(2,1)}), bf16[8,320,128]{2,1,0:T(8,128)(2,1)S(1)}, u32[]{:S(2)}, u32[]{:S(2)}) async-start(bf16[8,320,128]{2,1,0:T(8,128)(2,1)} %broadcast_in_dim.10), calls=%async_computation.9 | async-start | bytes 1310720 | tf_op jit(solution)/shard_map/all_to_all | solution.py:308

commit v4 on v3

--- a/solution.py
+++ b/solution.py
@@ -31,27 +31,10 @@
     return lax.dot_general(left, right, (((0,), (0,)), ((), ())), preferred_element_type=F32)
 
 
-def spread_kernel(array, out):
-    out[...] = array[...]
-
-
-def spread(array, parts):
-    rows, columns = array.shape
-    width = columns // parts
-    return pl.pallas_call(
-        spread_kernel,
-        grid=(parts,),
-        in_specs=[pl.BlockSpec((rows, width), lambda j: (0, j))],
-        out_specs=pl.BlockSpec((rows, width), lambda j: (j, 0)),
-        out_shape=jax.ShapeDtypeStruct((parts * rows, width), BF16),
-        compiler_params=pltpu.CompilerParams(vmem_limit_bytes=60 << 20),
-        name="spread",
-    )(array)
-
-
 def pack_kernel(
-    tokens, query_base, value_base, out_grad, down_q, down_v, up_q, up_v, vl, qg, copy, low
+    tokens, query_base, value_base, out_grad, down_q, down_v, up_q, up_v, vl, *rest
 ):
+    qgs, copy, low = rest[:-2], rest[-2], rest[-1]
     rank = down_q.shape[0]
     width = value_base.shape[1]
 
@@ -63,8 +46,13 @@
 
     vl[:, :width] = (value_base[...].astype(F32) + dot(low[:, rank:], up_v[...])).astype(BF16)
     vl[:, width:] = low[...]
-    qg[:, :width] = (query_base[...].astype(F32) + dot(low[:, :rank], up_q[...])).astype(BF16)
-    qg[:, width:] = out_grad[...]
+    query = (query_base[...].astype(F32) + dot(low[:, :rank], up_q[...])).astype(BF16)
+    first = 0
+    for qg, heads in zip(qgs, CALLS):
+        part = heads * HEAD
+        qg[:, :part] = query[:, first : first + part]
+        qg[:, part:] = out_grad[:, first : first + part]
+        first += part
 
 
 def pack(tokens, query_base, value_base, out_grad, down_q, up_q, down_v, up_v, parts):
@@ -74,7 +62,7 @@
     whole = lambda j: (0, 0)
     part = lambda j: (0, j)
     once = pl.Buffered(1)
-    sizes = (width + 2 * rank, 2 * width)
+    sizes = [width + 2 * rank] + [2 * heads * HEAD for heads in CALLS]
     return pl.pallas_call(
         pack_kernel,
         grid=(parts,),
@@ -188,7 +176,7 @@
     total = k.shape[1] // HEAD
     rank = up_q.shape[0]
     begins = lows is None
-    column = lambda offset: pl.BlockSpec((rows, HEAD), lambda h, place: (0, first + h + offset))
+    column = pl.BlockSpec((rows, HEAD), lambda h, place: (0, first + h))
     fixed = pl.BlockSpec((rows, HEAD), lambda h, place: (0, total))
     up = pl.BlockSpec((rank, HEAD), lambda h, place: (0, place[0] * total + first + h))
     shapes = ((rows, rank), (rank, rows), (rank, rows))
@@ -212,12 +200,12 @@
             num_scalar_prefetch=1,
             grid=(heads,),
             in_specs=[
-                column(0),
-                column(total),
-                column(0),
-                column(0),
-                column(0),
-                column(0),
+                pl.BlockSpec((rows, HEAD), lambda h, place: (0, h)),
+                pl.BlockSpec((rows, HEAD), lambda h, place: (0, heads + h)),
+                column,
+                column,
+                column,
+                column,
                 fixed,
                 fixed,
                 up,
@@ -331,40 +319,28 @@
     )(array, *others)
 
 
-def shifted(array, blocks):
-    wrap = blocks // 2 - 1
-    half = array.shape[0] // 2
-    direct = lax.ppermute(
-        array, "blk", [(i, i + 1) for i in range(blocks - 1) if i != wrap]
-    )
-    upper = lax.ppermute(array[:half], "blk", [(wrap, wrap + 1)])
-    lower = lax.ppermute(array[half:], "blk", [(wrap, blocks - 1)])
-    lower = lax.ppermute(lower, "blk", [(blocks - 1, wrap + 1)])
-    return direct + jnp.concatenate([upper, lower], 0)
-
-
 def per_device(tokens, query_base, key_base, value_base, out_grad, down_q, up_q, down_v, up_v):
     blocks = lax.axis_size("blk")
     parts = lax.axis_size("uly")
     rows, columns = tokens.shape
     rank = down_q.shape[1]
     width = columns // parts
-    vl, qg, copy = pack(
+    vl, qg_a, qg_b, copy = pack(
         tokens, query_base, value_base, out_grad, down_q.T, up_q, down_v.T, up_v, parts
     )
-    k = exchange(spread(key_base, parts), "uly")
-    k_prior = shifted(k, blocks)
-    vl = exchange(vl, "uly")
-    vl_prior = shifted(vl, blocks)
-    qg = exchange(after(qg, vl), "uly")
-    earlier = lax.ppermute(
-        after(copy, vl_prior), "blk", [(i, i + 1) for i in range(blocks - 1)]
-    )
+    forward = [(i, i + 1) for i in range(blocks - 1)]
+    k = lax.all_to_all(key_base, "uly", split_axis=1, concat_axis=0, tiled=True)
+    k_prior = lax.ppermute(k, "blk", forward)
+    vl = exchange(after(vl, k), "uly")
+    vl_prior = lax.ppermute(vl, "blk", forward)
+    qg_a = exchange(after(qg_a, vl, k_prior), "uly")
+    qg_b = exchange(after(qg_b, qg_a, vl_prior), "uly")
+    earlier = lax.ppermute(after(copy, qg_a), "blk", forward)
     place = jnp.stack([lax.axis_index("uly"), lax.axis_index("blk")]).astype(jnp.int32)
-    ready = (place, qg, k, k_prior, vl, vl_prior, up_q, up_v)
-    out, ups_a, *lows = attention(*ready, None, 0, CALLS[0], False)
+    ready = (k, k_prior, vl, vl_prior, up_q, up_v)
+    out, ups_a, *lows = attention(place, qg_a, *ready, None, 0, CALLS[0], False)
     piece = exchange(out, "uly")
-    out, ups_b = attention(*ready, lows, CALLS[0], CALLS[1], True)
+    out, ups_b = attention(place, qg_b, *ready, lows, CALLS[0], CALLS[1], True)
     back = exchange(out, "uly")
     pieces = (piece, back)
     both = outer(back, tokens, earlier, (ups_a, ups_b), rank, piece)

time: 286 us -> 292 us (1.021)
  waiting for transfers between devices: 89.8 us -> 109 us
  blocking collectives: 57.1 us -> 39 us
  starting transfers between devices: 57.8 us -> 72 us
  other arithmetic: 8.06 us -> 1.69 us
  Pallas kernels: 64.8 us -> 59.4 us
    all_to_all x7, starting transfers between devices: 34.6 us -> 56.3 us  [exchange(): lax.all_to_all(array, axis, split_axis=0, concat_axis=0, tiled=True, axis...]
    all_to_all x4, blocking collectives: 57.1 us -> 39 us  [exchange(): lax.all_to_all(array, axis, split_axis=0, concat_axis=0, tiled=True, axis...]
    all_to_all x7, waiting for transfers between devices: 80.2 us -> 96.5 us  [exchange(): lax.all_to_all(array, axis, split_axis=0, concat_axis=0, tiled=True, axis...]
    ppermute x9 -> x3, starting transfers between devices: 21.5 us -> 8.09 us  [the longest x1 4.28 us: per_device(): k_prior = lax.ppermute(k, 'blk', forward)]
    all_to_all x0 -> x1, waiting for transfers between devices: none -> 10.1 us  [per_device(): k = lax.all_to_all(key_base, 'uly', split_axis=1, concat_axis=0, tiled=True)]
    ppermute x9 -> x3, waiting for transfers between devices: 8.49 us -> 0.01 us  [the longest x1 0.01 us: per_device(): k_prior = lax.ppermute(k, 'blk', forward)]
    all_to_all x0 -> x1, starting transfers between devices: none -> 7.48 us  [per_device(): k = lax.all_to_all(key_base, 'uly', split_axis=1, concat_axis=0, tiled=True)]
    add x2 -> x0, other arithmetic: 6.38 us -> none  [shifted(): return direct + jnp.concatenate([upper, lower], 0)]
  transfers between devices with their start and end apart: 17 -> 12, of which waited for: 9 -> 7; matrix products, arithmetic and copies ran while one was open for 3% -> 1% of each run, Pallas kernels for 19% -> 18%
where the time goes in v4:
time: 292 us; the launch traced here: 291 us
  waiting for transfers between devices  109 us (37%)
  starting transfers between devices  72 us (25%)
  Pallas kernels  59.4 us (20%)
  blocking collectives  39 us (13%)
  local copies, waits for them, and re-layouts  9.01 us (3%)
    all_to_all x7, waiting for transfers between devices, exchange(): lax.all_to_all(array, axis, split_axis=0, concat_axis=0, tiled=True, axis...  96.5 us
    all_to_all x7, starting transfers between devices, exchange(): lax.all_to_all(array, axis, split_axis=0, concat_axis=0, tiled=True, axis...  56.3 us
    pallas_call x2, Pallas kernels, attention(): pl.pallas_call(functools.partial(attention_kernel, begins, ends), grid_sp...  42.8 us
    all_to_all x4, blocking collectives, exchange(): lax.all_to_all(array, axis, split_axis=0, concat_axis=0, tiled=True, axis...  39 us
    all_to_all x1, waiting for transfers between devices, per_device(): k = lax.all_to_all(key_base, 'uly', split_axis=1, concat_axis=0, tiled=True)  10.1 us
    pallas_call x1, Pallas kernels, pack(): pl.pallas_call(pack_kernel, grid=(parts,), in_specs=[pl.BlockSpec((rows,...  10 us
    all_to_all x1, starting transfers between devices, per_device(): k = lax.all_to_all(key_base, 'uly', split_axis=1, concat_axis=0, tiled=True)  7.48 us
  transfers between devices with their start and end apart: 12, of which 7 were waited for; matrix products, arithmetic and copies ran while one was open for 1% of the time, Pallas kernels for 18%

profile of v4, /device:TPU:1, one launch (start us, length us, event | category | flops | bytes accessed | tf_op | source)
XLA Modules:
  0.0 291.2 jit_solution(6223525371132490695)
XLA Ops:
  0.6 2.5 copy.25
  3.2 7.5 %all-to-all-start = ((bf16[128,8,640]{2,0,1:T(8,128)(2,1)}), bf16[128,8,640]{2,0,1:T(8,128)(2,1)S(1)}, u32[]{:S(2)}, u32[]{:S(2)}) async-start(bf16[128,8,640]{2,0,1:T(8,128)(2,1)} %bitcast.32), calls=%async_computation | async-start | bytes 2621440 | tf_op jit(solution)/shard_map/all_to_all | solution.py:332
  10.6 10.0 %pack.1 = (bf16[1024,768]{1,0:T(8,128)(2,1)}, bf16[1024,768]{1,0:T(8,128)(2,1)}, bf16[1024,512]{1,0:T(8,128)(2,1)}, bf16[128,5120]{1,0:T(8,128)(2,1)}) custom-call(bf16[128,5120]{1,0:T(8,128)(2,1)} %tokens.3, bf16[128,5120]{1,0:T(8,128)(2,1)} %query_base.1, bf16[128,5120]{1,0:T(8,128)(2,1)} %value_base.1, bf16[128,5120]{1,0:T(8,128)(2,1)} %out_grad.1, ...), custom_call_target="tpu_custom_call" | custom-call | flops 536870912 | bytes 14680064 | tf_op jit(solution)/shard_map/pack/pallas_call | solution.py:66
  20.7 10.1 %all-to-all-done = bf16[128,8,640]{2,0,1:T(8,128)(2,1)S(1)} async-done(((bf16[128,8,640]{2,0,1:T(8,128)(2,1)}), bf16[128,8,640]{2,0,1:T(8,128)(2,1)S(1)}, u32[]{:S(2)}, u32[]{:S(2)}) %all-to-all-start) | async-done | bytes 1310752 | tf_op jit(solution)/shard_map/all_to_all | solution.py:332
  30.8 0.0 copy-start.6
  30.8 1.1 copy-done.6
  31.9 0.0 copy-start.7
  31.9 3.7 %all-to-all-start.1 = ((bf16[8,128,768]{2,1,0:T(8,128)(2,1)}), bf16[8,128,768]{2,1,0:T(8,128)(2,1)S(1)}, u32[]{:S(2)}, u32[]{:S(2)}) async-start(bf16[8,128,768]{2,1,0:T(8,128)(2,1)} %bitcast.39), calls=%async_computation.1 | async-start | bytes 3145728 | tf_op jit(solution)/shard_map/all_to_all | solution.py:296
  35.6 0.0 copy-done.7
  35.6 4.3 %collective-permute-start = (bf16[1024,640]{1,0:T(8,128)(2,1)S(1)}, bf16[1024,640]{1,0:T(8,128)(2,1)}, u32[]{:S(2)}, u32[]{:S(2)}) collective-permute-start(bf16[1024,640]{1,0:T(8,128)(2,1)S(1)} %bitcast.50), channel_id=1, source_target_pairs={{0,8},{8,16},{16,24},{24,32},{32,40},{40,48},{48,56},{56,64},{64,7... | collective-permute-start | bytes 3932168 | tf_op jit(solution)/shard_map/ppermute | solution.py:333
  39.9 24.1 %all-to-all-done.1 = bf16[8,128,768]{2,1,0:T(8,128)(2,1)S(1)} async-done(((bf16[8,128,768]{2,1,0:T(8,128)(2,1)}), bf16[8,128,768]{2,1,0:T(8,128)(2,1)S(1)}, u32[]{:S(2)}, u32[]{:S(2)}) %all-to-all-start.1) | async-done | bytes 1572896 | tf_op jit(solution)/shard_map/all_to_all | solution.py:296
  63.9 0.0 copy-start.5
  63.9 1.9 collective-permute-start.1
  65.8 0.0 collective-permute-done.refs_2_.k_prior
  65.9 0.0 copy-done.5
  65.9 27.6 %all-to-all-start.2 = ((bf16[8,128,768]{2,1,0:T(8,128)(2,1)}), bf16[8,128,768]{2,1,0:T(8,128)(2,1)S(1)}, u32[]{:S(2)}, u32[]{:S(2)}) async-start(bf16[8,128,768]{2,1,0:T(8,128)(2,1)} %bitcast.46), calls=%async_computation.2 | async-start | bytes 3145728 | tf_op jit(solution)/shard_map/all_to_all | solution.py:296
  93.5 0.6 pad_add_fusion.place
  94.1 33.7 %all-to-all-done.2 = bf16[8,128,768]{2,1,0:T(8,128)(2,1)S(1)} async-done(((bf16[8,128,768]{2,1,0:T(8,128)(2,1)}), bf16[8,128,768]{2,1,0:T(8,128)(2,1)S(1)}, u32[]{:S(2)}, u32[]{:S(2)}) %all-to-all-start.2) | async-done | bytes 1572896 | tf_op jit(solution)/shard_map/all_to_all | solution.py:296
  127.8 0.0 copy-start
  127.8 1.2 copy-done
  129.0 1.9 collective-permute-start.2
  130.9 0.0 collective-permute-done.1.v_prior.low_prior.refs_2_
  130.9 4.6 %all-to-all-start.4 = ((bf16[8,128,512]{2,1,0:T(8,128)(2,1)}), bf16[8,128,512]{2,1,0:T(8,128)(2,1)S(1)}, u32[]{:S(2)}, u32[]{:S(2)}) async-start(bf16[8,128,512]{2,1,0:T(8,128)(2,1)} %bitcast.51), calls=%async_computation.4 | async-start | bytes 2097152 | tf_op jit(solution)/shard_map/all_to_all | solution.py:296
  135.5 24.7 %attention.2 = (bf16[1024,384]{1,0:T(8,128)(2,1)}, bf16[2,192,128]{2,1,0:T(8,128)(2,1)}, f32[1024,64]{1,0:T(8,128)}, f32[64,1024]{1,0:T(8,128)}, f32[64,1024]{1,0:T(8,128)}) custom-call(s32[2]{0:T(128)} %pad_add_fusion.place, bf16[1024,768]{1,0:T(8,128)(2,1)} %bitcast.35, bf16[1024,768]{1,0:T(8,128)(2,1)} %bitcast.36, bf16[1024,640]{1,0:T(8,128)(2,1)} %bitcast.48, ...), custom_call_target="tpu_custom_call" | custom-call | flops 32212254720 | bytes 6291456 | tf_op jit(solution)/shard_map/attention/pallas_call | solution.py:197
  160.2 0.0 all-to-all-done.4
  160.2 0.0 copy-start.9
  160.2 6.6 %all-to-all-start.3 = ((bf16[8,128,384]{2,1,0:T(8,128)(2,1)}), bf16[8,128,384]{2,1,0:T(8,128)(2,1)S(1)}, u32[]{:S(2)}, u32[]{:S(2)}) async-start(bf16[8,128,384]{2,1,0:T(8,128)(2,1)} %bitcast.58), calls=%async_computation.3 | async-start | bytes 1572864 | tf_op jit(solution)/shard_map/all_to_all | solution.py:296
  166.9 0.0 copy-done.9
  166.9 18.2 %attention.3 = (bf16[1024,512]{1,0:T(8,128)(2,1)}, bf16[2,128,128]{2,1,0:T(8,128)(2,1)}) custom-call(s32[2]{0:T(128)} %pad_add_fusion.place, bf16[1024,512]{1,0:T(8,128)(2,1)} %bitcast.55, bf16[1024,512]{1,0:T(8,128)(2,1)} %bitcast.56, bf16[1024,640]{1,0:T(8,128)(2,1)} %bitcast.49, bf16[1024,768]{1,0:T(8,128)(2,1)} %bitcast.44, ...), custom_call_target="tpu_custom_call" | custom-call | flops 21474836480 | bytes 4194304 | tf_op jit(solution)/shard_map/attention/pallas_call | solution.py:197
  185.0 0.0 all-to-all-done.3
  185.1 0.0 copy-start.1
  185.1 6.6 %all-to-all-start.5 = ((bf16[8,128,512]{2,1,0:T(8,128)(2,1)}), bf16[8,128,512]{2,1,0:T(8,128)(2,1)S(1)}, u32[]{:S(2)}, u32[]{:S(2)}) async-start(bf16[8,128,512]{2,1,0:T(8,128)(2,1)} %bitcast.57), calls=%async_computation.5 | async-start | bytes 2097152 | tf_op jit(solution)/shard_map/all_to_all | solution.py:296
  191.7 0.0 collective-permute-done.2.earlier
  191.7 0.0 copy-start.8
  191.7 17.3 %all-to-all-done.5 = bf16[8,128,512]{2,1,0:T(8,128)(2,1)S(1)} async-done(((bf16[8,128,512]{2,1,0:T(8,128)(2,1)}), bf16[8,128,512]{2,1,0:T(8,128)(2,1)S(1)}, u32[]{:S(2)}, u32[]{:S(2)}) %all-to-all-start.5) | async-done | bytes 1048608 | tf_op jit(solution)/shard_map/all_to_all | solution.py:296
  209.0 0.0 copy-start.3
  209.0 0.0 copy-done.1
  209.0 0.0 copy-done.8
  209.0 1.0 copy-done.3
  210.0 3.8 %outer.1 = bf16[2,2880,128]{2,1,0:T(8,128)(2,1)} custom-call(bf16[1024,512]{1,0:T(8,128)(2,1)} %bitcast.38, bf16[128,5120]{1,0:T(8,128)(2,1)} %tokens.3, bf16[128,5120]{1,0:T(8,128)(2,1)} %copy-done.8, bf16[2,192,128]{2,1,0:T(8,128)(2,1)} %get-tuple-element.29.rest_0_, bf16[2,128,128]{2,1,0:T(8,128)(2,1)} %get-tuple-element.30.rest_1_, ...), custom_call_target="tpu_custom_call" | custom-call | flops 536870912 | bytes 8388608 | tf_op jit(solution)/shard_map/outer/pallas_call | solution.py:257
  213.8 6.5 %all_to_all.116 = bf16[2,2880,128]{2,1,0:T(8,128)(2,1)S(1)} all-to-all(bf16[2,2880,128]{2,1,0:T(8,128)(2,1)} %outer.1), channel_id=1, replica_groups={{0,8},{16,24},{32,40},{48,56},{64,72},{80,88},{96,104},{112,120},{128,1..., dimensions={0} | all-to-all | bytes 2949120 | tf_op jit(solution)/shard_map/all_to_all | solution.py:296
  220.3 0.8 reduce_sum.36
  221.1 0.9 slice.21
  222.0 3.5 %all-to-all-start.7 = ((bf16[8,320,128]{2,1,0:T(8,128)(2,1)}), bf16[8,320,128]{2,1,0:T(8,128)(2,1)S(1)}, u32[]{:S(2)}, u32[]{:S(2)}) async-start(bf16[8,320,128]{2,1,0:T(8,128)(2,1)} %bitcast.18), calls=%async_computation.7 | async-start | bytes 1310720 | tf_op jit(solution)/shard_map/all_to_all | solution.py:296
  225.5 13.1 %all-to-all-done.7 = bf16[8,320,128]{2,1,0:T(8,128)(2,1)S(1)} async-done(((bf16[8,320,128]{2,1,0:T(8,128)(2,1)}), bf16[8,320,128]{2,1,0:T(8,128)(2,1)S(1)}, u32[]{:S(2)}, u32[]{:S(2)}) %all-to-all-start.7) | async-done | bytes 655392 | tf_op jit(solution)/shard_map/all_to_all | solution.py:296
  238.6 0.1 reduce_sum.37
  238.8 10.8 %all_to_all.117 = bf16[8,80,128]{2,1,0:T(8,128)(2,1)S(1)} all-to-all(bf16[8,80,128]{2,1,0:T(8,128)(2,1)S(1)} %pad_maximum_fusion.1), channel_id=1, replica_groups={{0,16,32,48,64,80,96,112},{8,24,40,56,72,88,104,120},{128,144,160,176,1..., dimensions={0} | all-to-all | bytes 327680 | tf_op jit(solution)/shard_map/all_to_all | solution.py:296
  249.6 0.0 copy-start.4
  249.6 0.1 collective-permute-start.3
  249.7 2.6 collective-permute-done.3
  252.3 11.0 %all_to_all.118 = bf16[8,80,128]{2,1,0:T(8,128)(2,1)S(1)} all-to-all(bf16[8,80,128]{2,1,0:T(8,128)(2,1)S(1)} %broadcast_in_dim.8), channel_id=1, replica_groups={{0,16,32,48,64,80,96,112},{8,24,40,56,72,88,104,120},{128,144,160,176,1..., dimensions={0} | all-to-all | bytes 327680 | tf_op jit(solution)/shard_map/all_to_all | solution.py:296
  263.4 0.0 copy-start.2
  263.4 0.9 broadcast_in_dim.10
  264.3 3.5 %all-to-all-start.10 = ((bf16[8,320,128]{2,1,0:T(8,128)(2,1)}), bf16[8,320,128]{2,1,0:T(8,128)(2,1)S(1)}, u32[]{:S(2)}, u32[]{:S(2)}) async-start(bf16[8,320,128]{2,1,0:T(8,128)(2,1)} %broadcast_in_dim.10), calls=%async_computation.10 | async-start | bytes 1310720 | tf_op jit(solution)/shard_map/all_to_all | solution.py:296
  267.9 0.0 copy-done.4
  267.9 0.0 copy-done.2
  267.9 0.2 maximum_bitcast_fusion
  268.1 1.2 copy.23
  269.3 8.3 %all-to-all-done.10 = bf16[8,320,128]{2,1,0:T(8,128)(2,1)S(1)} async-done(((bf16[8,320,128]{2,1,0:T(8,128)(2,1)}), bf16[8,320,128]{2,1,0:T(8,128)(2,1)S(1)}, u32[]{:S(2)}, u32[]{:S(2)}) %all-to-all-start.10) | async-done | bytes 655392 | tf_op jit(solution)/shard_map/all_to_all | solution.py:296
  277.7 0.1 broadcast_in_dim.22
  277.8 10.7 %all_to_all.119.both = bf16[2,2880,128]{2,1,0:T(8,128)(2,1)} all-to-all(bf16[2,2880,128]{2,1,0:T(8,128)(2,1)S(1)} %broadcast_in_dim.22), channel_id=1, replica_groups={{0,8},{16,24},{32,40},{48,56},{64,72},{80,88},{96,104},{112,120},{128,1..., dimensions={0} | all-to-all | bytes 2949120 | tf_op jit(solution)/shard_map/all_to_all | solution.py:296
  288.5 2.7 unpack.1
  (12 shorter events, 0.2 us)
Async XLA Ops:
  3.2 27.6 %all-to-all-start = ((bf16[128,8,640]{2,0,1:T(8,128)(2,1)}), bf16[128,8,640]{2,0,1:T(8,128)(2,1)S(1)}, u32[]{:S(2)}, u32[]{:S(2)}) async-start(bf16[128,8,640]{2,0,1:T(8,128)(2,1)} %bitcast.32), calls=%async_computation | async-start | bytes 2621440 | tf_op jit(solution)/shard_map/all_to_all | solution.py:332
  30.8 1.1 copy-start.6
  31.9 3.7 %copy-start.7 = (bf16[128,8,640]{2,0,1:T(8,128)(2,1)S(1)}, bf16[128,8,640]{2,0,1:T(8,128)(2,1)}, u32[]{:S(2)}) copy-start(bf16[128,8,640]{2,0,1:T(8,128)(2,1)} %copy-done.6) | copy-start | bytes 3932164
  31.9 32.1 %all-to-all-start.1 = ((bf16[8,128,768]{2,1,0:T(8,128)(2,1)}), bf16[8,128,768]{2,1,0:T(8,128)(2,1)S(1)}, u32[]{:S(2)}, u32[]{:S(2)}) async-start(bf16[8,128,768]{2,1,0:T(8,128)(2,1)} %bitcast.39), calls=%async_computation.1 | async-start | bytes 3145728 | tf_op jit(solution)/shard_map/all_to_all | solution.py:296
  35.6 30.3 %collective-permute-start = (bf16[1024,640]{1,0:T(8,128)(2,1)S(1)}, bf16[1024,640]{1,0:T(8,128)(2,1)}, u32[]{:S(2)}, u32[]{:S(2)}) collective-permute-start(bf16[1024,640]{1,0:T(8,128)(2,1)S(1)} %bitcast.50), channel_id=1, source_target_pairs={{0,8},{8,16},{16,24},{24,32},{32,40},{40,48},{48,56},{56,64},{64,7... | collective-permute-start | bytes 3932168 | tf_op jit(solution)/shard_map/ppermute | solution.py:333
  63.9 1.9 copy-start.5
  63.9 67.0 %collective-permute-start.1 = (bf16[1024,768]{1,0:T(8,128)(2,1)S(1)}, bf16[1024,768]{1,0:T(8,128)(2,1)}, u32[]{:S(2)}, u32[]{:S(2)}) collective-permute-start(bf16[1024,768]{1,0:T(8,128)(2,1)S(1)} %bitcast.40), channel_id=1, source_target_pairs={{0,8},{8,16},{16,24},{24,32},{32,40},{40,48},{48,56},{56,64},{64,7... | collective-permute-start | bytes 4718600 | tf_op jit(solution)/shard_map/ppermute | solution.py:335
  65.9 61.9 %all-to-all-start.2 = ((bf16[8,128,768]{2,1,0:T(8,128)(2,1)}), bf16[8,128,768]{2,1,0:T(8,128)(2,1)S(1)}, u32[]{:S(2)}, u32[]{:S(2)}) async-start(bf16[8,128,768]{2,1,0:T(8,128)(2,1)} %bitcast.46), calls=%async_computation.2 | async-start | bytes 3145728 | tf_op jit(solution)/shard_map/all_to_all | solution.py:296
  127.8 1.2 copy-start
  129.0 62.7 %collective-permute-start.2 = (bf16[128,5120]{1,0:T(8,128)(2,1)}, bf16[128,5120]{1,0:T(8,128)(2,1)S(1)}, u32[]{:S(2)}, u32[]{:S(2)}) collective-permute-start(bf16[128,5120]{1,0:T(8,128)(2,1)} %after.7), channel_id=1, source_target_pairs={{0,8},{8,16},{16,24},{24,32},{32,40},{40,48},{48,56},{56,64},{64,7... | collective-permute-start | bytes 3932168 | tf_op jit(solution)/shard_map/ppermute | solution.py:338
  130.9 29.3 %all-to-all-start.4 = ((bf16[8,128,512]{2,1,0:T(8,128)(2,1)}), bf16[8,128,512]{2,1,0:T(8,128)(2,1)S(1)}, u32[]{:S(2)}, u32[]{:S(2)}) async-start(bf16[8,128,512]{2,1,0:T(8,128)(2,1)} %bitcast.51), calls=%async_computation.4 | async-start | bytes 2097152 | tf_op jit(solution)/shard_map/all_to_all | solution.py:296
  160.2 6.7 %copy-start.9 = (bf16[8,128,512]{2,1,0:T(8,128)(2,1)}, bf16[8,128,512]{2,1,0:T(8,128)(2,1)S(1)}, u32[]{:S(2)}) copy-start(bf16[8,128,512]{2,1,0:T(8,128)(2,1)S(1)} %all-to-all-done.4) | copy-start | bytes 3145732
  160.2 24.8 %all-to-all-start.3 = ((bf16[8,128,384]{2,1,0:T(8,128)(2,1)}), bf16[8,128,384]{2,1,0:T(8,128)(2,1)S(1)}, u32[]{:S(2)}, u32[]{:S(2)}) async-start(bf16[8,128,384]{2,1,0:T(8,128)(2,1)} %bitcast.58), calls=%async_computation.3 | async-start | bytes 1572864 | tf_op jit(solution)/shard_map/all_to_all | solution.py:296
  185.1 24.0 %copy-start.1 = (bf16[8,128,384]{2,1,0:T(8,128)(2,1)}, bf16[8,128,384]{2,1,0:T(8,128)(2,1)S(1)}, u32[]{:S(2)}) copy-start(bf16[8,128,384]{2,1,0:T(8,128)(2,1)S(1)} %all-to-all-done.3) | copy-start | bytes 2359300
  185.1 23.9 %all-to-all-start.5 = ((bf16[8,128,512]{2,1,0:T(8,128)(2,1)}), bf16[8,128,512]{2,1,0:T(8,128)(2,1)S(1)}, u32[]{:S(2)}, u32[]{:S(2)}) async-start(bf16[8,128,512]{2,1,0:T(8,128)(2,1)} %bitcast.57), calls=%async_computation.5 | async-start | bytes 2097152 | tf_op jit(solution)/shard_map/all_to_all | solution.py:296
  191.7 17.3 %copy-start.8 = (bf16[128,5120]{1,0:T(8,128)(2,1)}, bf16[128,5120]{1,0:T(8,128)(2,1)S(1)}, u32[]{:S(2)}) copy-start(bf16[128,5120]{1,0:T(8,128)(2,1)S(1)} %collective-permute-done.2.earlier) | copy-start | bytes 3932164
  209.0 1.0 copy-start.3
  222.0 16.7 %all-to-all-start.7 = ((bf16[8,320,128]{2,1,0:T(8,128)(2,1)}), bf16[8,320,128]{2,1,0:T(8,128)(2,1)S(1)}, u32[]{:S(2)}, u32[]{:S(2)}) async-start(bf16[8,320,128]{2,1,0:T(8,128)(2,1)} %bitcast.18), calls=%async_computation.7 | async-start | bytes 1310720 | tf_op jit(solution)/shard_map/all_to_all | solution.py:296
  249.6 18.3 %copy-start.4 = (bf16[8,128,512]{2,1,0:T(8,128)(2,1)S(1)}, bf16[8,128,512]{2,1,0:T(8,128)(2,1)}, u32[]{:S(2)}) copy-start(bf16[8,128,512]{2,1,0:T(8,128)(2,1)} %copy-done.3) | copy-start | bytes 3145732
  249.6 2.7 collective-permute-start.3
  263.4 4.5 %copy-start.2 = (bf16[8,128,384]{2,1,0:T(8,128)(2,1)S(1)}, bf16[8,128,384]{2,1,0:T(8,128)(2,1)}, u32[]{:S(2)}) copy-start(bf16[8,128,384]{2,1,0:T(8,128)(2,1)} %copy-done.1) | copy-start | bytes 2359300
  264.3 13.3 %all-to-all-start.10 = ((bf16[8,320,128]{2,1,0:T(8,128)(2,1)}), bf16[8,320,128]{2,1,0:T(8,128)(2,1)S(1)}, u32[]{:S(2)}, u32[]{:S(2)}) async-start(bf16[8,320,128]{2,1,0:T(8,128)(2,1)} %broadcast_in_dim.10), calls=%async_computation.10 | async-start | bytes 1310720 | tf_op jit(solution)/shard_map/all_to_all | solution.py:296

commit v5 on v4

--- a/solution.py
+++ b/solution.py
@@ -34,7 +34,7 @@
 def pack_kernel(
     tokens, query_base, value_base, out_grad, down_q, down_v, up_q, up_v, vl, *rest
 ):
-    qgs, copy, low = rest[:-2], rest[-2], rest[-1]
+    qgs, low = rest[:-1], rest[-1]
     rank = down_q.shape[0]
     width = value_base.shape[1]
 
@@ -42,10 +42,11 @@
     def _():
         low[:, :rank] = dot_t(tokens[...], down_q[...]).astype(BF16)
         low[:, rank:] = dot_t(tokens[...], down_v[...]).astype(BF16)
-        copy[...] = tokens[...]
-
-    vl[:, :width] = (value_base[...].astype(F32) + dot(low[:, rank:], up_v[...])).astype(BF16)
-    vl[:, width:] = low[...]
+
+    vl[:, : 2 * rank] = low[...]
+    vl[:, 2 * rank :] = (value_base[...].astype(F32) + dot(low[:, rank:], up_v[...])).astype(
+        BF16
+    )
     query = (query_base[...].astype(F32) + dot(low[:, :rank], up_q[...])).astype(BF16)
     first = 0
     for qg, heads in zip(qgs, CALLS):
@@ -70,10 +71,8 @@
         + [pl.BlockSpec((rows, width), part)] * 3
         + [pl.BlockSpec((rank, columns), whole, pipeline_mode=once)] * 2
         + [pl.BlockSpec((rank, width), part)] * 2,
-        out_specs=[pl.BlockSpec((rows, size), lambda j: (j, 0)) for size in sizes]
-        + [pl.BlockSpec((rows, columns), whole)],
-        out_shape=[jax.ShapeDtypeStruct((parts * rows, size), BF16) for size in sizes]
-        + [jax.ShapeDtypeStruct((rows, columns), BF16)],
+        out_specs=[pl.BlockSpec((rows, size), lambda j: (j, 0)) for size in sizes],
+        out_shape=[jax.ShapeDtypeStruct((parts * rows, size), BF16) for size in sizes],
         scratch_shapes=[pltpu.VMEM((rows, 2 * rank), BF16)],
         compiler_params=pltpu.CompilerParams(vmem_limit_bytes=60 << 20),
         cost_estimate=pl.CostEstimate(flops=1 << 29, bytes_accessed=14 << 20, transcendentals=0),
@@ -82,9 +81,13 @@
 
 
 def attention_kernel(
-    begins, ends, place, q, g, k_own, v_own, k_prior, v_prior, low_own, low_prior, up_q, up_v, *rest
+    begins, ends, place, q, g, k_own, v_own, k_straight, v_straight, k_wrapped, v_wrapped,
+    low_own, low_straight, low_wrapped, up_q, up_v, *rest,
 ):
     rest = list(rest)
+    k_prior, v_prior = rest.pop(), rest.pop()
+    k_prior[...] = k_straight[...] + k_wrapped[...]
+    v_prior[...] = v_straight[...] + v_wrapped[...]
     low_in = None if begins else [rest.pop(0) for _ in range(3)]
     out, ups = rest.pop(0), rest.pop(0)
     low_out = None if ends else [rest.pop(0) for _ in range(3)]
@@ -155,7 +158,7 @@
     lo[...] += dot(up_v[...], own)
     lp[...] += dot(up_v[...], prior)
     ups[0] = up_q_grad.astype(BF16)
-    ups[1] = (dot(own, low_own[:, rank:]) + dot(prior, low_prior[:, rank:])).T.astype(BF16)
+    ups[1] = (dot(own, low_own[:, rank:]) + dot(prior, low_straight[:, rank:] + low_wrapped[:, rank:])).T.astype(BF16)
 
     @pl.when(head == heads - 1)
     def _():
@@ -171,13 +174,15 @@
             low_out[2][...] = lp[...]
 
 
-def attention(place, qg, k, k_prior, vl, vl_prior, up_q, up_v, lows, first, heads, ends):
+def attention(
+    place, qg, k, k_prior, vl, vl_prior, low_wrap, up_q, up_v, wrap, lows, first, heads, ends
+):
     rows = qg.shape[0]
     total = k.shape[1] // HEAD
     rank = up_q.shape[0]
     begins = lows is None
-    column = pl.BlockSpec((rows, HEAD), lambda h, place: (0, first + h))
-    fixed = pl.BlockSpec((rows, HEAD), lambda h, place: (0, total))
+    column = lambda at: pl.BlockSpec((rows, HEAD), lambda h, place: (0, at + h))
+    fixed = lambda at: pl.BlockSpec((rows, HEAD), lambda h, place: (0, at))
     up = pl.BlockSpec((rank, HEAD), lambda h, place: (0, place[0] * total + first + h))
     shapes = ((rows, rank), (rank, rows), (rank, rows))
     whole = lambda shape: pl.BlockSpec(shape, lambda h, place: (0, 0))
@@ -200,21 +205,25 @@
             num_scalar_prefetch=1,
             grid=(heads,),
             in_specs=[
-                pl.BlockSpec((rows, HEAD), lambda h, place: (0, h)),
-                pl.BlockSpec((rows, HEAD), lambda h, place: (0, heads + h)),
-                column,
-                column,
-                column,
-                column,
-                fixed,
-                fixed,
+                column(0),
+                column(heads),
+                column(first),
+                column(first + 1),
+                column(first),
+                column(first + 1),
+                column(0),
+                column(wrap.shape[1] // HEAD - heads),
+                fixed(0),
+                fixed(0),
+                fixed(CALLS[0]),
                 up,
                 up,
             ]
             + ([] if begins else [whole(shape) for shape in shapes]),
             out_specs=out_specs,
             scratch_shapes=[pltpu.VMEM(shape, F32) for shape in shapes]
-            + [pltpu.VMEM((HEAD, rows), F32)] * 2,
+            + [pltpu.VMEM((HEAD, rows), F32)] * 2
+            + [pltpu.VMEM((rows, HEAD), BF16)] * 2,
         ),
         out_shape=out_shape,
         compiler_params=pltpu.CompilerParams(vmem_limit_bytes=60 << 20),
@@ -225,20 +234,17 @@
         ),
         name="attention",
     )(
-        place, qg, qg, k, vl, k_prior, vl_prior, vl, vl_prior, up_q, up_v,
+        place, qg, qg, k, vl, k_prior, vl_prior, wrap, wrap, vl, vl_prior, low_wrap, up_q, up_v,
         *(() if begins else lows),
     )
 
 
-def outer_kernel(lows, tokens, earlier, *rest):
+def outer_kernel(low, tokens, *rest):
     ups, out = rest[:-2], rest[-1]
-    rows, columns = tokens.shape
-    rank = lows.shape[1] // 4
-    low = jnp.sum(lows[...].reshape(-1, rows, 4 * rank).astype(F32), axis=0).astype(BF16)
+    rank = low.shape[1] // 2
+    columns = tokens.shape[1]
     grad_q = t_dot(low[:, :rank], tokens[...])
-    grad_v = t_dot(low[:, rank : 2 * rank], tokens[...]) + t_dot(
-        low[:, 2 * rank : 3 * rank], earlier[...]
-    )
+    grad_v = t_dot(low[:, rank:], tokens[...])
     for block in range(columns // HEAD):
         to = slice(block * rank, (block + 1) * rank)
         out[0, to, :] = grad_q[:, block * HEAD : (block + 1) * HEAD].astype(BF16)
@@ -250,22 +256,21 @@
         first += size
 
 
-def outer(lows, tokens, earlier, ups, rank, settled):
+def outer(low, tokens, ups, settled):
+    rank = low.shape[1] // 2
     length = tokens.shape[1] // HEAD * rank + sum(up.shape[1] for up in ups)
     whole = lambda array: pl.BlockSpec(array.shape, lambda i: (0,) * array.ndim)
-    at = lows.shape[1] // (4 * rank) - 1
     return pl.pallas_call(
         outer_kernel,
         grid=(1,),
-        in_specs=[pl.BlockSpec((lows.shape[0], 4 * rank), lambda i: (0, at))]
-        + [whole(array) for array in (tokens, earlier, *ups)]
+        in_specs=[whole(array) for array in (low, tokens, *ups)]
         + [pl.BlockSpec(memory_space=pl.ANY)],
         out_specs=pl.BlockSpec((2, length, HEAD), lambda i: (0, 0, 0)),
         out_shape=jax.ShapeDtypeStruct((2, length, HEAD), BF16),
         compiler_params=pltpu.CompilerParams(vmem_limit_bytes=60 << 20),
         cost_estimate=pl.CostEstimate(flops=1 << 29, bytes_accessed=8 << 20, transcendentals=0),
         name="outer",
-    )(lows, tokens, earlier, *ups, settled)
+    )(low, tokens, *ups, settled)
 
 
 def unpack_kernel(both, down_q, down_v, up_q, up_v):
@@ -325,25 +330,37 @@
     rows, columns = tokens.shape
     rank = down_q.shape[1]
     width = columns // parts
-    vl, qg_a, qg_b, copy = pack(
+    vl, qg_a, qg_b = pack(
         tokens, query_base, value_base, out_grad, down_q.T, up_q, down_v.T, up_v, parts
     )
-    forward = [(i, i + 1) for i in range(blocks - 1)]
+    crossing = blocks // 2 - 1
+    forward = [(i, i + 1) for i in range(blocks - 1) if i != crossing]
+    wrapped = [(crossing, crossing + 1)]
     k = lax.all_to_all(key_base, "uly", split_axis=1, concat_axis=0, tiled=True)
     k_prior = lax.ppermute(k, "blk", forward)
     vl = exchange(after(vl, k), "uly")
     vl_prior = lax.ppermute(vl, "blk", forward)
     qg_a = exchange(after(qg_a, vl, k_prior), "uly")
+    split = CALLS[0] * HEAD
+    wrap_a = jnp.concatenate([k[:, :split], vl[:, : split + 2 * rank]], 1)
+    wrap_a = lax.ppermute(after(wrap_a, qg_a, vl_prior), "blk", wrapped)
+    wrap_b = jnp.concatenate([k[:, split:], vl[:, split + 2 * rank :]], 1)
+    wrap_b = lax.ppermute(after(wrap_b, wrap_a), "blk", wrapped)
     qg_b = exchange(after(qg_b, qg_a, vl_prior), "uly")
-    earlier = lax.ppermute(after(copy, qg_a), "blk", forward)
     place = jnp.stack([lax.axis_index("uly"), lax.axis_index("blk")]).astype(jnp.int32)
-    ready = (k, k_prior, vl, vl_prior, up_q, up_v)
-    out, ups_a, *lows = attention(place, qg_a, *ready, None, 0, CALLS[0], False)
+    ready = (k, k_prior, vl, vl_prior, wrap_a, up_q, up_v)
+    out, ups_a, *lows = attention(place, qg_a, *ready, wrap_a, None, 0, CALLS[0], False)
     piece = exchange(out, "uly")
-    out, ups_b = attention(place, qg_b, *ready, lows, CALLS[0], CALLS[1], True)
-    back = exchange(out, "uly")
+    out, ups_b = attention(place, qg_b, *ready, wrap_b, lows, CALLS[0], CALLS[1], True)
+    back = exchange(after(out, piece), "uly")
     pieces = (piece, back)
-    both = outer(back, tokens, earlier, (ups_a, ups_b), rank, piece)
+    low = back.reshape(parts, rows, -1)[:, :, CALLS[1] * HEAD :].astype(F32)
+    low = jnp.sum(low, axis=0)
+    returned = lax.ppermute(
+        low[:, 2 * rank : 3 * rank], "blk", [(i, i - 1) for i in range(1, blocks)]
+    )
+    low = jnp.concatenate([low[:, :rank], low[:, rank : 2 * rank] + returned], 1).astype(BF16)
+    both = outer(low, tokens, (ups_a, ups_b), piece)
     both = summed(both.reshape(-1, HEAD), "blk", 2, PAIR)
     length = columns // HEAD * rank
     down = summed(both[:length], "uly", parts)

time: 292 us -> 294 us (level)
  blocking collectives: 39 us -> 87.8 us
  waiting for transfers between devices: 109 us -> 75.4 us
  starting transfers between devices: 72 us -> 48.4 us
  local copies, waits for them, and re-layouts: 9.01 us -> 15.7 us
  other arithmetic: 1.69 us -> 5.1 us
    all_to_all x4 -> x5, blocking collectives: 39 us -> 87.8 us  [exchange(): lax.all_to_all(array, axis, split_axis=0, concat_axis=0, tiled=True, axis...]
    all_to_all x7 -> x6, waiting for transfers between devices: 96.5 us -> 61.1 us  [exchange(): lax.all_to_all(array, axis, split_axis=0, concat_axis=0, tiled=True, axis...]
    all_to_all x7 -> x6, starting transfers between devices: 56.3 us -> 26.7 us  [exchange(): lax.all_to_all(array, axis, split_axis=0, concat_axis=0, tiled=True, axis...]
    unnamed x20 -> x18, local copies, waits for them, and re-layouts: 3.28 us -> 7.46 us
    ppermute x1 -> x3, starting transfers between devices: 1.91 us -> 5.6 us  [the longest x1 4.12 us: per_device(): lax.ppermute(low[:, 2 * rank:3 * rank], 'blk', [(i, i - 1) for i in range...]
    concatenate x0 -> x3, other arithmetic: none -> 3.19 us  [the longest x1 1.45 us: per_device(): wrap_a = jnp.concatenate([k[:, :split], vl[:, :split + 2 * rank]], 1)]
  transfers between devices with their start and end apart: 12 -> 13, of which waited for: 7 -> 8; matrix products, arithmetic and copies ran while one was open for 1% -> 2% of each run, Pallas kernels for 18% -> 18%
where the time goes in v5:
time: 294 us; the launch traced here: 293 us
  blocking collectives  87.8 us (30%)
  waiting for transfers between devices  75.4 us (26%)
  Pallas kernels  59.8 us (20%)
  starting transfers between devices  48.4 us (16%)
  local copies, waits for them, and re-layouts  15.7 us (5%)
  other arithmetic  5.1 us (2%)
    all_to_all x5, blocking collectives, exchange(): lax.all_to_all(array, axis, split_axis=0, concat_axis=0, tiled=True, axis...  87.8 us
    all_to_all x6, waiting for transfers between devices, exchange(): lax.all_to_all(array, axis, split_axis=0, concat_axis=0, tiled=True, axis...  61.1 us
    pallas_call x2, Pallas kernels, attention(): pl.pallas_call(functools.partial(attention_kernel, begins, ends), grid_sp...  44.2 us
    all_to_all x6, starting transfers between devices, exchange(): lax.all_to_all(array, axis, split_axis=0, concat_axis=0, tiled=True, axis...  26.7 us
    all_to_all x1, waiting for transfers between devices, per_device(): k = lax.all_to_all(key_base, 'uly', split_axis=1, concat_axis=0, tiled=True)  10.2 us
    pallas_call x1, Pallas kernels, pack(): pl.pallas_call(pack_kernel, grid=(parts,), in_specs=[pl.BlockSpec((rows,...  9.9 us
    all_to_all x1, starting transfers between devices, per_device(): k = lax.all_to_all(key_base, 'uly', split_axis=1, concat_axis=0, tiled=True)  7.48 us
    unnamed x18, local copies, waits for them, and re-layouts  7.46 us
  transfers between devices with their start and end apart: 13, of which 8 were waited for; matrix products, arithmetic and copies ran while one was open for 2% of the time, Pallas kernels for 18%

profile of v5, /device:TPU:1, one launch (start us, length us, event | category | flops | bytes accessed | tf_op | source)
XLA Modules:
  0.0 293.1 jit_solution(8022174514255837603)
XLA Ops:
  0.6 2.5 copy.27
  3.1 7.5 %all-to-all-start = ((bf16[128,8,640]{2,0,1:T(8,128)(2,1)}), bf16[128,8,640]{2,0,1:T(8,128)(2,1)S(1)}, u32[]{:S(2)}, u32[]{:S(2)}) async-start(bf16[128,8,640]{2,0,1:T(8,128)(2,1)} %bitcast.31), calls=%async_computation | async-start | bytes 2621440 | tf_op jit(solution)/shard_map/all_to_all | solution.py:339
  10.6 9.9 %pack.1 = (bf16[1024,768]{1,0:T(8,128)(2,1)}, bf16[1024,768]{1,0:T(8,128)(2,1)}, bf16[1024,512]{1,0:T(8,128)(2,1)}) custom-call(bf16[128,5120]{1,0:T(8,128)(2,1)} %tokens.3, bf16[128,5120]{1,0:T(8,128)(2,1)} %query_base.1, bf16[128,5120]{1,0:T(8,128)(2,1)} %value_base.1, bf16[128,5120]{1,0:T(8,128)(2,1)} %out_grad.1, bf16[64,5120]{1,0:T(8,128)(2,1)} %bitcast.54, ...), custom_call_target="tpu_custom_call" | custom-call | flops 536870912 | bytes 14680064 | tf_op jit(solution)/shard_map/pack/pallas_call | solution.py:67
  20.5 10.2 %all-to-all-done = bf16[128,8,640]{2,0,1:T(8,128)(2,1)S(1)} async-done(((bf16[128,8,640]{2,0,1:T(8,128)(2,1)}), bf16[128,8,640]{2,0,1:T(8,128)(2,1)S(1)}, u32[]{:S(2)}, u32[]{:S(2)}) %all-to-all-start) | async-done | bytes 1310752 | tf_op jit(solution)/shard_map/all_to_all | solution.py:339
  30.7 1.1 copy-done.3
  31.8 4.4 %all-to-all-start.1 = ((bf16[8,128,768]{2,1,0:T(8,128)(2,1)}), bf16[8,128,768]{2,1,0:T(8,128)(2,1)}, u32[]{:S(2)}, u32[]{:S(2)}) async-start(bf16[8,128,768]{2,1,0:T(8,128)(2,1)} %bitcast.44), calls=%async_computation.1 | async-start | bytes 3145728 | tf_op jit(solution)/shard_map/all_to_all | solution.py:301
  36.2 0.0 copy-done.4
  36.2 4.3 %collective-permute-start = (bf16[1024,640]{1,0:T(8,128)(2,1)S(1)}, bf16[1024,640]{1,0:T(8,128)(2,1)S(1)}, u32[]{:S(2)}, u32[]{:S(2)}) collective-permute-start(bf16[1024,640]{1,0:T(8,128)(2,1)S(1)} %bitcast.41), channel_id=1, source_target_pairs={{0,8},{8,16},{16,24},{24,32},{32,40},{40,48},{48,56},{56,64},{64,7... | collective-permute-start | bytes 3932168 | tf_op jit(solution)/shard_map/ppermute | solution.py:340
  40.5 18.7 %all-to-all-done.1 = bf16[8,128,768]{2,1,0:T(8,128)(2,1)} async-done(((bf16[8,128,768]{2,1,0:T(8,128)(2,1)}), bf16[8,128,768]{2,1,0:T(8,128)(2,1)}, u32[]{:S(2)}, u32[]{:S(2)}) %all-to-all-start.1) | async-done | bytes 1572896 | tf_op jit(solution)/shard_map/all_to_all | solution.py:301
  59.2 4.2 %collective-permute-start.1 = (bf16[1024,768]{1,0:T(8,128)(2,1)}, bf16[1024,768]{1,0:T(8,128)(2,1)}, u32[]{:S(2)}, u32[]{:S(2)}) collective-permute-start(bf16[1024,768]{1,0:T(8,128)(2,1)} %bitcast.7.refs_1_.v_own.low_own), channel_id=1, source_target_pairs={{0,8},{8,16},{16,24},{24,32},{32,40},{40,48},{48,56},{56,64},{64,7... | collective-permute-start | bytes 4718600 | tf_op jit(solution)/shard_map/ppermute | solution.py:342
  63.4 0.0 collective-permute-done.refs_2_.k_straight
  63.5 1.0 copy-done.6
  64.5 3.6 %all-to-all-start.2 = ((bf16[8,128,768]{2,1,0:T(8,128)(2,1)}), bf16[8,128,768]{2,1,0:T(8,128)(2,1)S(1)}, u32[]{:S(2)}, u32[]{:S(2)}) async-start(bf16[8,128,768]{2,1,0:T(8,128)(2,1)} %bitcast.45), calls=%async_computation.2 | async-start | bytes 3145728 | tf_op jit(solution)/shard_map/all_to_all | solution.py:301
  68.1 0.1 slice.53
  68.2 1.3 slice.54
  69.5 1.4 pad_maximum_fusion.refs_0_
  70.9 20.0 %all-to-all-done.2 = bf16[8,128,768]{2,1,0:T(8,128)(2,1)S(1)} async-done(((bf16[8,128,768]{2,1,0:T(8,128)(2,1)}), bf16[8,128,768]{2,1,0:T(8,128)(2,1)S(1)}, u32[]{:S(2)}, u32[]{:S(2)}) %all-to-all-start.2) | async-done | bytes 1572896 | tf_op jit(solution)/shard_map/all_to_all | solution.py:301
  90.9 0.0 collective-permute-done.1.refs_2_.v_straight.low_straight
  90.9 1.2 copy-done
  92.1 0.8 collective-permute-start.2
  92.9 0.7 pad_add_fusion.place
  93.6 1.1 slice.56
  94.7 1.0 pad_maximum_fusion.1.refs_0_
  95.7 5.8 %all-to-all-start.4 = ((bf16[8,128,512]{2,1,0:T(8,128)(2,1)}), bf16[8,128,512]{2,1,0:T(8,128)(2,1)S(1)}, u32[]{:S(2)}, u32[]{:S(2)}) async-start(bf16[8,128,512]{2,1,0:T(8,128)(2,1)} %bitcast.46), calls=%async_computation.4 | async-start | bytes 2097152 | tf_op jit(solution)/shard_map/all_to_all | solution.py:301
  101.5 0.0 collective-permute-done.2.k_wrapped.v_wrapped.low_wrapped.refs_1_
  101.5 0.0 copy-start.5
  101.5 1.3 copy-done.5
  102.8 0.7 collective-permute-start.3
  103.5 25.4 %attention.2 = (bf16[1024,384]{1,0:T(8,128)(2,1)}, bf16[2,192,128]{2,1,0:T(8,128)(2,1)}, f32[1024,64]{1,0:T(8,128)}, f32[64,1024]{1,0:T(8,128)}, f32[64,1024]{1,0:T(8,128)}) custom-call(s32[2]{0:T(128)} %pad_add_fusion.place, bf16[1024,768]{1,0:T(8,128)(2,1)} %bitcast.34, bf16[1024,768]{1,0:T(8,128)(2,1)} %bitcast.35, bf16[1024,640]{1,0:T(8,128)(2,1)} %bitcast.39, ...), custom_call_target="tpu_custom_call" | custom-call | flops 32212254720 | bytes 6291456 | tf_op jit(solution)/shard_map/attention/pallas_call | solution.py:202
  128.9 1.0 all-to-all-done.4
  129.9 1.0 copy-done.7
  131.0 5.8 %all-to-all-start.3 = ((bf16[8,128,384]{2,1,0:T(8,128)(2,1)}), bf16[8,128,384]{2,1,0:T(8,128)(2,1)S(1)}, u32[]{:S(2)}, u32[]{:S(2)}) async-start(bf16[8,128,384]{2,1,0:T(8,128)(2,1)} %bitcast.53), calls=%async_computation.3 | async-start | bytes 1572864 | tf_op jit(solution)/shard_map/all_to_all | solution.py:301
  136.8 0.0 collective-permute-done.3.k_wrapped.v_wrapped
  136.8 1.0 copy-done.8
  137.8 18.8 %attention.3 = (bf16[1024,512]{1,0:T(8,128)(2,1)}, bf16[2,128,128]{2,1,0:T(8,128)(2,1)}) custom-call(s32[2]{0:T(128)} %pad_add_fusion.place, bf16[1024,512]{1,0:T(8,128)(2,1)} %bitcast.51, bf16[1024,512]{1,0:T(8,128)(2,1)} %bitcast.52, bf16[1024,640]{1,0:T(8,128)(2,1)} %bitcast.40, bf16[1024,768]{1,0:T(8,128)(2,1)} %bitcast.7.refs_1_.v_own.low_own, ...), custom_call_target="tpu_custom_call" | custom-call | flops 21474836480 | bytes 4194304 | tf_op jit(solution)/shard_map/attention/pallas_call | solution.py:202
  156.6 0.0 all-to-all-done.3
  156.6 0.0 copy-start.1
  156.6 0.9 copy-done.1
  157.5 22.6 %all_to_all.114 = bf16[8,128,512]{2,1,0:T(8,128)(2,1)S(1)} all-to-all(bf16[8,128,512]{2,1,0:T(8,128)(2,1)} %bitcast.47), channel_id=1, replica_groups=mesh['blk'=32,'uly'=8] {'uly'}, dimensions={0} | all-to-all | bytes 2097152 | tf_op jit(solution)/shard_map/all_to_all | solution.py:301
  180.1 0.1 convert_reduce_fusion
  180.2 4.1 %collective-permute-start.4 = (f32[128,64]{1,0:T(8,128)S(1)}, f32[128,64]{1,0:T(8,128)S(1)}, u32[]{:S(2)}, u32[]{:S(2)}) collective-permute-start(f32[128,64]{1,0:T(8,128)S(1)} %slice.61), channel_id=1, source_target_pairs={{8,0},{16,8},{24,16},{32,24},{40,32},{48,40},{56,48},{64,56},{72,6... | collective-permute-start | bytes 98312 | tf_op jit(solution)/shard_map/ppermute | solution.py:359
  184.3 1.4 collective-permute-done.4
  185.7 0.1 fusion
  185.8 0.7 pad_maximum_fusion.4.low
  186.5 3.0 %outer.1 = bf16[2,2880,128]{2,1,0:T(8,128)(2,1)} custom-call(bf16[128,128]{1,0:T(8,128)(2,1)} %pad_maximum_fusion.4.low, bf16[128,5120]{1,0:T(8,128)(2,1)} %tokens.3, bf16[2,192,128]{2,1,0:T(8,128)(2,1)} %get-tuple-element.27.rest_0_, bf16[2,128,128]{2,1,0:T(8,128)(2,1)} %get-tuple-element.28.rest_1_, bf16[1024,384]{1,0:T(8,128)(2,1)} %bitcast.37), custom_call_target="tpu_custom_call" | custom-call | flops 536870912 | bytes 8388608 | tf_op jit(solution)/shard_map/outer/pallas_call | solution.py:263
  189.5 5.7 %all_to_all.115 = bf16[2,2880,128]{2,1,0:T(8,128)(2,1)S(1)} all-to-all(bf16[2,2880,128]{2,1,0:T(8,128)(2,1)} %outer.1), channel_id=1, replica_groups={{0,8},{16,24},{32,40},{48,56},{64,72},{80,88},{96,104},{112,120},{128,1..., dimensions={0} | all-to-all | bytes 2949120 | tf_op jit(solution)/shard_map/all_to_all | solution.py:301
  195.2 0.8 reduce_sum.46
  196.0 0.9 slice.62
  196.9 3.5 %all-to-all-start.7 = ((bf16[8,320,128]{2,1,0:T(8,128)(2,1)}), bf16[8,320,128]{2,1,0:T(8,128)(2,1)S(1)}, u32[]{:S(2)}, u32[]{:S(2)}) async-start(bf16[8,320,128]{2,1,0:T(8,128)(2,1)} %bitcast.17), calls=%async_computation.7 | async-start | bytes 1310720 | tf_op jit(solution)/shard_map/all_to_all | solution.py:301
  200.4 13.1 %all-to-all-done.7 = bf16[8,320,128]{2,1,0:T(8,128)(2,1)S(1)} async-done(((bf16[8,320,128]{2,1,0:T(8,128)(2,1)}), bf16[8,320,128]{2,1,0:T(8,128)(2,1)S(1)}, u32[]{:S(2)}, u32[]{:S(2)}) %all-to-all-start.7) | async-done | bytes 655392 | tf_op jit(solution)/shard_map/all_to_all | solution.py:301
  213.5 0.1 reduce_sum.47
  213.7 37.4 %all_to_all.116 = bf16[8,80,128]{2,1,0:T(8,128)(2,1)S(1)} all-to-all(bf16[8,80,128]{2,1,0:T(8,128)(2,1)S(1)} %pad_maximum_fusion.3), channel_id=1, replica_groups={{0,16,32,48,64,80,96,112},{8,24,40,56,72,88,104,120},{128,144,160,176,1..., dimensions={0} | all-to-all | bytes 327680 | tf_op jit(solution)/shard_map/all_to_all | solution.py:301
  251.1 0.1 collective-permute-start.5
  251.2 2.6 collective-permute-done.5
  253.8 10.9 %all_to_all.117 = bf16[8,80,128]{2,1,0:T(8,128)(2,1)S(1)} all-to-all(bf16[8,80,128]{2,1,0:T(8,128)(2,1)S(1)} %broadcast_in_dim.8), channel_id=1, replica_groups={{0,16,32,48,64,80,96,112},{8,24,40,56,72,88,104,120},{128,144,160,176,1..., dimensions={0} | all-to-all | bytes 327680 | tf_op jit(solution)/shard_map/all_to_all | solution.py:301
  264.8 0.0 copy-start.2
  264.8 0.9 broadcast_in_dim.10
  265.7 3.5 %all-to-all-start.10 = ((bf16[8,320,128]{2,1,0:T(8,128)(2,1)}), bf16[8,320,128]{2,1,0:T(8,128)(2,1)S(1)}, u32[]{:S(2)}, u32[]{:S(2)}) async-start(bf16[8,320,128]{2,1,0:T(8,128)(2,1)} %broadcast_in_dim.10), calls=%async_computation.10 | async-start | bytes 1310720 | tf_op jit(solution)/shard_map/all_to_all | solution.py:301
  269.3 0.2 maximum_bitcast_fusion
  269.5 1.2 copy.25
  270.7 8.3 %all-to-all-done.10 = bf16[8,320,128]{2,1,0:T(8,128)(2,1)S(1)} async-done(((bf16[8,320,128]{2,1,0:T(8,128)(2,1)}), bf16[8,320,128]{2,1,0:T(8,128)(2,1)S(1)}, u32[]{:S(2)}, u32[]{:S(2)}) %all-to-all-start.10) | async-done | bytes 655392 | tf_op jit(solution)/shard_map/all_to_all | solution.py:301
  279.0 0.1 broadcast_in_dim.22
  279.1 11.2 %all_to_all.118.both = bf16[2,2880,128]{2,1,0:T(8,128)(2,1)} all-to-all(bf16[2,2880,128]{2,1,0:T(8,128)(2,1)S(1)} %broadcast_in_dim.22), channel_id=1, replica_groups={{0,8},{16,24},{32,40},{48,56},{64,72},{80,88},{96,104},{112,120},{128,1..., dimensions={0} | all-to-all | bytes 2949120 | tf_op jit(solution)/shard_map/all_to_all | solution.py:301
  290.3 2.7 unpack.1
  (24 shorter events, 0.2 us)
Async XLA Ops:
  3.1 27.6 %all-to-all-start = ((bf16[128,8,640]{2,0,1:T(8,128)(2,1)}), bf16[128,8,640]{2,0,1:T(8,128)(2,1)S(1)}, u32[]{:S(2)}, u32[]{:S(2)}) async-start(bf16[128,8,640]{2,0,1:T(8,128)(2,1)} %bitcast.31), calls=%async_computation | async-start | bytes 2621440 | tf_op jit(solution)/shard_map/all_to_all | solution.py:339
  30.7 1.1 copy-start.3
  31.8 4.4 %copy-start.4 = (bf16[128,8,640]{2,0,1:T(8,128)(2,1)S(1)}, bf16[128,8,640]{2,0,1:T(8,128)(2,1)}, u32[]{:S(2)}) copy-start(bf16[128,8,640]{2,0,1:T(8,128)(2,1)} %copy-done.3) | copy-start | bytes 3932164
  31.8 27.4 %all-to-all-start.1 = ((bf16[8,128,768]{2,1,0:T(8,128)(2,1)}), bf16[8,128,768]{2,1,0:T(8,128)(2,1)}, u32[]{:S(2)}, u32[]{:S(2)}) async-start(bf16[8,128,768]{2,1,0:T(8,128)(2,1)} %bitcast.44), calls=%async_computation.1 | async-start | bytes 3145728 | tf_op jit(solution)/shard_map/all_to_all | solution.py:301
  36.2 27.2 %collective-permute-start = (bf16[1024,640]{1,0:T(8,128)(2,1)S(1)}, bf16[1024,640]{1,0:T(8,128)(2,1)S(1)}, u32[]{:S(2)}, u32[]{:S(2)}) collective-permute-start(bf16[1024,640]{1,0:T(8,128)(2,1)S(1)} %bitcast.41), channel_id=1, source_target_pairs={{0,8},{8,16},{16,24},{24,32},{32,40},{40,48},{48,56},{56,64},{64,7... | collective-permute-start | bytes 3932168 | tf_op jit(solution)/shard_map/ppermute | solution.py:340
  59.2 31.7 %collective-permute-start.1 = (bf16[1024,768]{1,0:T(8,128)(2,1)}, bf16[1024,768]{1,0:T(8,128)(2,1)}, u32[]{:S(2)}, u32[]{:S(2)}) collective-permute-start(bf16[1024,768]{1,0:T(8,128)(2,1)} %bitcast.7.refs_1_.v_own.low_own), channel_id=1, source_target_pairs={{0,8},{8,16},{16,24},{24,32},{32,40},{40,48},{48,56},{56,64},{64,7... | collective-permute-start | bytes 4718600 | tf_op jit(solution)/shard_map/ppermute | solution.py:342
  63.5 1.1 copy-start.6
  64.5 26.4 %all-to-all-start.2 = ((bf16[8,128,768]{2,1,0:T(8,128)(2,1)}), bf16[8,128,768]{2,1,0:T(8,128)(2,1)S(1)}, u32[]{:S(2)}, u32[]{:S(2)}) async-start(bf16[8,128,768]{2,1,0:T(8,128)(2,1)} %bitcast.45), calls=%async_computation.2 | async-start | bytes 3145728 | tf_op jit(solution)/shard_map/all_to_all | solution.py:301
  90.9 1.2 copy-start
  92.1 9.4 %collective-permute-start.2 = (bf16[1024,896]{1,0:T(8,128)(2,1)}, bf16[1024,896]{1,0:T(8,128)(2,1)S(1)}, u32[]{:S(2)}, u32[]{:S(2)}) collective-permute-start(bf16[1024,896]{1,0:T(8,128)(2,1)} %after.8), channel_id=1, source_target_pairs={{120,128},{121,129},{122,130},{123,131},{124,132},{125,133},{126,1... | collective-permute-start | bytes 5505032 | tf_op jit(solution)/shard_map/ppermute | solution.py:346
  95.7 34.2 %all-to-all-start.4 = ((bf16[8,128,512]{2,1,0:T(8,128)(2,1)}), bf16[8,128,512]{2,1,0:T(8,128)(2,1)S(1)}, u32[]{:S(2)}, u32[]{:S(2)}) async-start(bf16[8,128,512]{2,1,0:T(8,128)(2,1)} %bitcast.46), calls=%async_computation.4 | async-start | bytes 2097152 | tf_op jit(solution)/shard_map/all_to_all | solution.py:301
  101.5 1.3 copy-start.5
  102.8 34.0 %collective-permute-start.3 = (bf16[1024,512]{1,0:T(8,128)(2,1)}, bf16[1024,512]{1,0:T(8,128)(2,1)S(1)}, u32[]{:S(2)}, u32[]{:S(2)}) collective-permute-start(bf16[1024,512]{1,0:T(8,128)(2,1)} %after.10), channel_id=1, source_target_pairs={{120,128},{121,129},{122,130},{123,131},{124,132},{125,133},{126,1... | collective-permute-start | bytes 3145736 | tf_op jit(solution)/shard_map/ppermute | solution.py:348
  129.9 1.0 copy-start.7
  131.0 25.6 %all-to-all-start.3 = ((bf16[8,128,384]{2,1,0:T(8,128)(2,1)}), bf16[8,128,384]{2,1,0:T(8,128)(2,1)S(1)}, u32[]{:S(2)}, u32[]{:S(2)}) async-start(bf16[8,128,384]{2,1,0:T(8,128)(2,1)} %bitcast.53), calls=%async_computation.3 | async-start | bytes 1572864 | tf_op jit(solution)/shard_map/all_to_all | solution.py:301
  136.8 1.0 copy-start.8
  156.6 0.9 copy-start.1
  180.2 5.6 %collective-permute-start.4 = (f32[128,64]{1,0:T(8,128)S(1)}, f32[128,64]{1,0:T(8,128)S(1)}, u32[]{:S(2)}, u32[]{:S(2)}) collective-permute-start(f32[128,64]{1,0:T(8,128)S(1)} %slice.61), channel_id=1, source_target_pairs={{8,0},{16,8},{24,16},{32,24},{40,32},{48,40},{56,48},{64,56},{72,6... | collective-permute-start | bytes 98312 | tf_op jit(solution)/shard_map/ppermute | solution.py:359
  196.9 16.7 %all-to-all-start.7 = ((bf16[8,320,128]{2,1,0:T(8,128)(2,1)}), bf16[8,320,128]{2,1,0:T(8,128)(2,1)S(1)}, u32[]{:S(2)}, u32[]{:S(2)}) async-start(bf16[8,320,128]{2,1,0:T(8,128)(2,1)} %bitcast.17), calls=%async_computation.7 | async-start | bytes 1310720 | tf_op jit(solution)/shard_map/all_to_all | solution.py:301
  251.1 2.7 collective-permute-start.5
  264.8 4.5 %copy-start.2 = (bf16[8,128,384]{2,1,0:T(8,128)(2,1)S(1)}, bf16[8,128,384]{2,1,0:T(8,128)(2,1)}, u32[]{:S(2)}) copy-start(bf16[8,128,384]{2,1,0:T(8,128)(2,1)} %copy-done.1) | copy-start | bytes 2359300
  265.7 13.3 %all-to-all-start.10 = ((bf16[8,320,128]{2,1,0:T(8,128)(2,1)}), bf16[8,320,128]{2,1,0:T(8,128)(2,1)S(1)}, u32[]{:S(2)}, u32[]{:S(2)}) async-start(bf16[8,320,128]{2,1,0:T(8,128)(2,1)} %broadcast_in_dim.10), calls=%async_computation.10 | async-start | bytes 1310720 | tf_op jit(solution)/shard_map/all_to_all | solution.py:301

commit v6 on v5

--- a/solution.py
+++ b/solution.py
@@ -12,7 +12,7 @@
 LOG2E = 1.4426950408889634
 F32 = jnp.float32
 BF16 = jnp.bfloat16
-CALLS = (3, 2)
+CALLS = (2, 3)
 
 PAIR = [[2 * i, 2 * i + 1] for i in range(16)]
 Z_RING = [[half * 16 + z * 2 + core for z in range(8)] for half in range(2) for core in range(2)]
@@ -34,7 +34,7 @@
 def pack_kernel(
     tokens, query_base, value_base, out_grad, down_q, down_v, up_q, up_v, vl, *rest
 ):
-    qgs, low = rest[:-1], rest[-1]
+    qgs, copies, low = rest[:-3], rest[-3:-1], rest[-1]
     rank = down_q.shape[0]
     width = value_base.shape[1]
 
@@ -42,6 +42,8 @@
     def _():
         low[:, :rank] = dot_t(tokens[...], down_q[...]).astype(BF16)
         low[:, rank:] = dot_t(tokens[...], down_v[...]).astype(BF16)
+        for copy in copies:
+            copy[...] = tokens[...]
 
     vl[:, : 2 * rank] = low[...]
     vl[:, 2 * rank :] = (value_base[...].astype(F32) + dot(low[:, rank:], up_v[...])).astype(
@@ -71,8 +73,10 @@
         + [pl.BlockSpec((rows, width), part)] * 3
         + [pl.BlockSpec((rank, columns), whole, pipeline_mode=once)] * 2
         + [pl.BlockSpec((rank, width), part)] * 2,
-        out_specs=[pl.BlockSpec((rows, size), lambda j: (j, 0)) for size in sizes],
-        out_shape=[jax.ShapeDtypeStruct((parts * rows, size), BF16) for size in sizes],
+        out_specs=[pl.BlockSpec((rows, size), lambda j: (j, 0)) for size in sizes]
+        + [pl.BlockSpec((rows, columns), whole)] * 2,
+        out_shape=[jax.ShapeDtypeStruct((parts * rows, size), BF16) for size in sizes]
+        + [jax.ShapeDtypeStruct((rows, columns), BF16)] * 2,
         scratch_shapes=[pltpu.VMEM((rows, 2 * rank), BF16)],
         compiler_params=pltpu.CompilerParams(vmem_limit_bytes=60 << 20),
         cost_estimate=pl.CostEstimate(flops=1 << 29, bytes_accessed=14 << 20, transcendentals=0),
@@ -175,7 +179,7 @@
 
 
 def attention(
-    place, qg, k, k_prior, vl, vl_prior, low_wrap, up_q, up_v, wrap, lows, first, heads, ends
+    place, qg, k, k_prior, vl, vl_prior, low_wrap, up_q, up_v, wraps, lows, first, heads, ends
 ):
     rows = qg.shape[0]
     total = k.shape[1] // HEAD
@@ -212,10 +216,10 @@
                 column(first),
                 column(first + 1),
                 column(0),
-                column(wrap.shape[1] // HEAD - heads),
+                column(0),
                 fixed(0),
                 fixed(0),
-                fixed(CALLS[0]),
+                fixed(0),
                 up,
                 up,
             ]
@@ -234,17 +238,20 @@
         ),
         name="attention",
     )(
-        place, qg, qg, k, vl, k_prior, vl_prior, wrap, wrap, vl, vl_prior, low_wrap, up_q, up_v,
+        place, qg, qg, k, vl, k_prior, vl_prior, *wraps, vl, vl_prior, low_wrap, up_q, up_v,
         *(() if begins else lows),
     )
 
 
-def outer_kernel(low, tokens, *rest):
-    ups, out = rest[:-2], rest[-1]
-    rank = low.shape[1] // 2
-    columns = tokens.shape[1]
+def outer_kernel(lows, tokens, straight, wrapped, *rest):
+    ups, out = rest[:-1], rest[-1]
+    rows, columns = tokens.shape
+    rank = lows.shape[1] // 4
+    low = jnp.sum(lows[...].reshape(-1, rows, 4 * rank).astype(F32), axis=0).astype(BF16)
     grad_q = t_dot(low[:, :rank], tokens[...])
-    grad_v = t_dot(low[:, rank:], tokens[...])
+    grad_v = t_dot(low[:, rank : 2 * rank], tokens[...]) + t_dot(
+        low[:, 2 * rank : 3 * rank], straight[...] + wrapped[...]
+    )
     for block in range(columns // HEAD):
         to = slice(block * rank, (block + 1) * rank)
         out[0, to, :] = grad_q[:, block * HEAD : (block + 1) * HEAD].astype(BF16)
@@ -256,21 +263,24 @@
         first += size
 
 
-def outer(low, tokens, ups, settled):
-    rank = low.shape[1] // 2
-    length = tokens.shape[1] // HEAD * rank + sum(up.shape[1] for up in ups)
+def outer(lows, first, tokens, straight, wrapped, ups):
+    columns = tokens.shape[1]
+    rank = ups[0].shape[1] // CALLS[0]
+    length = columns // HEAD * rank + sum(up.shape[1] for up in ups)
     whole = lambda array: pl.BlockSpec(array.shape, lambda i: (0,) * array.ndim)
+    at = pl.BlockSpec(
+        (pl.Element(lows.shape[0]), pl.Element(4 * rank)), lambda i: (0, first)
+    )
     return pl.pallas_call(
         outer_kernel,
         grid=(1,),
-        in_specs=[whole(array) for array in (low, tokens, *ups)]
-        + [pl.BlockSpec(memory_space=pl.ANY)],
+        in_specs=[at] + [whole(array) for array in (tokens, straight, wrapped, *ups)],
         out_specs=pl.BlockSpec((2, length, HEAD), lambda i: (0, 0, 0)),
         out_shape=jax.ShapeDtypeStruct((2, length, HEAD), BF16),
         compiler_params=pltpu.CompilerParams(vmem_limit_bytes=60 << 20),
         cost_estimate=pl.CostEstimate(flops=1 << 29, bytes_accessed=8 << 20, transcendentals=0),
         name="outer",
-    )(low, tokens, *ups, settled)
+    )(lows, tokens, straight, wrapped, *ups)
 
 
 def unpack_kernel(both, down_q, down_v, up_q, up_v):
@@ -330,7 +340,7 @@
     rows, columns = tokens.shape
     rank = down_q.shape[1]
     width = columns // parts
-    vl, qg_a, qg_b = pack(
+    vl, qg_a, qg_b, copy_a, copy_b = pack(
         tokens, query_base, value_base, out_grad, down_q.T, up_q, down_v.T, up_v, parts
     )
     crossing = blocks // 2 - 1
@@ -341,26 +351,31 @@
     vl = exchange(after(vl, k), "uly")
     vl_prior = lax.ppermute(vl, "blk", forward)
     qg_a = exchange(after(qg_a, vl, k_prior), "uly")
+    straight = lax.ppermute(after(copy_a, k_prior), "blk", forward)
     split = CALLS[0] * HEAD
-    wrap_a = jnp.concatenate([k[:, :split], vl[:, : split + 2 * rank]], 1)
-    wrap_a = lax.ppermute(after(wrap_a, qg_a, vl_prior), "blk", wrapped)
-    wrap_b = jnp.concatenate([k[:, split:], vl[:, split + 2 * rank :]], 1)
-    wrap_b = lax.ppermute(after(wrap_b, wrap_a), "blk", wrapped)
+    ready = (qg_a, vl_prior, straight)
+    low_wrap, *wraps_a = [
+        lax.ppermute(after(array, *ready), "blk", wrapped)
+        for array in (
+            vl[:, : 2 * rank],
+            k[:, :split],
+            vl[:, 2 * rank : 2 * rank + split],
+        )
+    ]
+    wraps_b = [
+        lax.ppermute(after(array, *wraps_a), "blk", wrapped)
+        for array in (k[:, split:], vl[:, 2 * rank + split :])
+    ]
+    tokens_wrap = lax.ppermute(after(copy_b, *wraps_b), "blk", wrapped)
     qg_b = exchange(after(qg_b, qg_a, vl_prior), "uly")
     place = jnp.stack([lax.axis_index("uly"), lax.axis_index("blk")]).astype(jnp.int32)
-    ready = (k, k_prior, vl, vl_prior, wrap_a, up_q, up_v)
-    out, ups_a, *lows = attention(place, qg_a, *ready, wrap_a, None, 0, CALLS[0], False)
+    ready = (k, k_prior, vl, vl_prior, low_wrap, up_q, up_v)
+    out, ups_a, *lows = attention(place, qg_a, *ready, wraps_a, None, 0, CALLS[0], False)
     piece = exchange(out, "uly")
-    out, ups_b = attention(place, qg_b, *ready, wrap_b, lows, CALLS[0], CALLS[1], True)
+    out, ups_b = attention(place, qg_b, *ready, wraps_b, lows, CALLS[0], CALLS[1], True)
     back = exchange(after(out, piece), "uly")
     pieces = (piece, back)
-    low = back.reshape(parts, rows, -1)[:, :, CALLS[1] * HEAD :].astype(F32)
-    low = jnp.sum(low, axis=0)
-    returned = lax.ppermute(
-        low[:, 2 * rank : 3 * rank], "blk", [(i, i - 1) for i in range(1, blocks)]
-    )
-    low = jnp.concatenate([low[:, :rank], low[:, rank : 2 * rank] + returned], 1).astype(BF16)
-    both = outer(low, tokens, (ups_a, ups_b), piece)
+    both = outer(back, CALLS[1] * HEAD, tokens, straight, tokens_wrap, (ups_a, ups_b))
     both = summed(both.reshape(-1, HEAD), "blk", 2, PAIR)
     length = columns // HEAD * rank
     down = summed(both[:length], "uly", parts)

time: 294 us -> 285 us (0.969)
  blocking collectives: 87.8 us -> 66 us
  waiting for transfers between devices: 75.4 us -> 85.5 us
  local copies, waits for them, and re-layouts: 15.7 us -> 21.8 us
  other arithmetic: 5.1 us -> 1.66 us
    all_to_all x5, blocking collectives: 87.8 us -> 66 us  [exchange(): lax.all_to_all(array, axis, split_axis=0, concat_axis=0, tiled=True, axis...]
    ppermute x3 -> x7, waiting for transfers between devices: 1.45 us -> 8.93 us  [the longest x1 8.91 us: per_device(): straight = lax.ppermute(after(copy_a, k_prior), 'blk', forward)]
    slice x6 -> x5, local copies, waits for them, and re-layouts: 2.5 us -> 8.49 us  [the longest x1 2.13 us: per_device(): vl[:, 2 * rank + split:]]
    all_to_all x6, starting transfers between devices: 26.7 us -> 23.2 us  [exchange(): lax.all_to_all(array, axis, split_axis=0, concat_axis=0, tiled=True, axis...]
    all_to_all x6, waiting for transfers between devices: 61.1 us -> 64.4 us  [exchange(): lax.all_to_all(array, axis, split_axis=0, concat_axis=0, tiled=True, axis...]
    concatenate x3 -> x0, other arithmetic: 3.19 us -> none  [the longest x1 1.45 us: per_device(): wrap_a = jnp.concatenate([k[:, :split], vl[:, :split + 2 * rank]], 1)]
    ppermute x3 -> x7, starting transfers between devices: 5.6 us -> 6.24 us  [the longest x3 2.17 us: per_device(): lax.ppermute(after(array, *ready), 'blk', wrapped)]
    unnamed x18 -> x28, local copies, waits for them, and re-layouts: 7.46 us -> 7.56 us
  transfers between devices with their start and end apart: 13 -> 17, of which waited for: 8 -> 8; matrix products, arithmetic and copies ran while one was open for 2% -> 4% of each run, Pallas kernels for 18% -> 19%
where the time goes in v6:
time: 285 us; the launch traced here: 283 us
  waiting for transfers between devices  85.5 us (30%)
  blocking collectives  66 us (23%)
  Pallas kernels  61.6 us (22%)
  starting transfers between devices  45.5 us (16%)
  local copies, waits for them, and re-layouts  21.8 us (8%)
    all_to_all x5, blocking collectives, exchange(): lax.all_to_all(array, axis, split_axis=0, concat_axis=0, tiled=True, axis...  66 us
    all_to_all x6, waiting for transfers between devices, exchange(): lax.all_to_all(array, axis, split_axis=0, concat_axis=0, tiled=True, axis...  64.4 us
    pallas_call x2, Pallas kernels, attention(): pl.pallas_call(functools.partial(attention_kernel, begins, ends), grid_sp...  44.1 us
    all_to_all x6, starting transfers between devices, exchange(): lax.all_to_all(array, axis, split_axis=0, concat_axis=0, tiled=True, axis...  23.2 us
    pallas_call x1, Pallas kernels, pack(): pl.pallas_call(pack_kernel, grid=(parts,), in_specs=[pl.BlockSpec((rows,...  10.6 us
    all_to_all x1, waiting for transfers between devices, per_device(): k = lax.all_to_all(key_base, 'uly', split_axis=1, concat_axis=0, tiled=True)  9.56 us
    ppermute x1, waiting for transfers between devices, per_device(): straight = lax.ppermute(after(copy_a, k_prior), 'blk', forward)  8.91 us
    unnamed x28, local copies, waits for them, and re-layouts  7.56 us
  transfers between devices with their start and end apart: 17, of which 8 were waited for; matrix products, arithmetic and copies ran while one was open for 4% of the time, Pallas kernels for 19%

profile of v6, /device:TPU:1, one launch (start us, length us, event | category | flops | bytes accessed | tf_op | source)
XLA Modules:
  0.0 283.1 jit_solution(15042407482660162237)
XLA Ops:
  0.6 2.5 copy.32
  3.2 7.5 %all-to-all-start = ((bf16[128,8,640]{2,0,1:T(8,128)(2,1)}), bf16[128,8,640]{2,0,1:T(8,128)(2,1)S(1)}, u32[]{:S(2)}, u32[]{:S(2)}) async-start(bf16[128,8,640]{2,0,1:T(8,128)(2,1)} %bitcast.32), calls=%async_computation | async-start | bytes 2621440 | tf_op jit(solution)/shard_map/all_to_all | solution.py:349
  10.6 10.6 %pack.1 = (bf16[1024,768]{1,0:T(8,128)(2,1)}, bf16[1024,512]{1,0:T(8,128)(2,1)}, bf16[1024,768]{1,0:T(8,128)(2,1)}, bf16[128,5120]{1,0:T(8,128)(2,1)}, bf16[128,5120]{1,0:T(8,128)(2,1)}) custom-call(bf16[128,5120]{1,0:T(8,128)(2,1)} %tokens.3, bf16[128,5120]{1,0:T(8,128)(2,1)} %query_base.1, bf16[128,5120]{1,0:T(8,128)(2,1)} %value_base.1, ...), custom_call_target="tpu_custom_call" | custom-call | flops 536870912 | bytes 14680064 | tf_op jit(solution)/shard_map/pack/pallas_call | solution.py:69
  21.2 9.6 %all-to-all-done = bf16[128,8,640]{2,0,1:T(8,128)(2,1)S(1)} async-done(((bf16[128,8,640]{2,0,1:T(8,128)(2,1)}), bf16[128,8,640]{2,0,1:T(8,128)(2,1)S(1)}, u32[]{:S(2)}, u32[]{:S(2)}) %all-to-all-start) | async-done | bytes 1310752 | tf_op jit(solution)/shard_map/all_to_all | solution.py:349
  30.8 1.1 copy-done.2
  31.8 4.4 %all-to-all-start.1 = ((bf16[8,128,768]{2,1,0:T(8,128)(2,1)}), bf16[8,128,768]{2,1,0:T(8,128)(2,1)}, u32[]{:S(2)}, u32[]{:S(2)}) async-start(bf16[8,128,768]{2,1,0:T(8,128)(2,1)} %bitcast.46), calls=%async_computation.1 | async-start | bytes 3145728 | tf_op jit(solution)/shard_map/all_to_all | solution.py:311
  36.3 4.3 %collective-permute-start = (bf16[1024,640]{1,0:T(8,128)(2,1)S(1)}, bf16[1024,640]{1,0:T(8,128)(2,1)}, u32[]{:S(2)}, u32[]{:S(2)}) collective-permute-start(bf16[1024,640]{1,0:T(8,128)(2,1)S(1)} %bitcast.43), channel_id=1, source_target_pairs={{0,8},{8,16},{16,24},{24,32},{32,40},{40,48},{48,56},{56,64},{64,7... | collective-permute-start | bytes 3932168 | tf_op jit(solution)/shard_map/ppermute | solution.py:350
  40.6 18.7 %all-to-all-done.1 = bf16[8,128,768]{2,1,0:T(8,128)(2,1)} async-done(((bf16[8,128,768]{2,1,0:T(8,128)(2,1)}), bf16[8,128,768]{2,1,0:T(8,128)(2,1)}, u32[]{:S(2)}, u32[]{:S(2)}) %all-to-all-start.1) | async-done | bytes 1572896 | tf_op jit(solution)/shard_map/all_to_all | solution.py:311
  59.2 4.2 %collective-permute-start.1 = (bf16[1024,768]{1,0:T(8,128)(2,1)}, bf16[1024,768]{1,0:T(8,128)(2,1)S(1)}, u32[]{:S(2)}, u32[]{:S(2)}) collective-permute-start(bf16[1024,768]{1,0:T(8,128)(2,1)} %bitcast.7.refs_1_.v_own.low_own), channel_id=1, source_target_pairs={{0,8},{8,16},{16,24},{24,32},{32,40},{40,48},{48,56},{56,64},{64,7... | collective-permute-start | bytes 4718600 | tf_op jit(solution)/shard_map/ppermute | solution.py:352
  63.5 0.0 collective-permute-done.refs_2_.refs_1_.k_straight
  63.5 1.9 collective-permute-start.2
  65.4 3.6 %all-to-all-start.2 = ((bf16[8,128,512]{2,1,0:T(8,128)(2,1)}), bf16[8,128,512]{2,1,0:T(8,128)(2,1)S(1)}, u32[]{:S(2)}, u32[]{:S(2)}) async-start(bf16[8,128,512]{2,1,0:T(8,128)(2,1)} %bitcast.50), calls=%async_computation.2 | async-start | bytes 2097152 | tf_op jit(solution)/shard_map/all_to_all | solution.py:311
  69.0 1.9 slice.40.refs_0_
  70.9 1.9 slice.41.refs_0_
  72.8 13.5 %all-to-all-done.2 = bf16[8,128,512]{2,1,0:T(8,128)(2,1)S(1)} async-done(((bf16[8,128,512]{2,1,0:T(8,128)(2,1)}), bf16[8,128,512]{2,1,0:T(8,128)(2,1)S(1)}, u32[]{:S(2)}, u32[]{:S(2)}) %all-to-all-start.2) | async-done | bytes 1048608 | tf_op jit(solution)/shard_map/all_to_all | solution.py:311
  86.3 8.9 %collective-permute-done.2.refs_3_.straight = bf16[128,5120]{1,0:T(8,128)(2,1)} collective-permute-done((bf16[128,5120]{1,0:T(8,128)(2,1)}, bf16[128,5120]{1,0:T(8,128)(2,1)}, u32[]{:S(2)}, u32[]{:S(2)}) %collective-permute-start.2) | collective-permute-done | bytes 1310752 | tf_op jit(solution)/shard_map/ppermute | solution.py:354
  95.2 1.1 copy-done.1
  96.3 0.7 collective-permute-start.3
  97.0 0.7 collective-permute-start.4
  97.7 1.7 slice.42.refs_0_
  99.4 0.8 collective-permute-start.5
  100.2 0.6 pad_add_fusion.place
  100.8 1.0 slice.43.refs_0_
  101.8 2.1 slice.44.refs_0_
  103.9 4.3 %all-to-all-start.4 = ((bf16[8,128,768]{2,1,0:T(8,128)(2,1)}), bf16[8,128,768]{2,1,0:T(8,128)(2,1)}, u32[]{:S(2)}, u32[]{:S(2)}) async-start(bf16[8,128,768]{2,1,0:T(8,128)(2,1)} %bitcast.47), calls=%async_computation.4 | async-start | bytes 3145728 | tf_op jit(solution)/shard_map/all_to_all | solution.py:311
  108.2 0.0 collective-permute-done.3.k_wrapped.refs_1_
  108.2 0.0 copy-start.8
  108.2 0.8 copy-done.8
  109.0 0.8 copy-done.9
  109.8 0.7 collective-permute-start.6
  110.5 0.7 collective-permute-start.7
  111.2 0.0 collective-permute-done.5.low_wrapped
  111.3 0.7 copy-done.13
  112.0 18.2 %attention.2 = (bf16[1024,256]{1,0:T(8,128)(2,1)}, bf16[2,128,128]{2,1,0:T(8,128)(2,1)}, f32[1024,64]{1,0:T(8,128)}, f32[64,1024]{1,0:T(8,128)}, f32[64,1024]{1,0:T(8,128)}) custom-call(s32[2]{0:T(128)} %pad_add_fusion.place, bf16[1024,512]{1,0:T(8,128)(2,1)} %bitcast.37, bf16[1024,512]{1,0:T(8,128)(2,1)} %bitcast.38, bf16[1024,640]{1,0:T(8,128)(2,1)} %bitcast.41, ...), custom_call_target="tpu_custom_call" | custom-call | flops 21474836480 | bytes 4194304 | tf_op jit(solution)/shard_map/attention/pallas_call | solution.py:206
  130.2 0.9 copy-done.11
  131.1 0.3 copy-done.12
  131.4 0.7 collective-permute-start.8
  132.1 10.8 %all-to-all-done.4 = bf16[8,128,768]{2,1,0:T(8,128)(2,1)} async-done(((bf16[8,128,768]{2,1,0:T(8,128)(2,1)}), bf16[8,128,768]{2,1,0:T(8,128)(2,1)}, u32[]{:S(2)}, u32[]{:S(2)}) %all-to-all-start.4) | async-done | bytes 1572896 | tf_op jit(solution)/shard_map/all_to_all | solution.py:311
  142.9 3.7 %all-to-all-start.3 = ((bf16[8,128,256]{2,1,0:T(8,128)(2,1)}), bf16[8,128,256]{2,1,0:T(8,128)(2,1)S(1)}, u32[]{:S(2)}, u32[]{:S(2)}) async-start(bf16[8,128,256]{2,1,0:T(8,128)(2,1)} %bitcast.11), calls=%async_computation.3 | async-start | bytes 1048576 | tf_op jit(solution)/shard_map/all_to_all | solution.py:311
  146.6 25.9 %attention.3 = (bf16[1024,640]{1,0:T(8,128)(2,1)}, bf16[2,192,128]{2,1,0:T(8,128)(2,1)}) custom-call(s32[2]{0:T(128)} %pad_add_fusion.place, bf16[1024,768]{1,0:T(8,128)(2,1)} %bitcast.13.q.g, bf16[1024,768]{1,0:T(8,128)(2,1)} %bitcast.13.q.g, bf16[1024,640]{1,0:T(8,128)(2,1)} %bitcast.42, bf16[1024,768]{1,0:T(8,128)(2,1)} %bitcast.7.refs_1_.v_own.low_own, ...), custom_call_target="tpu_custom_call" | custom-call | flops 32212254720 | bytes 6291456 | tf_op jit(solution)/shard_map/attention/pallas_call | solution.py:206
  172.6 0.0 copy-start.6
  172.6 0.8 copy-done.6
  173.4 25.4 %all_to_all.116 = bf16[8,128,640]{2,1,0:T(8,128)(2,1)} all-to-all(bf16[8,128,640]{2,1,0:T(8,128)(2,1)} %bitcast.48), channel_id=1, replica_groups=mesh['blk'=32,'uly'=8] {'uly'}, dimensions={0} | all-to-all | bytes 2621440 | tf_op jit(solution)/shard_map/all_to_all | solution.py:311
  198.7 1.1 copy-done.10
  199.8 4.2 %outer.1 = bf16[2,2880,128]{2,1,0:T(8,128)(2,1)} custom-call(bf16[1024,640]{1,0:T(8,128)(2,1)} %bitcast.45, bf16[128,5120]{1,0:T(8,128)(2,1)} %tokens.3, bf16[128,5120]{1,0:T(8,128)(2,1)} %collective-permute-done.2.refs_3_.straight, bf16[128,5120]{1,0:T(8,128)(2,1)} %copy-done.10, bf16[2,128,128]{2,1,0:T(8,128)(2,1)} %get-tuple-element.31.rest_0_, ...), custom_call_target="tpu_custom_call" | custom-call | flops 536870912 | bytes 8388608 | tf_op jit(solution)/shard_map/outer/pallas_call | solution.py:274
  203.9 8.0 %all_to_all.117 = bf16[2,2880,128]{2,1,0:T(8,128)(2,1)S(1)} all-to-all(bf16[2,2880,128]{2,1,0:T(8,128)(2,1)} %outer.1), channel_id=1, replica_groups={{0,8},{16,24},{32,40},{48,56},{64,72},{80,88},{96,104},{112,120},{128,1..., dimensions={0} | all-to-all | bytes 2949120 | tf_op jit(solution)/shard_map/all_to_all | solution.py:311
  212.0 0.8 reduce_sum.36
  212.7 0.9 slice.46
  213.6 3.5 %all-to-all-start.7 = ((bf16[8,320,128]{2,1,0:T(8,128)(2,1)}), bf16[8,320,128]{2,1,0:T(8,128)(2,1)S(1)}, u32[]{:S(2)}, u32[]{:S(2)}) async-start(bf16[8,320,128]{2,1,0:T(8,128)(2,1)} %bitcast.18), calls=%async_computation.7 | async-start | bytes 1310720 | tf_op jit(solution)/shard_map/all_to_all | solution.py:311
  217.2 13.1 %all-to-all-done.7 = bf16[8,320,128]{2,1,0:T(8,128)(2,1)S(1)} async-done(((bf16[8,320,128]{2,1,0:T(8,128)(2,1)}), bf16[8,320,128]{2,1,0:T(8,128)(2,1)S(1)}, u32[]{:S(2)}, u32[]{:S(2)}) %all-to-all-start.7) | async-done | bytes 655392 | tf_op jit(solution)/shard_map/all_to_all | solution.py:311
  230.3 0.1 reduce_sum.37
  230.4 10.8 %all_to_all.118 = bf16[8,80,128]{2,1,0:T(8,128)(2,1)S(1)} all-to-all(bf16[8,80,128]{2,1,0:T(8,128)(2,1)S(1)} %pad_maximum_fusion.1), channel_id=1, replica_groups={{0,16,32,48,64,80,96,112},{8,24,40,56,72,88,104,120},{128,144,160,176,1..., dimensions={0} | all-to-all | bytes 327680 | tf_op jit(solution)/shard_map/all_to_all | solution.py:311
  241.2 0.1 collective-permute-start.9
  241.3 2.6 collective-permute-done.9
  244.0 11.2 %all_to_all.119 = bf16[8,80,128]{2,1,0:T(8,128)(2,1)S(1)} all-to-all(bf16[8,80,128]{2,1,0:T(8,128)(2,1)S(1)} %broadcast_in_dim.8), channel_id=1, replica_groups={{0,16,32,48,64,80,96,112},{8,24,40,56,72,88,104,120},{128,144,160,176,1..., dimensions={0} | all-to-all | bytes 327680 | tf_op jit(solution)/shard_map/all_to_all | solution.py:311
  255.1 0.9 broadcast_in_dim.10
  256.1 3.7 %all-to-all-start.10 = ((bf16[8,320,128]{2,1,0:T(8,128)(2,1)}), bf16[8,320,128]{2,1,0:T(8,128)(2,1)S(1)}, u32[]{:S(2)}, u32[]{:S(2)}) async-start(bf16[8,320,128]{2,1,0:T(8,128)(2,1)} %broadcast_in_dim.10), calls=%async_computation.10 | async-start | bytes 1310720 | tf_op jit(solution)/shard_map/all_to_all | solution.py:311
  259.8 0.1 slice.45
  259.9 0.1 maximum_bitcast_fusion
  260.0 1.2 copy.30
  261.2 8.3 %all-to-all-done.10 = bf16[8,320,128]{2,1,0:T(8,128)(2,1)S(1)} async-done(((bf16[8,320,128]{2,1,0:T(8,128)(2,1)}), bf16[8,320,128]{2,1,0:T(8,128)(2,1)S(1)}, u32[]{:S(2)}, u32[]{:S(2)}) %all-to-all-start.10) | async-done | bytes 655392 | tf_op jit(solution)/shard_map/all_to_all | solution.py:311
  269.6 0.1 broadcast_in_dim.22
  269.7 10.7 %all_to_all.120.both = bf16[2,2880,128]{2,1,0:T(8,128)(2,1)} all-to-all(bf16[2,2880,128]{2,1,0:T(8,128)(2,1)S(1)} %broadcast_in_dim.22), channel_id=1, replica_groups={{0,8},{16,24},{32,40},{48,56},{64,72},{80,88},{96,104},{112,120},{128,1..., dimensions={0} | all-to-all | bytes 2949120 | tf_op jit(solution)/shard_map/all_to_all | solution.py:311
  280.4 2.7 unpack.1
  (41 shorter events, 0.2 us)
Async XLA Ops:
  3.2 27.6 %all-to-all-start = ((bf16[128,8,640]{2,0,1:T(8,128)(2,1)}), bf16[128,8,640]{2,0,1:T(8,128)(2,1)S(1)}, u32[]{:S(2)}, u32[]{:S(2)}) async-start(bf16[128,8,640]{2,0,1:T(8,128)(2,1)} %bitcast.32), calls=%async_computation | async-start | bytes 2621440 | tf_op jit(solution)/shard_map/all_to_all | solution.py:349
  30.8 1.1 copy-start.2
  31.8 4.4 %copy-start.3 = (bf16[128,8,640]{2,0,1:T(8,128)(2,1)S(1)}, bf16[128,8,640]{2,0,1:T(8,128)(2,1)}, u32[]{:S(2)}) copy-start(bf16[128,8,640]{2,0,1:T(8,128)(2,1)} %copy-done.2) | copy-start | bytes 3932164
  31.8 27.4 %all-to-all-start.1 = ((bf16[8,128,768]{2,1,0:T(8,128)(2,1)}), bf16[8,128,768]{2,1,0:T(8,128)(2,1)}, u32[]{:S(2)}, u32[]{:S(2)}) async-start(bf16[8,128,768]{2,1,0:T(8,128)(2,1)} %bitcast.46), calls=%async_computation.1 | async-start | bytes 3145728 | tf_op jit(solution)/shard_map/all_to_all | solution.py:311
  36.3 27.2 %collective-permute-start = (bf16[1024,640]{1,0:T(8,128)(2,1)S(1)}, bf16[1024,640]{1,0:T(8,128)(2,1)}, u32[]{:S(2)}, u32[]{:S(2)}) collective-permute-start(bf16[1024,640]{1,0:T(8,128)(2,1)S(1)} %bitcast.43), channel_id=1, source_target_pairs={{0,8},{8,16},{16,24},{24,32},{32,40},{40,48},{48,56},{56,64},{64,7... | collective-permute-start | bytes 3932168 | tf_op jit(solution)/shard_map/ppermute | solution.py:350
  59.2 36.0 %collective-permute-start.1 = (bf16[1024,768]{1,0:T(8,128)(2,1)}, bf16[1024,768]{1,0:T(8,128)(2,1)S(1)}, u32[]{:S(2)}, u32[]{:S(2)}) collective-permute-start(bf16[1024,768]{1,0:T(8,128)(2,1)} %bitcast.7.refs_1_.v_own.low_own), channel_id=1, source_target_pairs={{0,8},{8,16},{16,24},{24,32},{32,40},{40,48},{48,56},{56,64},{64,7... | collective-permute-start | bytes 4718600 | tf_op jit(solution)/shard_map/ppermute | solution.py:352
  63.5 31.7 %collective-permute-start.2 = (bf16[128,5120]{1,0:T(8,128)(2,1)}, bf16[128,5120]{1,0:T(8,128)(2,1)}, u32[]{:S(2)}, u32[]{:S(2)}) collective-permute-start(bf16[128,5120]{1,0:T(8,128)(2,1)} %after.13), channel_id=1, source_target_pairs={{0,8},{8,16},{16,24},{24,32},{32,40},{40,48},{48,56},{56,64},{64,7... | collective-permute-start | bytes 3932168 | tf_op jit(solution)/shard_map/ppermute | solution.py:354
  65.4 20.8 %all-to-all-start.2 = ((bf16[8,128,512]{2,1,0:T(8,128)(2,1)}), bf16[8,128,512]{2,1,0:T(8,128)(2,1)S(1)}, u32[]{:S(2)}, u32[]{:S(2)}) async-start(bf16[8,128,512]{2,1,0:T(8,128)(2,1)} %bitcast.50), calls=%async_computation.2 | async-start | bytes 2097152 | tf_op jit(solution)/shard_map/all_to_all | solution.py:311
  86.3 8.9 %copy-start = (bf16[8,128,512]{2,1,0:T(8,128)(2,1)}, bf16[8,128,512]{2,1,0:T(8,128)(2,1)S(1)}, u32[]{:S(2)}) copy-start(bf16[8,128,512]{2,1,0:T(8,128)(2,1)S(1)} %all-to-all-done.2) | copy-start | bytes 3145732
  95.2 1.2 copy-start.1
  96.3 11.9 %collective-permute-start.3 = (bf16[1024,256]{1,0:T(8,128)(2,1)}, bf16[1024,256]{1,0:T(8,128)(2,1)S(1)}, u32[]{:S(2)}, u32[]{:S(2)}) collective-permute-start(bf16[1024,256]{1,0:T(8,128)(2,1)} %after.14), channel_id=1, source_target_pairs={{120,128},{121,129},{122,130},{123,131},{124,132},{125,133},{126,1... | collective-permute-start | bytes 1572872 | tf_op jit(solution)/shard_map/ppermute | solution.py:358
  97.0 11.2 %collective-permute-start.4 = (bf16[1024,256]{1,0:T(8,128)(2,1)}, bf16[1024,256]{1,0:T(8,128)(2,1)S(1)}, u32[]{:S(2)}, u32[]{:S(2)}) collective-permute-start(bf16[1024,256]{1,0:T(8,128)(2,1)} %after.15), channel_id=1, source_target_pairs={{120,128},{121,129},{122,130},{123,131},{124,132},{125,133},{126,1... | collective-permute-start | bytes 1572872 | tf_op jit(solution)/shard_map/ppermute | solution.py:358
  99.4 1.4 copy-start.4
  99.4 11.8 %collective-permute-start.5 = (bf16[1024,128]{1,0:T(8,128)(2,1)}, bf16[1024,128]{1,0:T(8,128)(2,1)S(1)}, u32[]{:S(2)}, u32[]{:S(2)}) collective-permute-start(bf16[1024,128]{1,0:T(8,128)(2,1)} %after.16), channel_id=1, source_target_pairs={{120,128},{121,129},{122,130},{123,131},{124,132},{125,133},{126,1... | collective-permute-start | bytes 786440 | tf_op jit(solution)/shard_map/ppermute | solution.py:358
  103.9 39.0 %all-to-all-start.4 = ((bf16[8,128,768]{2,1,0:T(8,128)(2,1)}), bf16[8,128,768]{2,1,0:T(8,128)(2,1)}, u32[]{:S(2)}, u32[]{:S(2)}) async-start(bf16[8,128,768]{2,1,0:T(8,128)(2,1)} %bitcast.47), calls=%async_computation.4 | async-start | bytes 3145728 | tf_op jit(solution)/shard_map/all_to_all | solution.py:311
  108.2 0.8 copy-start.8
  109.0 0.8 copy-start.9
  109.8 20.4 %collective-permute-start.6 = (bf16[1024,384]{1,0:T(8,128)(2,1)}, bf16[1024,384]{1,0:T(8,128)(2,1)S(1)}, u32[]{:S(2)}, u32[]{:S(2)}) collective-permute-start(bf16[1024,384]{1,0:T(8,128)(2,1)} %after.18), channel_id=1, source_target_pairs={{120,128},{121,129},{122,130},{123,131},{124,132},{125,133},{126,1... | collective-permute-start | bytes 2359304 | tf_op jit(solution)/shard_map/ppermute | solution.py:366
  110.5 19.7 %collective-permute-start.7 = (bf16[1024,384]{1,0:T(8,128)(2,1)}, bf16[1024,384]{1,0:T(8,128)(2,1)S(1)}, u32[]{:S(2)}, u32[]{:S(2)}) collective-permute-start(bf16[1024,384]{1,0:T(8,128)(2,1)} %after.19), channel_id=1, source_target_pairs={{120,128},{121,129},{122,130},{123,131},{124,132},{125,133},{126,1... | collective-permute-start | bytes 2359304 | tf_op jit(solution)/shard_map/ppermute | solution.py:366
  111.3 0.7 copy-start.13
  130.2 0.9 copy-start.11
  130.2 1.2 copy-start.12
  131.4 67.3 %collective-permute-start.8 = (bf16[128,5120]{1,0:T(8,128)(2,1)}, bf16[128,5120]{1,0:T(8,128)(2,1)S(1)}, u32[]{:S(2)}, u32[]{:S(2)}) collective-permute-start(bf16[128,5120]{1,0:T(8,128)(2,1)} %after.21), channel_id=1, source_target_pairs={{120,128},{121,129},{122,130},{123,131},{124,132},{125,133},{126,1... | collective-permute-start | bytes 3932168 | tf_op jit(solution)/shard_map/ppermute | solution.py:369
  142.9 29.6 %all-to-all-start.3 = ((bf16[8,128,256]{2,1,0:T(8,128)(2,1)}), bf16[8,128,256]{2,1,0:T(8,128)(2,1)S(1)}, u32[]{:S(2)}, u32[]{:S(2)}) async-start(bf16[8,128,256]{2,1,0:T(8,128)(2,1)} %bitcast.11), calls=%async_computation.3 | async-start | bytes 1048576 | tf_op jit(solution)/shard_map/all_to_all | solution.py:311
  172.6 0.8 copy-start.6
  198.7 1.1 copy-start.10
  213.6 16.7 %all-to-all-start.7 = ((bf16[8,320,128]{2,1,0:T(8,128)(2,1)}), bf16[8,320,128]{2,1,0:T(8,128)(2,1)S(1)}, u32[]{:S(2)}, u32[]{:S(2)}) async-start(bf16[8,320,128]{2,1,0:T(8,128)(2,1)} %bitcast.18), calls=%async_computation.7 | async-start | bytes 1310720 | tf_op jit(solution)/shard_map/all_to_all | solution.py:311
  241.2 2.7 collective-permute-start.9
  244.0 15.8 %copy-start.5 = (bf16[8,128,640]{2,1,0:T(8,128)(2,1)S(1)}, bf16[8,128,640]{2,1,0:T(8,128)(2,1)}, u32[]{:S(2)}) copy-start(bf16[8,128,640]{2,1,0:T(8,128)(2,1)} %all_to_all.116) | copy-start | bytes 3932164
  256.1 3.8 %copy-start.7 = (bf16[8,128,256]{2,1,0:T(8,128)(2,1)S(1)}, bf16[8,128,256]{2,1,0:T(8,128)(2,1)}, u32[]{:S(2)}) copy-start(bf16[8,128,256]{2,1,0:T(8,128)(2,1)} %copy-done.6) | copy-start | bytes 1572868
  256.1 13.5 %all-to-all-start.10 = ((bf16[8,320,128]{2,1,0:T(8,128)(2,1)}), bf16[8,320,128]{2,1,0:T(8,128)(2,1)S(1)}, u32[]{:S(2)}, u32[]{:S(2)}) async-start(bf16[8,320,128]{2,1,0:T(8,128)(2,1)} %broadcast_in_dim.10), calls=%async_computation.10 | async-start | bytes 1310720 | tf_op jit(solution)/shard_map/all_to_all | solution.py:311

commit v7 on v6

--- a/solution.py
+++ b/solution.py
@@ -82,6 +82,33 @@
         cost_estimate=pl.CostEstimate(flops=1 << 29, bytes_accessed=14 << 20, transcendentals=0),
         name="pack",
     )(tokens, query_base, value_base, out_grad, down_q, down_v, up_q, up_v)
+
+
+def cut_kernel(k, vl, low, k_a, v_a, k_b, v_b):
+    rank2, split = low.shape[1], k_a.shape[1]
+    low[...] = vl[:, :rank2]
+    k_a[...] = k[:, :split]
+    v_a[...] = vl[:, rank2 : rank2 + split]
+    k_b[...] = k[:, split:]
+    v_b[...] = vl[:, rank2 + split :]
+
+
+def cut(k, vl):
+    rows, columns = k.shape
+    tile = rows // 4
+    split = CALLS[0] * HEAD
+    sizes = (vl.shape[1] - columns, split, split, columns - split, columns - split)
+    block = lambda width: pl.BlockSpec((tile, width), lambda i: (i, 0))
+    return pl.pallas_call(
+        cut_kernel,
+        grid=(rows // tile,),
+        in_specs=[block(columns), block(vl.shape[1])],
+        out_specs=[block(size) for size in sizes],
+        out_shape=[jax.ShapeDtypeStruct((rows, size), BF16) for size in sizes],
+        compiler_params=pltpu.CompilerParams(vmem_limit_bytes=60 << 20),
+        cost_estimate=pl.CostEstimate(flops=0, bytes_accessed=6 << 20, transcendentals=0),
+        name="cut",
+    )(k, vl)
 
 
 def attention_kernel(
@@ -352,21 +379,14 @@
     vl_prior = lax.ppermute(vl, "blk", forward)
     qg_a = exchange(after(qg_a, vl, k_prior), "uly")
     straight = lax.ppermute(after(copy_a, k_prior), "blk", forward)
-    split = CALLS[0] * HEAD
-    ready = (qg_a, vl_prior, straight)
+    pieces = cut(k, vl)
     low_wrap, *wraps_a = [
-        lax.ppermute(after(array, *ready), "blk", wrapped)
-        for array in (
-            vl[:, : 2 * rank],
-            k[:, :split],
-            vl[:, 2 * rank : 2 * rank + split],
-        )
+        lax.ppermute(after(array, qg_a, vl_prior), "blk", wrapped) for array in pieces[:3]
     ]
     wraps_b = [
-        lax.ppermute(after(array, *wraps_a), "blk", wrapped)
-        for array in (k[:, split:], vl[:, 2 * rank + split :])
+        lax.ppermute(after(array, wraps_a[1]), "blk", wrapped) for array in pieces[3:]
     ]
-    tokens_wrap = lax.ppermute(after(copy_b, *wraps_b), "blk", wrapped)
+    tokens_wrap = lax.ppermute(after(copy_b, *wraps_b, straight), "blk", wrapped)
     qg_b = exchange(after(qg_b, qg_a, vl_prior), "uly")
     place = jnp.stack([lax.axis_index("uly"), lax.axis_index("blk")]).astype(jnp.int32)
     ready = (k, k_prior, vl, vl_prior, low_wrap, up_q, up_v)

time: 285 us -> 282 us (0.989)
  local copies, waits for them, and re-layouts: 21.8 us -> 13.2 us
  starting transfers between devices: 45.5 us -> 50.1 us
  Pallas kernels: 61.6 us -> 65.4 us
    ppermute x1, waiting for transfers between devices: 8.91 us -> 0.01 us  [per_device(): straight = lax.ppermute(after(copy_a, k_prior), 'blk', forward)]
    slice x5 -> x0, local copies, waits for them, and re-layouts: 8.49 us -> none  [the longest x1 2.13 us: per_device(): vl[:, 2 * rank + split:]]
    all_to_all x6, waiting for transfers between devices: 64.4 us -> 71.1 us  [exchange(): lax.all_to_all(array, axis, split_axis=0, concat_axis=0, tiled=True, axis...]
    pallas_call x0 -> x1, Pallas kernels: none -> 4.07 us  [cut(): pl.pallas_call(cut_kernel, grid=(rows // tile,), in_specs=[block(columns)...]
    ppermute x6, starting transfers between devices: 4.32 us -> 7.31 us  [the longest x3 3.51 us: per_device(): lax.ppermute(after(array, qg_a, vl_prior), 'blk', wrapped)]
    unnamed x28 -> x22, local copies, waits for them, and re-layouts: 7.56 us -> 7.43 us
  transfers between devices with their start and end apart: 17 -> 17, of which waited for: 8 -> 7; matrix products, arithmetic and copies ran while one was open for 4% -> 1% of each run, Pallas kernels for 19% -> 21%
where the time goes in v7:
time: 282 us; the launch traced here: 281 us
  waiting for transfers between devices  83.5 us (30%)
  blocking collectives  66 us (23%)
  Pallas kernels  65.4 us (23%)
  starting transfers between devices  50.1 us (18%)
  local copies, waits for them, and re-layouts  13.2 us (5%)
    all_to_all x6, waiting for transfers between devices, exchange(): lax.all_to_all(array, axis, split_axis=0, concat_axis=0, tiled=True, axis...  71.1 us
    all_to_all x5, blocking collectives, exchange(): lax.all_to_all(array, axis, split_axis=0, concat_axis=0, tiled=True, axis...  66 us
    pallas_call x2, Pallas kernels, attention(): pl.pallas_call(functools.partial(attention_kernel, begins, ends), grid_sp...  44.1 us
    all_to_all x6, starting transfers between devices, exchange(): lax.all_to_all(array, axis, split_axis=0, concat_axis=0, tiled=True, axis...  22.8 us
    pallas_call x1, Pallas kernels, pack(): pl.pallas_call(pack_kernel, grid=(parts,), in_specs=[pl.BlockSpec((rows,...  10.3 us
    all_to_all x1, waiting for transfers between devices, per_device(): k = lax.all_to_all(key_base, 'uly', split_axis=1, concat_axis=0, tiled=True)  9.82 us
    all_to_all x1, starting transfers between devices, per_device(): k = lax.all_to_all(key_base, 'uly', split_axis=1, concat_axis=0, tiled=True)  7.48 us
    unnamed x22, local copies, waits for them, and re-layouts  7.43 us
  transfers between devices with their start and end apart: 17, of which 7 were waited for; matrix products, arithmetic and copies ran while one was open for 1% of the time, Pallas kernels for 21%

profile of v7, /device:TPU:1, one launch (start us, length us, event | category | flops | bytes accessed | tf_op | source)
XLA Modules:
  0.0 280.9 jit_solution(12107011807986888829)
XLA Ops:
  0.6 2.6 copy.32
  3.2 7.5 %all-to-all-start = ((bf16[128,8,640]{2,0,1:T(8,128)(2,1)}), bf16[128,8,640]{2,0,1:T(8,128)(2,1)S(1)}, u32[]{:S(2)}, u32[]{:S(2)}) async-start(bf16[128,8,640]{2,0,1:T(8,128)(2,1)} %bitcast.32), calls=%async_computation | async-start | bytes 2621440 | tf_op jit(solution)/shard_map/all_to_all | solution.py:376
  10.7 10.3 %pack.1 = (bf16[1024,768]{1,0:T(8,128)(2,1)}, bf16[1024,512]{1,0:T(8,128)(2,1)}, bf16[1024,768]{1,0:T(8,128)(2,1)}, bf16[128,5120]{1,0:T(8,128)(2,1)}, bf16[128,5120]{1,0:T(8,128)(2,1)}) custom-call(bf16[128,5120]{1,0:T(8,128)(2,1)} %tokens.3, bf16[128,5120]{1,0:T(8,128)(2,1)} %query_base.1, bf16[128,5120]{1,0:T(8,128)(2,1)} %value_base.1, ...), custom_call_target="tpu_custom_call" | custom-call | flops 536870912 | bytes 14680064 | tf_op jit(solution)/shard_map/pack/pallas_call | solution.py:69
  21.0 9.8 %all-to-all-done = bf16[128,8,640]{2,0,1:T(8,128)(2,1)S(1)} async-done(((bf16[128,8,640]{2,0,1:T(8,128)(2,1)}), bf16[128,8,640]{2,0,1:T(8,128)(2,1)S(1)}, u32[]{:S(2)}, u32[]{:S(2)}) %all-to-all-start) | async-done | bytes 1310752 | tf_op jit(solution)/shard_map/all_to_all | solution.py:376
  30.8 1.1 copy-done.2
  31.9 4.4 %all-to-all-start.1 = ((bf16[8,128,768]{2,1,0:T(8,128)(2,1)}), bf16[8,128,768]{2,1,0:T(8,128)(2,1)}, u32[]{:S(2)}, u32[]{:S(2)}) async-start(bf16[8,128,768]{2,1,0:T(8,128)(2,1)} %bitcast.45), calls=%async_computation.1 | async-start | bytes 3145728 | tf_op jit(solution)/shard_map/all_to_all | solution.py:338
  36.3 4.3 %collective-permute-start = (bf16[1024,640]{1,0:T(8,128)(2,1)S(1)}, bf16[1024,640]{1,0:T(8,128)(2,1)}, u32[]{:S(2)}, u32[]{:S(2)}) collective-permute-start(bf16[1024,640]{1,0:T(8,128)(2,1)S(1)} %bitcast.43), channel_id=1, source_target_pairs={{0,8},{8,16},{16,24},{24,32},{32,40},{40,48},{48,56},{56,64},{64,7... | collective-permute-start | bytes 3932168 | tf_op jit(solution)/shard_map/ppermute | solution.py:377
  40.6 18.7 %all-to-all-done.1 = bf16[8,128,768]{2,1,0:T(8,128)(2,1)} async-done(((bf16[8,128,768]{2,1,0:T(8,128)(2,1)}), bf16[8,128,768]{2,1,0:T(8,128)(2,1)}, u32[]{:S(2)}, u32[]{:S(2)}) %all-to-all-start.1) | async-done | bytes 1572896 | tf_op jit(solution)/shard_map/all_to_all | solution.py:338
  59.3 4.2 %collective-permute-start.1 = (bf16[1024,768]{1,0:T(8,128)(2,1)}, bf16[1024,768]{1,0:T(8,128)(2,1)S(1)}, u32[]{:S(2)}, u32[]{:S(2)}) collective-permute-start(bf16[1024,768]{1,0:T(8,128)(2,1)} %bitcast.7.refs_1_.vl.v_own.low_own), channel_id=1, source_target_pairs={{0,8},{8,16},{16,24},{24,32},{32,40},{40,48},{48,56},{56,64},{64,7... | collective-permute-start | bytes 4718600 | tf_op jit(solution)/shard_map/ppermute | solution.py:379
  63.6 0.0 collective-permute-done.refs_2_.k_straight.refs_1_
  63.6 3.6 %all-to-all-start.2 = ((bf16[8,128,512]{2,1,0:T(8,128)(2,1)}), bf16[8,128,512]{2,1,0:T(8,128)(2,1)S(1)}, u32[]{:S(2)}, u32[]{:S(2)}) async-start(bf16[8,128,512]{2,1,0:T(8,128)(2,1)} %bitcast.49), calls=%async_computation.2 | async-start | bytes 2097152 | tf_op jit(solution)/shard_map/all_to_all | solution.py:338
  67.2 4.1 %cut.1 = (bf16[1024,128]{1,0:T(8,128)(2,1)}, bf16[1024,256]{1,0:T(8,128)(2,1)}, bf16[1024,256]{1,0:T(8,128)(2,1)}, bf16[1024,384]{1,0:T(8,128)(2,1)}, bf16[1024,384]{1,0:T(8,128)(2,1)}) custom-call(bf16[1024,640]{1,0:T(8,128)(2,1)} %bitcast.40, bf16[1024,768]{1,0:T(8,128)(2,1)} %bitcast.7.refs_1_.vl.v_own.low_own), custom_call_target="tpu_custom_call" | custom-call | bytes 6291456 | tf_op jit(solution)/shard_map/cut/pallas_call | solution.py:102
  71.2 12.1 %all-to-all-done.2 = bf16[8,128,512]{2,1,0:T(8,128)(2,1)S(1)} async-done(((bf16[8,128,512]{2,1,0:T(8,128)(2,1)}), bf16[8,128,512]{2,1,0:T(8,128)(2,1)S(1)}, u32[]{:S(2)}, u32[]{:S(2)}) %all-to-all-start.2) | async-done | bytes 1048608 | tf_op jit(solution)/shard_map/all_to_all | solution.py:338
  83.3 0.0 collective-permute-done.1.refs_2_.v_straight.low_straight
  83.3 1.0 copy-done
  84.3 0.5 copy-done.1
  84.8 0.7 collective-permute-start.3
  85.5 1.5 collective-permute-start.2
  86.9 1.4 collective-permute-start.4
  88.3 0.6 pad_add_fusion.place
  88.9 3.9 %collective-permute-start.7 = (bf16[128,5120]{1,0:T(8,128)(2,1)}, bf16[128,5120]{1,0:T(8,128)(2,1)S(1)}, u32[]{:S(2)}, u32[]{:S(2)}) collective-permute-start(bf16[128,5120]{1,0:T(8,128)(2,1)} %after.20), channel_id=1, source_target_pairs={{0,8},{8,16},{16,24},{24,32},{32,40},{40,48},{48,56},{56,64},{64,7... | collective-permute-start | bytes 3932168 | tf_op jit(solution)/shard_map/ppermute | solution.py:381
  92.9 3.6 %all-to-all-start.4 = ((bf16[8,128,768]{2,1,0:T(8,128)(2,1)}), bf16[8,128,768]{2,1,0:T(8,128)(2,1)S(1)}, u32[]{:S(2)}, u32[]{:S(2)}) async-start(bf16[8,128,768]{2,1,0:T(8,128)(2,1)} %bitcast.46), calls=%async_computation.4 | async-start | bytes 3145728 | tf_op jit(solution)/shard_map/all_to_all | solution.py:338
  96.5 0.0 collective-permute-done.3.v_wrapped.refs_1_
  96.5 0.0 copy-start.8
  96.5 0.8 copy-done.8
  97.3 1.5 collective-permute-start.5
  98.8 1.5 collective-permute-start.6
  100.3 0.0 collective-permute-done.4.low_wrapped
  100.3 0.0 collective-permute-done.2.k_wrapped
  100.3 18.2 %attention.2 = (bf16[1024,256]{1,0:T(8,128)(2,1)}, bf16[2,128,128]{2,1,0:T(8,128)(2,1)}, f32[1024,64]{1,0:T(8,128)}, f32[64,1024]{1,0:T(8,128)}, f32[64,1024]{1,0:T(8,128)}) custom-call(s32[2]{0:T(128)} %pad_add_fusion.place, bf16[1024,512]{1,0:T(8,128)(2,1)} %bitcast.37, bf16[1024,512]{1,0:T(8,128)(2,1)} %bitcast.38, bf16[1024,640]{1,0:T(8,128)(2,1)} %bitcast.41, ...), custom_call_target="tpu_custom_call" | custom-call | flops 21474836480 | bytes 4194304 | tf_op jit(solution)/shard_map/attention/pallas_call | solution.py:233
  118.5 0.0 collective-permute-done.7.refs_3_.straight
  118.6 0.0 collective-permute-done.5.k_wrapped.refs_1_
  118.6 0.0 collective-permute-done.6.v_wrapped.refs_2_
  118.6 1.0 copy-done.5
  119.6 0.7 collective-permute-start.8
  120.4 18.9 %all-to-all-done.4 = bf16[8,128,768]{2,1,0:T(8,128)(2,1)S(1)} async-done(((bf16[8,128,768]{2,1,0:T(8,128)(2,1)}), bf16[8,128,768]{2,1,0:T(8,128)(2,1)S(1)}, u32[]{:S(2)}, u32[]{:S(2)}) %all-to-all-start.4) | async-done | bytes 1572896 | tf_op jit(solution)/shard_map/all_to_all | solution.py:338
  139.3 1.2 copy-done.9
  140.4 4.0 %all-to-all-start.3 = ((bf16[8,128,256]{2,1,0:T(8,128)(2,1)}), bf16[8,128,256]{2,1,0:T(8,128)(2,1)S(1)}, u32[]{:S(2)}, u32[]{:S(2)}) async-start(bf16[8,128,256]{2,1,0:T(8,128)(2,1)} %bitcast.57), calls=%async_computation.3 | async-start | bytes 1048576 | tf_op jit(solution)/shard_map/all_to_all | solution.py:338
  144.4 25.9 %attention.3 = (bf16[1024,640]{1,0:T(8,128)(2,1)}, bf16[2,192,128]{2,1,0:T(8,128)(2,1)}) custom-call(s32[2]{0:T(128)} %pad_add_fusion.place, bf16[1024,768]{1,0:T(8,128)(2,1)} %bitcast.51, bf16[1024,768]{1,0:T(8,128)(2,1)} %bitcast.52, bf16[1024,640]{1,0:T(8,128)(2,1)} %bitcast.42, bf16[1024,768]{1,0:T(8,128)(2,1)} %bitcast.7.refs_1_.vl.v_own.low_own, ...), custom_call_target="tpu_custom_call" | custom-call | flops 32212254720 | bytes 6291456 | tf_op jit(solution)/shard_map/attention/pallas_call | solution.py:233
  170.3 0.0 all-to-all-done.3
  170.3 0.0 copy-start.6
  170.3 0.8 copy-done.6
  171.1 25.4 %all_to_all.116 = bf16[8,128,640]{2,1,0:T(8,128)(2,1)} all-to-all(bf16[8,128,640]{2,1,0:T(8,128)(2,1)} %bitcast.47), channel_id=1, replica_groups=mesh['blk'=32,'uly'=8] {'uly'}, dimensions={0} | all-to-all | bytes 2621440 | tf_op jit(solution)/shard_map/all_to_all | solution.py:338
  196.5 1.1 copy-done.10
  197.6 4.2 %outer.1 = bf16[2,2880,128]{2,1,0:T(8,128)(2,1)} custom-call(bf16[1024,640]{1,0:T(8,128)(2,1)} %bitcast.44, bf16[128,5120]{1,0:T(8,128)(2,1)} %tokens.3, bf16[128,5120]{1,0:T(8,128)(2,1)} %copy-done.5, bf16[128,5120]{1,0:T(8,128)(2,1)} %copy-done.10, bf16[2,128,128]{2,1,0:T(8,128)(2,1)} %get-tuple-element.41.rest_0_, ...), custom_call_target="tpu_custom_call" | custom-call | flops 536870912 | bytes 8388608 | tf_op jit(solution)/shard_map/outer/pallas_call | solution.py:301
  201.8 8.0 %all_to_all.117 = bf16[2,2880,128]{2,1,0:T(8,128)(2,1)S(1)} all-to-all(bf16[2,2880,128]{2,1,0:T(8,128)(2,1)} %outer.1), channel_id=1, replica_groups={{0,8},{16,24},{32,40},{48,56},{64,72},{80,88},{96,104},{112,120},{128,1..., dimensions={0} | all-to-all | bytes 2949120 | tf_op jit(solution)/shard_map/all_to_all | solution.py:338
  209.8 0.8 reduce_sum.36
  210.5 0.9 slice.21
  211.4 3.5 %all-to-all-start.7 = ((bf16[8,320,128]{2,1,0:T(8,128)(2,1)}), bf16[8,320,128]{2,1,0:T(8,128)(2,1)S(1)}, u32[]{:S(2)}, u32[]{:S(2)}) async-start(bf16[8,320,128]{2,1,0:T(8,128)(2,1)} %bitcast.18), calls=%async_computation.7 | async-start | bytes 1310720 | tf_op jit(solution)/shard_map/all_to_all | solution.py:338
  215.0 13.1 %all-to-all-done.7 = bf16[8,320,128]{2,1,0:T(8,128)(2,1)S(1)} async-done(((bf16[8,320,128]{2,1,0:T(8,128)(2,1)}), bf16[8,320,128]{2,1,0:T(8,128)(2,1)S(1)}, u32[]{:S(2)}, u32[]{:S(2)}) %all-to-all-start.7) | async-done | bytes 655392 | tf_op jit(solution)/shard_map/all_to_all | solution.py:338
  228.1 0.1 reduce_sum.37
  228.2 10.8 %all_to_all.118 = bf16[8,80,128]{2,1,0:T(8,128)(2,1)S(1)} all-to-all(bf16[8,80,128]{2,1,0:T(8,128)(2,1)S(1)} %pad_maximum_fusion.1), channel_id=1, replica_groups={{0,16,32,48,64,80,96,112},{8,24,40,56,72,88,104,120},{128,144,160,176,1..., dimensions={0} | all-to-all | bytes 327680 | tf_op jit(solution)/shard_map/all_to_all | solution.py:338
  239.0 0.1 collective-permute-start.9
  239.1 2.6 collective-permute-done.9
  241.8 11.2 %all_to_all.119 = bf16[8,80,128]{2,1,0:T(8,128)(2,1)S(1)} all-to-all(bf16[8,80,128]{2,1,0:T(8,128)(2,1)S(1)} %broadcast_in_dim.8), channel_id=1, replica_groups={{0,16,32,48,64,80,96,112},{8,24,40,56,72,88,104,120},{128,144,160,176,1..., dimensions={0} | all-to-all | bytes 327680 | tf_op jit(solution)/shard_map/all_to_all | solution.py:338
  253.0 0.9 broadcast_in_dim.10
  253.9 3.7 %all-to-all-start.10 = ((bf16[8,320,128]{2,1,0:T(8,128)(2,1)}), bf16[8,320,128]{2,1,0:T(8,128)(2,1)S(1)}, u32[]{:S(2)}, u32[]{:S(2)}) async-start(bf16[8,320,128]{2,1,0:T(8,128)(2,1)} %broadcast_in_dim.10), calls=%async_computation.10 | async-start | bytes 1310720 | tf_op jit(solution)/shard_map/all_to_all | solution.py:338
  257.6 0.1 slice.20
  257.7 0.1 maximum_bitcast_fusion
  257.8 1.2 copy.30
  259.0 8.3 %all-to-all-done.10 = bf16[8,320,128]{2,1,0:T(8,128)(2,1)S(1)} async-done(((bf16[8,320,128]{2,1,0:T(8,128)(2,1)}), bf16[8,320,128]{2,1,0:T(8,128)(2,1)S(1)}, u32[]{:S(2)}, u32[]{:S(2)}) %all-to-all-start.10) | async-done | bytes 655392 | tf_op jit(solution)/shard_map/all_to_all | solution.py:338
  267.4 0.1 broadcast_in_dim.22
  267.5 10.7 %all_to_all.120.both = bf16[2,2880,128]{2,1,0:T(8,128)(2,1)} all-to-all(bf16[2,2880,128]{2,1,0:T(8,128)(2,1)S(1)} %broadcast_in_dim.22), channel_id=1, replica_groups={{0,8},{16,24},{32,40},{48,56},{64,72},{80,88},{96,104},{112,120},{128,1..., dimensions={0} | all-to-all | bytes 2949120 | tf_op jit(solution)/shard_map/all_to_all | solution.py:338
  278.2 2.7 unpack.1
  (31 shorter events, 0.2 us)
Async XLA Ops:
  3.2 27.6 %all-to-all-start = ((bf16[128,8,640]{2,0,1:T(8,128)(2,1)}), bf16[128,8,640]{2,0,1:T(8,128)(2,1)S(1)}, u32[]{:S(2)}, u32[]{:S(2)}) async-start(bf16[128,8,640]{2,0,1:T(8,128)(2,1)} %bitcast.32), calls=%async_computation | async-start | bytes 2621440 | tf_op jit(solution)/shard_map/all_to_all | solution.py:376
  30.8 1.1 copy-start.2
  31.9 4.4 %copy-start.3 = (bf16[128,8,640]{2,0,1:T(8,128)(2,1)S(1)}, bf16[128,8,640]{2,0,1:T(8,128)(2,1)}, u32[]{:S(2)}) copy-start(bf16[128,8,640]{2,0,1:T(8,128)(2,1)} %copy-done.2) | copy-start | bytes 3932164
  31.9 27.4 %all-to-all-start.1 = ((bf16[8,128,768]{2,1,0:T(8,128)(2,1)}), bf16[8,128,768]{2,1,0:T(8,128)(2,1)}, u32[]{:S(2)}, u32[]{:S(2)}) async-start(bf16[8,128,768]{2,1,0:T(8,128)(2,1)} %bitcast.45), calls=%async_computation.1 | async-start | bytes 3145728 | tf_op jit(solution)/shard_map/all_to_all | solution.py:338
  36.3 27.2 %collective-permute-start = (bf16[1024,640]{1,0:T(8,128)(2,1)S(1)}, bf16[1024,640]{1,0:T(8,128)(2,1)}, u32[]{:S(2)}, u32[]{:S(2)}) collective-permute-start(bf16[1024,640]{1,0:T(8,128)(2,1)S(1)} %bitcast.43), channel_id=1, source_target_pairs={{0,8},{8,16},{16,24},{24,32},{32,40},{40,48},{48,56},{56,64},{64,7... | collective-permute-start | bytes 3932168 | tf_op jit(solution)/shard_map/ppermute | solution.py:377
  59.3 24.0 %collective-permute-start.1 = (bf16[1024,768]{1,0:T(8,128)(2,1)}, bf16[1024,768]{1,0:T(8,128)(2,1)S(1)}, u32[]{:S(2)}, u32[]{:S(2)}) collective-permute-start(bf16[1024,768]{1,0:T(8,128)(2,1)} %bitcast.7.refs_1_.vl.v_own.low_own), channel_id=1, source_target_pairs={{0,8},{8,16},{16,24},{24,32},{32,40},{40,48},{48,56},{56,64},{64,7... | collective-permute-start | bytes 4718600 | tf_op jit(solution)/shard_map/ppermute | solution.py:379
  63.6 19.7 %all-to-all-start.2 = ((bf16[8,128,512]{2,1,0:T(8,128)(2,1)}), bf16[8,128,512]{2,1,0:T(8,128)(2,1)S(1)}, u32[]{:S(2)}, u32[]{:S(2)}) async-start(bf16[8,128,512]{2,1,0:T(8,128)(2,1)} %bitcast.49), calls=%async_computation.2 | async-start | bytes 2097152 | tf_op jit(solution)/shard_map/all_to_all | solution.py:338
  83.3 1.0 copy-start
  83.3 1.5 copy-start.1
  84.8 11.7 %collective-permute-start.3 = (bf16[1024,256]{1,0:T(8,128)(2,1)}, bf16[1024,256]{1,0:T(8,128)(2,1)S(1)}, u32[]{:S(2)}, u32[]{:S(2)}) collective-permute-start(bf16[1024,256]{1,0:T(8,128)(2,1)} %after.14), channel_id=1, source_target_pairs={{120,128},{121,129},{122,130},{123,131},{124,132},{125,133},{126,1... | collective-permute-start | bytes 1572872 | tf_op jit(solution)/shard_map/ppermute | solution.py:384
  85.5 14.9 %collective-permute-start.2 = (bf16[1024,256]{1,0:T(8,128)(2,1)}, bf16[1024,256]{1,0:T(8,128)(2,1)}, u32[]{:S(2)}, u32[]{:S(2)}) collective-permute-start(bf16[1024,256]{1,0:T(8,128)(2,1)} %after.13), channel_id=1, source_target_pairs={{120,128},{121,129},{122,130},{123,131},{124,132},{125,133},{126,1... | collective-permute-start | bytes 1572872 | tf_op jit(solution)/shard_map/ppermute | solution.py:384
  86.9 13.4 %collective-permute-start.4 = (bf16[1024,128]{1,0:T(8,128)(2,1)}, bf16[1024,128]{1,0:T(8,128)(2,1)}, u32[]{:S(2)}, u32[]{:S(2)}) collective-permute-start(bf16[1024,128]{1,0:T(8,128)(2,1)} %after.15), channel_id=1, source_target_pairs={{120,128},{121,129},{122,130},{123,131},{124,132},{125,133},{126,1... | collective-permute-start | bytes 786440 | tf_op jit(solution)/shard_map/ppermute | solution.py:384
  88.9 29.7 %collective-permute-start.7 = (bf16[128,5120]{1,0:T(8,128)(2,1)}, bf16[128,5120]{1,0:T(8,128)(2,1)S(1)}, u32[]{:S(2)}, u32[]{:S(2)}) collective-permute-start(bf16[128,5120]{1,0:T(8,128)(2,1)} %after.20), channel_id=1, source_target_pairs={{0,8},{8,16},{16,24},{24,32},{32,40},{40,48},{48,56},{56,64},{64,7... | collective-permute-start | bytes 3932168 | tf_op jit(solution)/shard_map/ppermute | solution.py:381
  92.9 46.4 %all-to-all-start.4 = ((bf16[8,128,768]{2,1,0:T(8,128)(2,1)}), bf16[8,128,768]{2,1,0:T(8,128)(2,1)S(1)}, u32[]{:S(2)}, u32[]{:S(2)}) async-start(bf16[8,128,768]{2,1,0:T(8,128)(2,1)} %bitcast.46), calls=%async_computation.4 | async-start | bytes 3145728 | tf_op jit(solution)/shard_map/all_to_all | solution.py:338
  96.5 0.8 copy-start.8
  97.3 21.3 %collective-permute-start.5 = (bf16[1024,384]{1,0:T(8,128)(2,1)}, bf16[1024,384]{1,0:T(8,128)(2,1)}, u32[]{:S(2)}, u32[]{:S(2)}) collective-permute-start(bf16[1024,384]{1,0:T(8,128)(2,1)} %after.17), channel_id=1, source_target_pairs={{120,128},{121,129},{122,130},{123,131},{124,132},{125,133},{126,1... | collective-permute-start | bytes 2359304 | tf_op jit(solution)/shard_map/ppermute | solution.py:387
  98.8 19.8 %collective-permute-start.6 = (bf16[1024,384]{1,0:T(8,128)(2,1)}, bf16[1024,384]{1,0:T(8,128)(2,1)}, u32[]{:S(2)}, u32[]{:S(2)}) collective-permute-start(bf16[1024,384]{1,0:T(8,128)(2,1)} %after.18), channel_id=1, source_target_pairs={{120,128},{121,129},{122,130},{123,131},{124,132},{125,133},{126,1... | collective-permute-start | bytes 2359304 | tf_op jit(solution)/shard_map/ppermute | solution.py:387
  118.6 1.1 copy-start.5
  119.6 76.9 %collective-permute-start.8 = (bf16[128,5120]{1,0:T(8,128)(2,1)}, bf16[128,5120]{1,0:T(8,128)(2,1)S(1)}, u32[]{:S(2)}, u32[]{:S(2)}) collective-permute-start(bf16[128,5120]{1,0:T(8,128)(2,1)} %after.21), channel_id=1, source_target_pairs={{120,128},{121,129},{122,130},{123,131},{124,132},{125,133},{126,1... | collective-permute-start | bytes 3932168 | tf_op jit(solution)/shard_map/ppermute | solution.py:389
  139.3 1.2 copy-start.9
  140.4 29.9 %all-to-all-start.3 = ((bf16[8,128,256]{2,1,0:T(8,128)(2,1)}), bf16[8,128,256]{2,1,0:T(8,128)(2,1)S(1)}, u32[]{:S(2)}, u32[]{:S(2)}) async-start(bf16[8,128,256]{2,1,0:T(8,128)(2,1)} %bitcast.57), calls=%async_computation.3 | async-start | bytes 1048576 | tf_op jit(solution)/shard_map/all_to_all | solution.py:338
  170.3 0.8 copy-start.6
  196.5 1.1 copy-start.10
  211.4 16.7 %all-to-all-start.7 = ((bf16[8,320,128]{2,1,0:T(8,128)(2,1)}), bf16[8,320,128]{2,1,0:T(8,128)(2,1)S(1)}, u32[]{:S(2)}, u32[]{:S(2)}) async-start(bf16[8,320,128]{2,1,0:T(8,128)(2,1)} %bitcast.18), calls=%async_computation.7 | async-start | bytes 1310720 | tf_op jit(solution)/shard_map/all_to_all | solution.py:338
  239.0 2.7 collective-permute-start.9
  241.8 15.8 %copy-start.4 = (bf16[8,128,640]{2,1,0:T(8,128)(2,1)S(1)}, bf16[8,128,640]{2,1,0:T(8,128)(2,1)}, u32[]{:S(2)}) copy-start(bf16[8,128,640]{2,1,0:T(8,128)(2,1)} %all_to_all.116) | copy-start | bytes 3932164
  253.9 3.8 %copy-start.7 = (bf16[8,128,256]{2,1,0:T(8,128)(2,1)S(1)}, bf16[8,128,256]{2,1,0:T(8,128)(2,1)}, u32[]{:S(2)}) copy-start(bf16[8,128,256]{2,1,0:T(8,128)(2,1)} %copy-done.6) | copy-start | bytes 1572868
  253.9 13.5 %all-to-all-start.10 = ((bf16[8,320,128]{2,1,0:T(8,128)(2,1)}), bf16[8,320,128]{2,1,0:T(8,128)(2,1)S(1)}, u32[]{:S(2)}, u32[]{:S(2)}) async-start(bf16[8,320,128]{2,1,0:T(8,128)(2,1)} %broadcast_in_dim.10), calls=%async_computation.10 | async-start | bytes 1310720 | tf_op jit(solution)/shard_map/all_to_all | solution.py:338
